TPU v7x, 32 devices: a whole 2x2x4 slice. The times are simulated.
32 devices in a mesh: vol: 2 (over core), wide: 8 (over z, x), narrow: 2 (over y).
Axes of the slice: x: 2, y: 2, z: 4, core: 2. Of those that a mesh axis runs over, the one named last changes fastest.
Arguments:
- forcing: float32 [2, 4, 384, 1024], P(None, 'vol', 'narrow', 'wide'), may hold values from -180 to 180
- material_ids: int32 [4, 384, 1024], P('vol', 'narrow', 'wide'), may hold values from 0 to 7
- materials: float32 [8], replicated, may hold values from 0.5 to 2
- boundary_operator: bfloat16 [1024, 32768], P('wide', 'narrow'), may hold values from -0.03125 to 0.03125
Outputs:
- pressure: float32 [2, 4, 384, 1024], P(None, 'vol', 'narrow', 'wide')
- traction: float32 [1024, 2], P(('wide', 'narrow'), 'vol')
All inputs are finite; a program needn't handle non-finite values.
Results may differ from a plain program's by a relative error of at most 0.0031.
Values may be sent and summed in bfloat16 or wider, within the bound.
No kernel may reach another device: no remote copies, remote signals or barrier semaphores. Data moves between devices by JAX's collectives and lax.ppermute only.
A program may use at most 128 MiB of HBM per device.

v0:
```python
import jax
import jax.numpy as jnp
from jax import lax
from jax.sharding import PartitionSpec as P

BY = 16
RY = 1
RX = 64
MAT = 8
ITERS = 2


lower_edge = 0.25
upper_edge = 1.75
mass_ratio = 26.0
couple_gain = 40.0


def with_halo(shard, sides, width):
    for axis, dim in sides:
        peers, length = (lax.axis_size(axis), shard.shape[dim])
        up = [(i, (i + 1) % peers) for i in range(peers - 1)]
        down = [(j, i) for i, j in up]
        last = lax.slice_in_dim(shard, length - width, length, axis=dim)
        first = lax.slice_in_dim(shard, 0, width, axis=dim)
        before = lax.ppermute(last, axis, up)
        after = lax.ppermute(first, axis, down)
        shard = jnp.concatenate([before, shard, after], axis=dim)
    return shard


def from_root(shard, axis, root):
    mine = lax.axis_index(axis) == root
    return lax.psum(jnp.where(mine, shard, jnp.zeros_like(shard)), axis)


def sweep_weights():
    middle = (upper_edge + lower_edge) / 2.0
    spread = (upper_edge - lower_edge) / 2.0
    center_ratio = middle / spread
    ratio_last = 1.0 / center_ratio
    weights = [(0.0, 1.0 / middle)]
    ratio_next = 1.0 / (2.0 * center_ratio - ratio_last)
    weights.append((ratio_next * ratio_last, 2.0 * ratio_next / spread))
    return weights


def box_sum(padded):
    along = padded[..., :-2] + padded[..., 1:-1] + padded[..., 2:]
    along = along[..., :-2, :] + along[..., 1:-1, :] + along[..., 2:, :]
    return along[..., :-2, :, :] + along[..., 1:-1, :, :] + along[..., 2:, :, :]


def apply_operator(padded, center, cond_pad, conductance, diagonal):
    neighbours = box_sum(padded) - center
    weighted = box_sum(padded * cond_pad) - conductance * center
    return diagonal * center - 0.5 * (conductance * neighbours + weighted)


def relax(vol_field, source, cond_pad, conductance, diagonal):
    moved = jnp.zeros_like(vol_field)
    for keep_weight, gain_weight in sweep_weights():
        padded = with_halo(vol_field, (("vol", 1), ("wide", 3), ("narrow", 2)), 1)
        scaled = (
            source - apply_operator(padded, vol_field, cond_pad, conductance, diagonal)
        ) / diagonal
        moved = keep_weight * moved + gain_weight * scaled
        vol_field = vol_field + moved
    return vol_field


def fold_traces(mine, plane):
    return jnp.einsum(
        "ryx,kyx->rk",
        plane,
        lax.all_gather(mine, "wide", axis=2, tiled=True),
        preferred_element_type=jnp.float32,
    )


def local(forcing, material_ids, materials, boundary_operator):
    conductance = jnp.zeros(material_ids.shape, jnp.float32)
    for number in range(MAT):
        conductance = conductance + jnp.where(material_ids == number, materials[number], 0.0)
    cond_pad = with_halo(conductance, (("vol", 0), ("wide", 2), ("narrow", 1)), 1)
    diagonal = (
        0.5 * (26.0 * conductance + (box_sum(cond_pad) - conductance)) + mass_ratio * conductance
    )
    vol_count = lax.axis_size("vol")
    last_vol = vol_count - 1
    own_vol = lax.axis_index("vol")
    excite = forcing.shape[0]
    half_count = excite // vol_count
    tile_rows = boundary_operator.shape[0]
    cells_y = forcing.shape[2]
    cells_x = forcing.shape[3]
    stride = cells_y // BY
    plane = boundary_operator.reshape(tile_rows, BY, -1)
    is_top = (own_vol == last_vol).astype(jnp.float32)
    pressure = jnp.zeros(forcing.shape, jnp.float32)
    source = forcing
    traction = jnp.zeros((tile_rows // lax.axis_size("narrow"), half_count), jnp.float32)
    for outer in range(ITERS):
        pressure = relax(pressure, source, cond_pad, conductance, diagonal)
        surface = pressure[:, -1, ::stride].astype(jnp.bfloat16)
        copied = from_root(surface, "vol", last_vol)
        mine = lax.dynamic_slice_in_dim(copied, own_vol * half_count, half_count, 0)
        partial_rows = fold_traces(mine, plane)
        summed = lax.psum(partial_rows, "narrow")
        share = summed.shape[0] // lax.axis_size("narrow")
        traction = lax.dynamic_slice_in_dim(summed, lax.axis_index("narrow") * share, share, 0)
        if outer + 1 < ITERS:
            shared = lax.all_gather(traction, "vol", axis=1, tiled=True)
            placed = jnp.transpose(shared).reshape(excite, RY, RX)
            placed = jnp.pad(placed, ((0, 0), (0, cells_y - RY), (0, cells_x - RX)))
            source = forcing.at[:, -1].add(couple_gain * is_top * placed)
    return (pressure, traction)


def solution(mesh):
    placed = (
        P(None, "vol", "narrow", "wide"),
        P("vol", "narrow", "wide"),
        P(),
        P("wide", "narrow"),
    )
    return jax.shard_map(
        local,
        mesh=mesh,
        in_specs=placed,
        out_specs=(P(None, "vol", "narrow", "wide"), P(("wide", "narrow"), "vol")),
        check_vma=False,
    )
```

profile of v0, /device:TPU:0, one launch (start us, length us, event | category | flops | bytes accessed | tf_op | source)
XLA Modules:
  0.0 236.0 jit_solution(11555738974021824176)
XLA Ops:
  2.3 6.8 %broadcast_multiply_fusion.5 = (f32[2,192,128]{2,1,0:T(8,128)}, f32[2,192,128]{2,1,0:T(8,128)S(1)}) fusion(f32[]{:T(128)} %bitcast.7, s32[2,192,128]{2,1,0:T(8,128)} %param.7, f32[]{:T(128)} %bitcast.6, f32[]{:T(128)} %bitcast.5, f32[]{:T(128)} %bitcast.4, f32[]{:T(128)} %bitcast.3, f32[]{:T(128)} %bitcast.2, f32[]{:T(128)} %bitcast.1, f32[]{:T(128)} %bitcast), kind=kLoop, calls=%fused_computation.111 | loop fusion | flops 1179648 | bytes 589856 | tf_op jit(solution)/shard_map/mul | solution.py:56
  9.1 2.4 %collective-permute-start = (f32[1,192,128]{2,1,0:T(8,128)S(1)}, f32[1,192,128]{2,1,0:T(8,128)S(1)}, u32[]{:S(2)}, u32[]{:S(2)}) collective-permute-start(f32[1,192,128]{2,1,0:T(8,128)S(1)} %get-tuple-element.64), channel_id=1, source_target_pairs={{0,16},{1,17},{2,18},{3,19},{4,20},{5,21},{6,22},{7,23},{8,24},{9,... | collective-permute-start | bytes 294920 | tf_op jit(solution)/shard_map/ppermute | solution.py:26
  12.8 1.9 collective-permute-done.1
  14.9 4.2 %collective-permute-start.2 = (f32[4,192,1]{2,1,0:T(8,128)S(1)}, f32[4,192,1]{2,1,0:T(8,128)S(1)}, u32[]{:S(2)}, u32[]{:S(2)}) collective-permute-start(f32[4,192,1]{2,1,0:T(8,128)S(1)} %get-tuple-element.62), channel_id=1, source_target_pairs={{0,2},{2,4},{4,6},{6,8},{8,10},{10,12},{12,14},{1,3},{3,5},{5,7},{... | collective-permute-start | bytes 9224 | tf_op jit(solution)/shard_map/ppermute | solution.py:26
  20.5 15.8 %collective-permute-done.2 = f32[4,192,1]{2,1,0:T(8,128)S(1)} collective-permute-done((f32[4,192,1]{2,1,0:T(8,128)S(1)}, f32[4,192,1]{2,1,0:T(8,128)S(1)}, u32[]{:S(2)}, u32[]{:S(2)}) %collective-permute-start.2) | collective-permute-done | bytes 3104 | tf_op jit(solution)/shard_map/ppermute | solution.py:26
  36.3 3.4 %collective-permute-start.4 = (f32[4,1,130]{2,1,0:T(1,128)S(1)}, f32[4,1,130]{2,1,0:T(1,128)S(1)}, u32[]{:S(2)}, u32[]{:S(2)}) collective-permute-start(f32[4,1,130]{2,1,0:T(1,128)S(1)} %get-tuple-element.44), channel_id=1, source_target_pairs={{0,1},{2,3},{4,5},{6,7},{8,9},{10,11},{12,13},{14,15},{16,17},{18,... | collective-permute-start | bytes 6248 | tf_op jit(solution)/shard_map/ppermute | solution.py:26
  42.4 3.0 %collective-permute-start.6 = (f32[2,1,192,128]{3,2,0,1:T(8,128)S(1)}, f32[2,1,192,128]{3,2,0,1:T(8,128)S(1)}, u32[]{:S(2)}, u32[]{:S(2)}) collective-permute-start(f32[2,1,192,128]{3,2,0,1:T(8,128)S(1)} %broadcast.51), channel_id=1, source_target_pairs={{0,16},{1,17},{2,18},{3,19},{4,20},{5,21},{6,22},{7,23},{8,24},{9,... | collective-permute-start | bytes 589832 | tf_op jit(solution)/shard_map/ppermute | solution.py:26
  50.9 5.0 %collective-permute-start.8 = (f32[2,4,192,1]{2,1,3,0:T(4,128)S(1)}, f32[2,4,192,1]{2,1,3,0:T(4,128)S(1)}, u32[]{:S(2)}, u32[]{:S(2)}) collective-permute-start(f32[2,4,192,1]{2,1,3,0:T(4,128)S(1)} %copy.19), channel_id=1, source_target_pairs={{0,2},{2,4},{4,6},{6,8},{8,10},{10,12},{12,14},{1,3},{3,5},{5,7},{... | collective-permute-start | bytes 18440 | tf_op jit(solution)/shard_map/ppermute | solution.py:26
  58.0 4.5 %collective-permute-start.10 = (f32[2,4,1,130]{3,2,0,1:T(1,128)S(1)}, f32[2,4,1,130]{3,2,0,1:T(1,128)S(1)}, u32[]{:S(2)}, u32[]{:S(2)}) collective-permute-start(f32[2,4,1,130]{3,2,0,1:T(1,128)S(1)} %get-tuple-element.42), channel_id=1, source_target_pairs={{0,1},{2,3},{4,5},{6,7},{8,9},{10,11},{12,13},{14,15},{16,17},{18,... | collective-permute-start | bytes 12488 | tf_op jit(solution)/shard_map/ppermute | solution.py:26
  65.1 3.0 %collective-permute-done.11 = f32[2,4,1,130]{3,2,0,1:T(1,128)S(1)} collective-permute-done((f32[2,4,1,130]{3,2,0,1:T(1,128)S(1)}, f32[2,4,1,130]{3,2,0,1:T(1,128)S(1)}, u32[]{:S(2)}, u32[]{:S(2)}) %collective-permute-start.11) | collective-permute-done | bytes 4192 | tf_op jit(solution)/shard_map/ppermute | solution.py:27
  68.1 1.6 broadcast_multiply_fusion.3
  75.5 2.0 collective-permute-done.13
  78.8 4.8 %collective-permute-start.14 = (f32[2,4,192,1]{2,1,3,0:T(4,128)S(1)}, f32[2,4,192,1]{2,1,3,0:T(4,128)S(1)}, u32[]{:S(2)}, u32[]{:S(2)}) collective-permute-start(f32[2,4,192,1]{2,1,3,0:T(4,128)S(1)} %copy.24), channel_id=1, source_target_pairs={{0,2},{2,4},{4,6},{6,8},{8,10},{10,12},{12,14},{1,3},{3,5},{5,7},{... | collective-permute-start | bytes 18440 | tf_op jit(solution)/shard_map/ppermute | solution.py:26
  85.6 5.1 %collective-permute-done.15 = f32[2,4,192,1]{2,1,3,0:T(4,128)S(1)} collective-permute-done((f32[2,4,192,1]{2,1,3,0:T(4,128)S(1)}, f32[2,4,192,1]{2,1,3,0:T(4,128)S(1)}, u32[]{:S(2)}, u32[]{:S(2)}) %collective-permute-start.15) | collective-permute-done | bytes 6176 | tf_op jit(solution)/shard_map/ppermute | solution.py:27
  94.8 6.4 %copy.43 = bf16[128,16384]{0,1:T(8,128)(2,1)} copy(bf16[128,16384]{1,0:T(8,128)(2,1)} %param.9) | data formatting | bytes 8388608 | tf_op jit(solution)/shard_map/reshape | solution.py:98
  101.2 1.7 broadcast_multiply_fusion.2
  105.4 2.5 %psum.28 = bf16[2,16,128]{2,1,0:T(8,128)(2,1)S(1)} all-reduce(bf16[2,16,128]{2,1,0:T(8,128)(2,1)S(1)} %select_bitcast_fusion.1), channel_id=1, replica_groups=mesh['vol'=2,'wide'=8,'narrow'=2] {'vol'}, use_global_device_ids=true, to_apply=%region_0.1 | all-reduce | flops 4096 | bytes 16384 | tf_op jit(solution)/shard_map/psum | solution.py:34
  107.9 26.0 %all_gather.9 = bf16[1,16,1024]{2,1,0:T(8,128)(2,1)S(1)} all-gather(bf16[1,16,128]{2,1,0:T(8,128)(2,1)S(1)} %constant_dynamic-slice_fusion.3), channel_id=1, replica_groups=mesh['vol'=2,'wide'=8,'narrow'=2] {'wide'}, dimensions={2}, use_global_device_ids=true | all-gather | bytes 36864 | tf_op jit(solution)/shard_map/all_gather | solution.py:76
  136.6 2.9 %convolution_bitcast_fusion.1 = f32[128,1]{0,1:T(1,128)S(1)} fusion(bf16[128,16,1024]{0,2,1:T(8,128)(2,1)} %bitcast.31, bf16[16,1024,1]{1,0,2:T(8,128)(2,1)S(1)} %bitcast.33), kind=kOutput, calls=%fused_computation.5 | convolution fusion | flops 4194304 | bytes 4227584 | tf_op jit(solution)/shard_map/ryx,kyx->rk/dot_general | solution.py:73
  139.4 5.5 %psum.29 = f32[128,1]{0,1:T(1,128)S(1)} all-reduce(f32[128,1]{0,1:T(1,128)S(1)} %convolution_bitcast_fusion.1), channel_id=1, replica_groups=mesh['vol'=2,'wide'=8,'narrow'=2] {'narrow'}, use_global_device_ids=true, to_apply=%region_1.2 | all-reduce | flops 128 | bytes 1024 | tf_op jit(solution)/shard_map/psum | solution.py:109
  147.7 4.5 %collective-permute-start.20 = (f32[2,4,192,1]{2,1,3,0:T(4,128)S(1)}, f32[2,4,192,1]{2,1,3,0:T(4,128)S(1)}, u32[]{:S(2)}, u32[]{:S(2)}) collective-permute-start(f32[2,4,192,1]{2,1,3,0:T(4,128)S(1)} %copy.31), channel_id=1, source_target_pairs={{0,2},{2,4},{4,6},{6,8},{8,10},{10,12},{12,14},{1,3},{3,5},{5,7},{... | collective-permute-start | bytes 18440 | tf_op jit(solution)/shard_map/ppermute | solution.py:26
  152.4 1.8 all-gather
  155.7 3.9 %collective-permute-start.22 = (f32[2,4,1,130]{3,2,0,1:T(1,128)S(1)}, f32[2,4,1,130]{3,2,0,1:T(1,128)S(1)}, u32[]{:S(2)}, u32[]{:S(2)}) collective-permute-start(f32[2,4,1,130]{3,2,0,1:T(1,128)S(1)} %get-tuple-element.38), channel_id=1, source_target_pairs={{0,1},{2,3},{4,5},{6,7},{8,9},{10,11},{12,13},{14,15},{16,17},{18,... | collective-permute-start | bytes 12488 | tf_op jit(solution)/shard_map/ppermute | solution.py:26
  161.1 4.2 %collective-permute-done.23 = f32[2,4,1,130]{3,2,0,1:T(1,128)S(1)} collective-permute-done((f32[2,4,1,130]{3,2,0,1:T(1,128)S(1)}, f32[2,4,1,130]{3,2,0,1:T(1,128)S(1)}, u32[]{:S(2)}, u32[]{:S(2)}) %collective-permute-start.23) | collective-permute-done | bytes 4192 | tf_op jit(solution)/shard_map/ppermute | solution.py:27
  171.9 2.0 collective-permute-done.25
  175.3 4.8 %collective-permute-start.26 = (f32[2,4,192,1]{2,1,3,0:T(4,128)S(1)}, f32[2,4,192,1]{2,1,3,0:T(4,128)S(1)}, u32[]{:S(2)}, u32[]{:S(2)}) collective-permute-start(f32[2,4,192,1]{2,1,3,0:T(4,128)S(1)} %copy.35), channel_id=1, source_target_pairs={{0,2},{2,4},{4,6},{6,8},{8,10},{10,12},{12,14},{1,3},{3,5},{5,7},{... | collective-permute-start | bytes 18440 | tf_op jit(solution)/shard_map/ppermute | solution.py:26
  182.0 4.6 %collective-permute-done.27 = f32[2,4,192,1]{2,1,3,0:T(4,128)S(1)} collective-permute-done((f32[2,4,192,1]{2,1,3,0:T(4,128)S(1)}, f32[2,4,192,1]{2,1,3,0:T(4,128)S(1)}, u32[]{:S(2)}, u32[]{:S(2)}) %collective-permute-start.27) | collective-permute-done | bytes 6176 | tf_op jit(solution)/shard_map/ppermute | solution.py:27
  190.8 4.2 %collective-permute-done.29 = f32[2,4,1,130]{3,2,0,1:T(1,128)S(1)} collective-permute-done((f32[2,4,1,130]{3,2,0,1:T(1,128)S(1)}, f32[2,4,1,130]{3,2,0,1:T(1,128)S(1)}, u32[]{:S(2)}, u32[]{:S(2)}) %collective-permute-start.29) | collective-permute-done | bytes 4192 | tf_op jit(solution)/shard_map/ppermute | solution.py:27
  198.3 2.5 %psum.30 = bf16[2,16,128]{2,1,0:T(8,128)(2,1)S(1)} all-reduce(bf16[2,16,128]{2,1,0:T(8,128)(2,1)S(1)} %select_bitcast_fusion), channel_id=1, replica_groups=mesh['vol'=2,'wide'=8,'narrow'=2] {'vol'}, use_global_device_ids=true, to_apply=%region_2.3 | all-reduce | flops 4096 | bytes 16384 | tf_op jit(solution)/shard_map/psum | solution.py:34
  200.8 26.0 %all_gather.11 = bf16[1,16,1024]{2,1,0:T(8,128)(2,1)S(1)} all-gather(bf16[1,16,128]{2,1,0:T(8,128)(2,1)S(1)} %constant_dynamic-slice_fusion.1), channel_id=1, replica_groups=mesh['vol'=2,'wide'=8,'narrow'=2] {'wide'}, dimensions={2}, use_global_device_ids=true | all-gather | bytes 36864 | tf_op jit(solution)/shard_map/all_gather | solution.py:76
  226.8 2.9 %convolution_bitcast_fusion = f32[128,1]{0,1:T(1,128)S(1)} fusion(bf16[128,16,1024]{0,2,1:T(8,128)(2,1)} %bitcast.32, bf16[16,1024,1]{1,0,2:T(8,128)(2,1)S(1)} %bitcast.34), kind=kOutput, calls=%fused_computation.4 | convolution fusion | flops 4194304 | bytes 4227584 | tf_op jit(solution)/shard_map/ryx,kyx->rk/dot_general | solution.py:73
  229.7 4.9 %psum.31 = f32[128,1]{0,1:T(1,128)S(1)} all-reduce(f32[128,1]{0,1:T(1,128)S(1)} %convolution_bitcast_fusion), channel_id=1, replica_groups=mesh['vol'=2,'wide'=8,'narrow'=2] {'narrow'}, use_global_device_ids=true, to_apply=%region_3.4 | all-reduce | flops 128 | bytes 1024 | tf_op jit(solution)/shard_map/psum | solution.py:109
  (150 shorter events, 59.4 us)
Async XLA Ops:
  9.1 3.7 %collective-permute-start = (f32[1,192,128]{2,1,0:T(8,128)S(1)}, f32[1,192,128]{2,1,0:T(8,128)S(1)}, u32[]{:S(2)}, u32[]{:S(2)}) collective-permute-start(f32[1,192,128]{2,1,0:T(8,128)S(1)} %get-tuple-element.64), channel_id=1, source_target_pairs={{0,16},{1,17},{2,18},{3,19},{4,20},{5,21},{6,22},{7,23},{8,24},{9,... | collective-permute-start | bytes 294920 | tf_op jit(solution)/shard_map/ppermute | solution.py:26
  11.5 3.2 %collective-permute-start.1 = (f32[1,192,128]{2,1,0:T(8,128)S(1)}, f32[1,192,128]{2,1,0:T(8,128)S(1)}, u32[]{:S(2)}, u32[]{:S(2)}) collective-permute-start(f32[1,192,128]{2,1,0:T(8,128)S(1)} %get-tuple-element.65), channel_id=1, source_target_pairs={{16,0},{17,1},{18,2},{19,3},{20,4},{21,5},{22,6},{23,7},{24,8},{25... | collective-permute-start | bytes 294920 | tf_op jit(solution)/shard_map/ppermute | solution.py:27
  14.9 21.3 %collective-permute-start.2 = (f32[4,192,1]{2,1,0:T(8,128)S(1)}, f32[4,192,1]{2,1,0:T(8,128)S(1)}, u32[]{:S(2)}, u32[]{:S(2)}) collective-permute-start(f32[4,192,1]{2,1,0:T(8,128)S(1)} %get-tuple-element.62), channel_id=1, source_target_pairs={{0,2},{2,4},{4,6},{6,8},{8,10},{10,12},{12,14},{1,3},{3,5},{5,7},{... | collective-permute-start | bytes 9224 | tf_op jit(solution)/shard_map/ppermute | solution.py:26
  19.2 17.1 %collective-permute-start.3 = (f32[4,192,1]{2,1,0:T(8,128)S(1)}, f32[4,192,1]{2,1,0:T(8,128)S(1)}, u32[]{:S(2)}, u32[]{:S(2)}) collective-permute-start(f32[4,192,1]{2,1,0:T(8,128)S(1)} %get-tuple-element.63), channel_id=1, source_target_pairs={{2,0},{4,2},{6,4},{8,6},{10,8},{12,10},{14,12},{3,1},{5,3},{7,5},{... | collective-permute-start | bytes 9224 | tf_op jit(solution)/shard_map/ppermute | solution.py:27
  36.3 9.1 %collective-permute-start.4 = (f32[4,1,130]{2,1,0:T(1,128)S(1)}, f32[4,1,130]{2,1,0:T(1,128)S(1)}, u32[]{:S(2)}, u32[]{:S(2)}) collective-permute-start(f32[4,1,130]{2,1,0:T(1,128)S(1)} %get-tuple-element.44), channel_id=1, source_target_pairs={{0,1},{2,3},{4,5},{6,7},{8,9},{10,11},{12,13},{14,15},{16,17},{18,... | collective-permute-start | bytes 6248 | tf_op jit(solution)/shard_map/ppermute | solution.py:26
  39.8 5.7 %collective-permute-start.5 = (f32[4,1,130]{2,1,0:T(1,128)S(1)}, f32[4,1,130]{2,1,0:T(1,128)S(1)}, u32[]{:S(2)}, u32[]{:S(2)}) collective-permute-start(f32[4,1,130]{2,1,0:T(1,128)S(1)} %get-tuple-element.45), channel_id=1, source_target_pairs={{1,0},{3,2},{5,4},{7,6},{9,8},{11,10},{13,12},{15,14},{17,16},{19,... | collective-permute-start | bytes 6248 | tf_op jit(solution)/shard_map/ppermute | solution.py:27
  41.1 5.1 %collective-permute-start.7 = (f32[2,1,192,128]{3,2,0,1:T(8,128)S(1)}, f32[2,1,192,128]{3,2,0,1:T(8,128)S(1)}, u32[]{:S(2)}, u32[]{:S(2)}) collective-permute-start(f32[2,1,192,128]{3,2,0,1:T(8,128)S(1)} %broadcast.51), channel_id=1, source_target_pairs={{16,0},{17,1},{18,2},{19,3},{20,4},{21,5},{22,6},{23,7},{24,8},{25... | collective-permute-start | bytes 589832 | tf_op jit(solution)/shard_map/ppermute | solution.py:27
  42.4 4.1 %collective-permute-start.6 = (f32[2,1,192,128]{3,2,0,1:T(8,128)S(1)}, f32[2,1,192,128]{3,2,0,1:T(8,128)S(1)}, u32[]{:S(2)}, u32[]{:S(2)}) collective-permute-start(f32[2,1,192,128]{3,2,0,1:T(8,128)S(1)} %broadcast.51), channel_id=1, source_target_pairs={{0,16},{1,17},{2,18},{3,19},{4,20},{5,21},{6,22},{7,23},{8,24},{9,... | collective-permute-start | bytes 589832 | tf_op jit(solution)/shard_map/ppermute | solution.py:26
  46.5 11.4 %copy-start.7 = (f32[2,1,192,128]{3,2,0,1:T(8,128)}, f32[2,1,192,128]{3,2,0,1:T(8,128)S(1)}, u32[]{:S(2)}) copy-start(f32[2,1,192,128]{3,2,0,1:T(8,128)S(1)} %collective-permute-done.6) | copy-start | bytes 589828
  49.6 8.0 %collective-permute-start.9 = (f32[2,4,192,1]{2,1,3,0:T(4,128)S(1)}, f32[2,4,192,1]{2,1,3,0:T(4,128)S(1)}, u32[]{:S(2)}, u32[]{:S(2)}) collective-permute-start(f32[2,4,192,1]{2,1,3,0:T(4,128)S(1)} %copy.20), channel_id=1, source_target_pairs={{2,0},{4,2},{6,4},{8,6},{10,8},{12,10},{14,12},{3,1},{5,3},{7,5},{... | collective-permute-start | bytes 18440 | tf_op jit(solution)/shard_map/ppermute | solution.py:27
  50.9 6.4 %collective-permute-start.8 = (f32[2,4,192,1]{2,1,3,0:T(4,128)S(1)}, f32[2,4,192,1]{2,1,3,0:T(4,128)S(1)}, u32[]{:S(2)}, u32[]{:S(2)}) collective-permute-start(f32[2,4,192,1]{2,1,3,0:T(4,128)S(1)} %copy.19), channel_id=1, source_target_pairs={{0,2},{2,4},{4,6},{6,8},{8,10},{10,12},{12,14},{1,3},{3,5},{5,7},{... | collective-permute-start | bytes 18440 | tf_op jit(solution)/shard_map/ppermute | solution.py:26
  58.0 7.0 %collective-permute-start.10 = (f32[2,4,1,130]{3,2,0,1:T(1,128)S(1)}, f32[2,4,1,130]{3,2,0,1:T(1,128)S(1)}, u32[]{:S(2)}, u32[]{:S(2)}) collective-permute-start(f32[2,4,1,130]{3,2,0,1:T(1,128)S(1)} %get-tuple-element.42), channel_id=1, source_target_pairs={{0,1},{2,3},{4,5},{6,7},{8,9},{10,11},{12,13},{14,15},{16,17},{18,... | collective-permute-start | bytes 12488 | tf_op jit(solution)/shard_map/ppermute | solution.py:26
  62.6 5.5 %collective-permute-start.11 = (f32[2,4,1,130]{3,2,0,1:T(1,128)S(1)}, f32[2,4,1,130]{3,2,0,1:T(1,128)S(1)}, u32[]{:S(2)}, u32[]{:S(2)}) collective-permute-start(f32[2,4,1,130]{3,2,0,1:T(1,128)S(1)} %get-tuple-element.43), channel_id=1, source_target_pairs={{1,0},{3,2},{5,4},{7,6},{9,8},{11,10},{13,12},{15,14},{17,16},{19,... | collective-permute-start | bytes 12488 | tf_op jit(solution)/shard_map/ppermute | solution.py:27
  65.1 39.2 %copy-start = (f32[2,192,128]{2,1,0:T(8,128)}, f32[2,192,128]{2,1,0:T(8,128)S(1)}, u32[]{:S(2)}) copy-start(f32[2,192,128]{2,1,0:T(8,128)S(1)} %get-tuple-element.31) | copy-start | bytes 589828
  72.8 2.6 %collective-permute-start.12 = (f32[2,1,192,128]{3,2,0,1:T(8,128)S(1)}, f32[2,1,192,128]{3,2,0,1:T(8,128)S(1)}, u32[]{:S(2)}, u32[]{:S(2)}) collective-permute-start(f32[2,1,192,128]{3,2,0,1:T(8,128)S(1)} %get-tuple-element.60), channel_id=1, source_target_pairs={{0,16},{1,17},{2,18},{3,19},{4,20},{5,21},{6,22},{7,23},{8,24},{9,... | collective-permute-start | bytes 589832 | tf_op jit(solution)/shard_map/ppermute | solution.py:26
  74.1 3.3 %collective-permute-start.13 = (f32[2,1,192,128]{3,2,0,1:T(8,128)S(1)}, f32[2,1,192,128]{3,2,0,1:T(8,128)S(1)}, u32[]{:S(2)}, u32[]{:S(2)}) collective-permute-start(f32[2,1,192,128]{3,2,0,1:T(8,128)S(1)} %get-tuple-element.61), channel_id=1, source_target_pairs={{16,0},{17,1},{18,2},{19,3},{20,4},{21,5},{22,6},{23,7},{24,8},{25... | collective-permute-start | bytes 589832 | tf_op jit(solution)/shard_map/ppermute | solution.py:27
  78.8 6.5 %collective-permute-start.14 = (f32[2,4,192,1]{2,1,3,0:T(4,128)S(1)}, f32[2,4,192,1]{2,1,3,0:T(4,128)S(1)}, u32[]{:S(2)}, u32[]{:S(2)}) collective-permute-start(f32[2,4,192,1]{2,1,3,0:T(4,128)S(1)} %copy.24), channel_id=1, source_target_pairs={{0,2},{2,4},{4,6},{6,8},{8,10},{10,12},{12,14},{1,3},{3,5},{5,7},{... | collective-permute-start | bytes 18440 | tf_op jit(solution)/shard_map/ppermute | solution.py:26
  84.0 6.7 %collective-permute-start.15 = (f32[2,4,192,1]{2,1,3,0:T(4,128)S(1)}, f32[2,4,192,1]{2,1,3,0:T(4,128)S(1)}, u32[]{:S(2)}, u32[]{:S(2)}) collective-permute-start(f32[2,4,192,1]{2,1,3,0:T(4,128)S(1)} %copy.25), channel_id=1, source_target_pairs={{2,0},{4,2},{6,4},{8,6},{10,8},{12,10},{14,12},{3,1},{5,3},{7,5},{... | collective-permute-start | bytes 18440 | tf_op jit(solution)/shard_map/ppermute | solution.py:27
  91.9 9.4 %collective-permute-start.16 = (f32[2,4,1,130]{3,2,0,1:T(1,128)S(1)}, f32[2,4,1,130]{3,2,0,1:T(1,128)S(1)}, u32[]{:S(2)}, u32[]{:S(2)}) collective-permute-start(f32[2,4,1,130]{3,2,0,1:T(1,128)S(1)} %get-tuple-element.40), channel_id=1, source_target_pairs={{0,1},{2,3},{4,5},{6,7},{8,9},{10,11},{12,13},{14,15},{16,17},{18,... | collective-permute-start | bytes 12488 | tf_op jit(solution)/shard_map/ppermute | solution.py:26
  93.5 7.7 %collective-permute-start.17 = (f32[2,4,1,130]{3,2,0,1:T(1,128)S(1)}, f32[2,4,1,130]{3,2,0,1:T(1,128)S(1)}, u32[]{:S(2)}, u32[]{:S(2)}) collective-permute-start(f32[2,4,1,130]{3,2,0,1:T(1,128)S(1)} %get-tuple-element.41), channel_id=1, source_target_pairs={{1,0},{3,2},{5,4},{7,6},{9,8},{11,10},{13,12},{15,14},{17,16},{19,... | collective-permute-start | bytes 12488 | tf_op jit(solution)/shard_map/ppermute | solution.py:27
  134.0 11.0 %collective-permute-start.18 = (f32[2,1,192,128]{3,2,0,1:T(8,128)S(1)}, f32[2,1,192,128]{3,2,0,1:T(8,128)S(1)}, u32[]{:S(2)}, u32[]{:S(2)}) collective-permute-start(f32[2,1,192,128]{3,2,0,1:T(8,128)S(1)} %get-tuple-element.56), channel_id=1, source_target_pairs={{0,16},{1,17},{2,18},{3,19},{4,20},{5,21},{6,22},{7,23},{8,24},{9,... | collective-permute-start | bytes 589832 | tf_op jit(solution)/shard_map/ppermute | solution.py:26
  135.3 9.7 %collective-permute-start.19 = (f32[2,1,192,128]{3,2,0,1:T(8,128)S(1)}, f32[2,1,192,128]{3,2,0,1:T(8,128)S(1)}, u32[]{:S(2)}, u32[]{:S(2)}) collective-permute-start(f32[2,1,192,128]{3,2,0,1:T(8,128)S(1)} %get-tuple-element.57), channel_id=1, source_target_pairs={{16,0},{17,1},{18,2},{19,3},{20,4},{21,5},{22,6},{23,7},{24,8},{25... | collective-permute-start | bytes 589832 | tf_op jit(solution)/shard_map/ppermute | solution.py:27
  146.4 8.1 %collective-permute-start.21 = (f32[2,4,192,1]{2,1,3,0:T(4,128)S(1)}, f32[2,4,192,1]{2,1,3,0:T(4,128)S(1)}, u32[]{:S(2)}, u32[]{:S(2)}) collective-permute-start(f32[2,4,192,1]{2,1,3,0:T(4,128)S(1)} %copy.32), channel_id=1, source_target_pairs={{2,0},{4,2},{6,4},{8,6},{10,8},{12,10},{14,12},{3,1},{5,3},{7,5},{... | collective-permute-start | bytes 18440 | tf_op jit(solution)/shard_map/ppermute | solution.py:27
  147.7 6.4 %collective-permute-start.20 = (f32[2,4,192,1]{2,1,3,0:T(4,128)S(1)}, f32[2,4,192,1]{2,1,3,0:T(4,128)S(1)}, u32[]{:S(2)}, u32[]{:S(2)}) collective-permute-start(f32[2,4,192,1]{2,1,3,0:T(4,128)S(1)} %copy.31), channel_id=1, source_target_pairs={{0,2},{2,4},{4,6},{6,8},{8,10},{10,12},{12,14},{1,3},{3,5},{5,7},{... | collective-permute-start | bytes 18440 | tf_op jit(solution)/shard_map/ppermute | solution.py:26
  155.7 5.3 %collective-permute-start.22 = (f32[2,4,1,130]{3,2,0,1:T(1,128)S(1)}, f32[2,4,1,130]{3,2,0,1:T(1,128)S(1)}, u32[]{:S(2)}, u32[]{:S(2)}) collective-permute-start(f32[2,4,1,130]{3,2,0,1:T(1,128)S(1)} %get-tuple-element.38), channel_id=1, source_target_pairs={{0,1},{2,3},{4,5},{6,7},{8,9},{10,11},{12,13},{14,15},{16,17},{18,... | collective-permute-start | bytes 12488 | tf_op jit(solution)/shard_map/ppermute | solution.py:26
  159.7 5.5 %collective-permute-start.23 = (f32[2,4,1,130]{3,2,0,1:T(1,128)S(1)}, f32[2,4,1,130]{3,2,0,1:T(1,128)S(1)}, u32[]{:S(2)}, u32[]{:S(2)}) collective-permute-start(f32[2,4,1,130]{3,2,0,1:T(1,128)S(1)} %get-tuple-element.39), channel_id=1, source_target_pairs={{1,0},{3,2},{5,4},{7,6},{9,8},{11,10},{13,12},{15,14},{17,16},{19,... | collective-permute-start | bytes 12488 | tf_op jit(solution)/shard_map/ppermute | solution.py:27
  169.3 2.6 %collective-permute-start.24 = (f32[2,1,192,128]{3,2,0,1:T(8,128)S(1)}, f32[2,1,192,128]{3,2,0,1:T(8,128)S(1)}, u32[]{:S(2)}, u32[]{:S(2)}) collective-permute-start(f32[2,1,192,128]{3,2,0,1:T(8,128)S(1)} %get-tuple-element.54), channel_id=1, source_target_pairs={{0,16},{1,17},{2,18},{3,19},{4,20},{5,21},{6,22},{7,23},{8,24},{9,... | collective-permute-start | bytes 589832 | tf_op jit(solution)/shard_map/ppermute | solution.py:26
  170.6 3.3 %collective-permute-start.25 = (f32[2,1,192,128]{3,2,0,1:T(8,128)S(1)}, f32[2,1,192,128]{3,2,0,1:T(8,128)S(1)}, u32[]{:S(2)}, u32[]{:S(2)}) collective-permute-start(f32[2,1,192,128]{3,2,0,1:T(8,128)S(1)} %get-tuple-element.55), channel_id=1, source_target_pairs={{16,0},{17,1},{18,2},{19,3},{20,4},{21,5},{22,6},{23,7},{24,8},{25... | collective-permute-start | bytes 589832 | tf_op jit(solution)/shard_map/ppermute | solution.py:27
  175.3 6.4 %collective-permute-start.26 = (f32[2,4,192,1]{2,1,3,0:T(4,128)S(1)}, f32[2,4,192,1]{2,1,3,0:T(4,128)S(1)}, u32[]{:S(2)}, u32[]{:S(2)}) collective-permute-start(f32[2,4,192,1]{2,1,3,0:T(4,128)S(1)} %copy.35), channel_id=1, source_target_pairs={{0,2},{2,4},{4,6},{6,8},{8,10},{10,12},{12,14},{1,3},{3,5},{5,7},{... | collective-permute-start | bytes 18440 | tf_op jit(solution)/shard_map/ppermute | solution.py:26
  180.4 6.2 %collective-permute-start.27 = (f32[2,4,192,1]{2,1,3,0:T(4,128)S(1)}, f32[2,4,192,1]{2,1,3,0:T(4,128)S(1)}, u32[]{:S(2)}, u32[]{:S(2)}) collective-permute-start(f32[2,4,192,1]{2,1,3,0:T(4,128)S(1)} %copy.36), channel_id=1, source_target_pairs={{2,0},{4,2},{6,4},{8,6},{10,8},{12,10},{14,12},{3,1},{5,3},{7,5},{... | collective-permute-start | bytes 18440 | tf_op jit(solution)/shard_map/ppermute | solution.py:27
  187.7 3.0 %collective-permute-start.28 = (f32[2,4,1,130]{3,2,0,1:T(1,128)S(1)}, f32[2,4,1,130]{3,2,0,1:T(1,128)S(1)}, u32[]{:S(2)}, u32[]{:S(2)}) collective-permute-start(f32[2,4,1,130]{3,2,0,1:T(1,128)S(1)} %get-tuple-element.36), channel_id=1, source_target_pairs={{0,1},{2,3},{4,5},{6,7},{8,9},{10,11},{12,13},{14,15},{16,17},{18,... | collective-permute-start | bytes 12488 | tf_op jit(solution)/shard_map/ppermute | solution.py:26
  189.4 5.5 %collective-permute-start.29 = (f32[2,4,1,130]{3,2,0,1:T(1,128)S(1)}, f32[2,4,1,130]{3,2,0,1:T(1,128)S(1)}, u32[]{:S(2)}, u32[]{:S(2)}) collective-permute-start(f32[2,4,1,130]{3,2,0,1:T(1,128)S(1)} %get-tuple-element.37), channel_id=1, source_target_pairs={{1,0},{3,2},{5,4},{7,6},{9,8},{11,10},{13,12},{15,14},{17,16},{19,... | collective-permute-start | bytes 12488 | tf_op jit(solution)/shard_map/ppermute | solution.py:27
  (16 other events, 50.4 us)
where the time goes:
time: 237 us; the launch traced here: 236 us
  blocking collectives  69.3 us (29%)
  starting transfers between devices  67.3 us (28%)
  waiting for transfers between devices  43.7 us (18%)
  other arithmetic  24.9 us (11%)
  local copies, waits for them, and re-layouts  23.5 us (10%)
  matrix products  5.73 us (2%)
    all_gather x2, blocking collectives, fold_traces(): lax.all_gather(mine, 'wide', axis=2, tiled=True)  52 us
    ppermute x15, starting transfers between devices, with_halo(): before = lax.ppermute(last, axis, up)  47.9 us
    ppermute x15, waiting for transfers between devices, with_halo(): after = lax.ppermute(first, axis, down)  27 us
    ppermute x15, starting transfers between devices, with_halo(): after = lax.ppermute(first, axis, down)  19.4 us
    ppermute x15, waiting for transfers between devices, with_halo(): before = lax.ppermute(last, axis, up)  16.7 us
    mul x5, other arithmetic, apply_operator(): weighted = box_sum(padded * cond_pad) - conductance * center  11.6 us
    psum x2, blocking collectives, local(): summed = lax.psum(partial_rows, 'narrow')  10.5 us
    reshape x1, local copies, waits for them, and re-layouts, local(): plane = boundary_operator.reshape(tile_rows, BY, -1)  6.41 us
  transfers between devices with their start and end apart: 30, of which 11 were waited for; matrix products, arithmetic and copies ran while one was open for 6% of the time, Pallas kernels for 0%

commit v1 on v0

v1 whole, which is shorter than its diff:
```python
import jax
import jax.numpy as jnp
from jax import lax
from jax.experimental import pallas as pl
from jax.experimental.pallas import tpu as pltpu
from jax.sharding import PartitionSpec as P

BY = 16
HALO = 4
TILE = 8
LANES = 128

lower_edge = 0.25
upper_edge = 1.75
mass_ratio = 26.0
couple_gain = 40.0


def sweep_weights():
    middle = (upper_edge + lower_edge) / 2.0
    spread = (upper_edge - lower_edge) / 2.0
    center_ratio = middle / spread
    ratio_last = 1.0 / center_ratio
    ratio_next = 1.0 / (2.0 * center_ratio - ratio_last)
    return 1.0 / middle, ratio_next * ratio_last, 2.0 * ratio_next / spread


GAIN0, KEEP1, GAIN1 = sweep_weights()


def lookup(ids, table):
    found = jnp.zeros(ids.shape, jnp.float32)
    for number in range(table.shape[0]):
        found = jnp.where(ids == number, table[number], found)
    return found


def layer(own, other, m, v):
    return (own if m < 2 else other), (v if m % 2 == 0 else 1 - v)


def nt(a, b):
    return lax.dot_general(a, b, (((1,), (1,)), ((), ())), preferred_element_type=jnp.float32)


def rows_kernel(table, f_own, f_oth, id_own, id_oth, out):
    v, n = lax.axis_index("vol"), lax.axis_index("narrow")
    excite, _, cells_y, _ = f_own.shape
    for m in range(4):
        for e in range(excite):
            ref, li = layer(f_own, f_oth, m, v)
            out[e * 4 + m] = jnp.where(
                n == 0, ref[e, li, cells_y - HALO : cells_y, :], ref[e, li, 0:HALO, :]
            )
        ref, li = layer(id_own, id_oth, m, v)
        picked = jnp.where(n == 0, ref[li, cells_y - HALO : cells_y, :], ref[li, 0:HALO, :])
        out[excite * 4 + m] = lookup(picked, table)


def turn_kernel(table, f_own, f_oth, id_own, id_oth, got, turned, even, odd, pad):
    v, w, n = lax.axis_index("vol"), lax.axis_index("wide"), lax.axis_index("narrow")
    excite, _, cells_y, cells_x = f_own.shape
    width = pad.shape[1]
    for slab in range(excite * 4 + 4):
        m = slab % 4
        if slab < excite * 4:
            ref, li = layer(f_own, f_oth, m, v)
            block = ref[slab // 4, li]
        else:
            ref, li = layer(id_own, id_oth, m, v)
            block = lookup(ref[li], table)
        pad[slab, 0:cells_y] = block
        pad[slab, cells_y:width] = jnp.zeros((width - cells_y, cells_x), jnp.float32)
        rows = got[slab]
        pad[slab, cells_y : cells_y + HALO] = jnp.where(n == 0, rows, 0.0)
        pad[slab, width - HALO : width] = jnp.where(n == 0, 0.0, rows)
        flat = pad[slab].T
        turned[slab] = flat
        first, last = flat[0:HALO], flat[cells_x - HALO : cells_x]
        left = lax.rem(w, 2) == 0
        even[slab] = jnp.where(left, last, first)
        odd[slab] = jnp.where(left, first, last)


def sweep_kernel(turned, even, odd, pressure, trace, aux, near, ext, hh, qq, uu, cu, mv):
    v, w = lax.axis_index("vol"), lax.axis_index("wide")
    excite = pressure.shape[0]
    cells_y, cells_x = pressure.shape[2], pressure.shape[3]
    rows, width = ext.shape[1], ext.shape[2]
    right = TILE + cells_x
    left = lax.rem(w, 2) == 0
    for slab in range(ext.shape[0]):
        ext[slab, 0:TILE] = jnp.zeros((TILE, width), jnp.float32)
        ext[slab, right : right + TILE] = jnp.zeros((TILE, width), jnp.float32)
        ext[slab, TILE:right] = turned[slab]
        ext[slab, TILE - HALO : TILE] = jnp.where(left, odd[slab], even[slab])
        ext[slab, right : right + HALO] = jnp.where(left, even[slab], odd[slab])

    def box(ref, first, m):
        total = ref[first + m]
        for z in (m - 1, m + 1):
            if 0 <= z < 4:
                total = total + ref[first + z]
        total = total + pltpu.roll(total, 1, 0) + pltpu.roll(total, rows - 1, 0)
        return total + pltpu.roll(total, 1, 1) + pltpu.roll(total, width - 1, 1)

    base = excite * 4
    for m in range(4):
        c = ext[base + m]
        diagonal = 0.5 * (26.0 * c + (box(ext, base, m) - c)) + mass_ratio * c
        inverse = jnp.where(c > 0.0, 1.0 / diagonal, 0.0)
        hh[m] = 0.5 * inverse
        for e in range(excite):
            q = ext[e * 4 + m] * inverse
            qq[e * 4 + m] = q
            uu[0, e * 4 + m] = GAIN0 * q
            cu[0, e * 4 + m] = (GAIN0 * q) * c

    def residual(slot, e, m):
        u, c = uu[slot, e * 4 + m], ext[base + m]
        near_sum = box(uu.at[slot], e * 4, m) - u
        weighted = box(cu.at[slot], e * 4, m) - cu[slot, e * 4 + m]
        return (qq[e * 4 + m] - u) + hh[m] * (c * near_sum + weighted)

    for e in range(excite):
        for m in range(4):
            p = (1.0 + KEEP1) * uu[0, e * 4 + m] + GAIN1 * residual(0, e, m)
            uu[1, e * 4 + m] = p
            cu[1, e * 4 + m] = p * ext[base + m]
        for m in range(3):
            step = GAIN0 * residual(1, e, m)
            p = uu[1, e * 4 + m] + step
            mv[e * 4 + m] = step
            uu[2, e * 4 + m] = p
            cu[2, e * 4 + m] = p * ext[base + m]
        for m in range(2):
            uu[3, e * 4 + m] = (
                uu[2, e * 4 + m] + KEEP1 * mv[e * 4 + m] + GAIN1 * residual(2, e, m)
            )

    columns = 2 * excite
    r = lax.broadcasted_iota(jnp.int32, trace.shape[:1] + (width,), 0)
    lane = lax.broadcasted_iota(jnp.int32, trace.shape[:1] + (width,), 1)
    s = lax.div(r, columns)
    hit = lane == s * (cells_y // BY)
    picked = jnp.zeros(trace.shape, jnp.float32)
    for col in range(columns):
        e, late = col % excite, col >= excite
        match = hit & (lax.rem(r, columns) == col)
        if late:
            match = match & (s > 0)
        values = uu[3 if late else 1, e * 4, TILE:right].astype(jnp.bfloat16)
        picked = picked + nt(jnp.where(match, 1.0, 0.0).astype(jnp.bfloat16), values)
    trace[...] = picked.astype(jnp.bfloat16)

    aux[...] = jnp.zeros(aux.shape, jnp.float32)
    near[...] = jnp.zeros(near.shape, jnp.float32)
    for m in range(2):
        li = v if m == 0 else 1 - v
        for e in range(excite):
            back = uu[3, e * 4 + m, TILE:right].T
            pressure[e, li] = back[0:cells_y]
            if m == 0:
                aux[e : e + 1] = back[0:1]
        for k, source in enumerate((ext[base + m, TILE:right], hh[m, TILE:right])):
            back = source.T
            for i, y in enumerate((0, 1, cells_y - 1)):
                row = 6 * k + 3 * m + i
                near[row : row + 1] = back[y : y + 1]
            if m == 0:
                aux[excite + k : excite + k + 1] = back[0:1]


def product_kernel(blocks, operator, aux, out):
    w = lax.axis_index("wide")
    count = blocks.shape[0]
    tile_rows = operator.shape[0]
    odd = lax.rem(w, 2)

    def pair(p, sums):
        base = lax.div(w ^ (2 * p), 2) * 2
        low, high = blocks[2 * p + odd], blocks[2 * p + 1 - odd]
        both = jnp.concatenate([low, high], axis=1)
        sums = list(sums)
        for s in range(BY):
            start = pl.multiple_of(s * count * LANES + base * LANES, LANES)
            group = s // 4 * 16
            sums[s % 4] = sums[s % 4] + nt(both[group : group + 16], operator[:, pl.ds(start, 2 * LANES)])
        return tuple(sums)

    zero = jnp.zeros((16, tile_rows), jnp.float32)
    sums = lax.fori_loop(0, count // 2, pair, (zero,) * 4)
    r = lax.broadcasted_iota(jnp.int32, zero.shape, 0)
    total = zero
    for q in range(4):
        total = total + jnp.where((r >= 4 * q) & (r < 4 * q + 4), sums[q], 0.0)
    total = total[0:8] + total[8:16]
    total = total + pltpu.roll(total, 4, 0)
    r = lax.broadcasted_iota(jnp.int32, total.shape, 0)
    out[...] = jnp.where(r < 4, total, pltpu.roll(aux[...], 4, 0))


def couple_kernel(blocks, mine, theirs, traction, fix, flat, save):
    v, w, n = lax.axis_index("vol"), lax.axis_index("wide"), lax.axis_index("narrow")
    count = blocks.shape[0]
    excite = 2
    targets = mine.shape[0]
    for j in range(count):
        flat[pl.ds(j * 16, 8), :] = blocks[w ^ j, 0]
        flat[pl.ds(j * 16 + 8, 8), :] = blocks[w ^ j, 1]

    def field(k, r):
        return flat[pl.ds(k * 8 + r, count, stride=16), :]

    lane = lax.broadcasted_iota(jnp.int32, (count, LANES), 1)
    sub = lax.broadcasted_iota(jnp.int32, (count, LANES), 0)

    def before(a):
        return pltpu.roll(a, 1, 1)

    def after(a):
        moved = pltpu.roll(a, LANES - 1, 1)
        following = jnp.where(sub == count - 1, 0.0, pltpu.roll(moved, count - 1, 0))
        return jnp.where(lane == LANES - 1, following, moved)

    own = (1.0 + KEEP1) * GAIN0 + GAIN1 - GAIN1 * GAIN0
    sides = []
    for k in range(2):
        c, h = field(k, 4 + excite), field(k, 5 + excite)
        rows = []
        for e in range(excite):
            t = field(0, e) + field(1, e)
            if k:
                t = pltpu.roll(t, LANES - targets, 1)
            t = jnp.where(lane < targets, t, 0.0)
            u = (2.0 * couple_gain) * h * t
            cu = c * u
            around, c_around = before(u) + after(u), before(cu) + after(cu)
            change = own * u + (GAIN0 * GAIN1) * h * (c * around + c_around)
            save[k, 0, e] = change
            save[k, 1, e] = around + u
            save[k, 2, e] = c_around + cu
            rows.append(field(k, 4 + e) + change)
        sides.append(rows)

    groups = count // 8
    total = jnp.zeros((16, targets), jnp.float32)
    r = lax.broadcasted_iota(jnp.int32, total.shape, 0)
    for g in range(groups):
        both = [
            jnp.concatenate([sides[k][e][8 * g : 8 * g + 8] for e in range(excite)], axis=0)
            for k in range(2)
        ]
        for ref, left in (
            (mine, jnp.where(n == 0, both[0], both[1])),
            (theirs, jnp.where(n == 0, both[1], both[0])),
        ):
            left = left.astype(jnp.bfloat16)
            for j in range(8):
                part = nt(left, ref[:, (8 * g + j) * LANES : (8 * g + j + 1) * LANES])
                total = total + jnp.where((r & 7) == j, part, 0.0)
    first = blocks[0, 0] + blocks[0, 1]
    first = jnp.where(n == 0, first, pltpu.roll(first, LANES - targets, 1))
    traction[...] = jnp.zeros(traction.shape, jnp.float32)
    for e in range(excite):
        traction[e : e + 1, 0:targets] = (
            jnp.sum(total[8 * e : 8 * e + 8], axis=0, keepdims=True)
            + first[2 + e : 3 + e, 0:targets]
        )

    top = v == lax.axis_size("vol") - 1
    fix[...] = jnp.zeros(fix.shape, jnp.float32)
    for e in range(excite):
        for i in range(3):
            row = 2 * i + e
            fix[row : row + 1] = jnp.where(top, save[n, i, e, pl.ds(w, 1), :], 0.0)
        for i in range(1, 3):
            row = 4 + 2 * i + e
            fix[row : row + 1] = jnp.where(
                top & (n == 0), save[1, i, e, pl.ds(w, 1), :], 0.0
            )


def mend_kernel(pressure, near, fix, out):
    v = lax.axis_index("vol")
    excite, _, cells_y, cells_x = pressure.shape
    r = lax.broadcasted_iota(jnp.int32, (8, cells_x), 0)
    out[...] = pressure[...]
    for e in range(excite):
        for m in range(2):
            li = v if m == 0 else 1 - v

            def change(i, a, b):
                c, h = near[3 * m + i : 3 * m + i + 1], near[6 + 3 * m + i : 7 + 3 * m + i]
                return (GAIN0 * GAIN1) * h * (c * fix[a + e : a + e + 1] + fix[b + e : b + e + 1])

            row0 = fix[e : e + 1] if m == 0 else change(0, 2, 4)
            delta = jnp.where(r == 0, row0, jnp.where(r == 1, change(1, 2, 4), 0.0))
            out[e, li, 0:8] = pressure[e, li, 0:8] + delta
            delta = jnp.where(r == 7, change(2, 6, 8), 0.0)
            out[e, li, cells_y - 8 : cells_y] = pressure[e, li, cells_y - 8 : cells_y] + delta


def local(forcing, material_ids, materials, boundary_operator):
    vols, wides, narrows = (lax.axis_size(a) for a in ("vol", "wide", "narrow"))
    v, w, n = lax.axis_index("vol"), lax.axis_index("wide"), lax.axis_index("narrow")
    excite, layers, cells_y, cells_x = forcing.shape
    assert (vols, narrows, excite, layers, cells_x) == (2, 2, 2, 2, LANES)
    assert wides % 8 == 0 and wides & (wides - 1) == 0
    tile_rows = boundary_operator.shape[0]
    targets = tile_rows // narrows
    assert tile_rows == LANES and BY * 2 * excite == 64
    width = -(-(cells_y + 2 * HALO) // LANES) * LANES
    slabs = 4 * excite + 4
    f32, bf16 = jnp.float32, jnp.bfloat16
    everyone = ("vol", "wide", "narrow")
    vmem, smem = pl.BlockSpec(memory_space=pltpu.VMEM), pl.BlockSpec(memory_space=pltpu.SMEM)

    def call(kernel, shapes, specs, scratch=()):
        return pl.pallas_call(
            kernel,
            out_shape=[jax.ShapeDtypeStruct(*s) for s in shapes],
            in_specs=specs,
            out_specs=[vmem] * len(shapes),
            scratch_shapes=list(scratch),
        )

    def swap(x, axis):
        return lax.ppermute(x, axis, [(0, 1), (1, 0)])

    def number(a, b, c):
        return (a * wides + b) * narrows + c

    def top_permute(x, partner):
        return lax.ppermute(
            x,
            everyone,
            [
                (number(vols - 1, b, c), number(vols - 1, *partner(b, c)))
                for b in range(wides)
                for c in range(narrows)
            ],
        )

    f_other, id_other = swap(forcing, "vol"), swap(material_ids, "vol")
    cells = (forcing, f_other, material_ids, id_other)
    (edge,) = call(rows_kernel, [((slabs, HALO, cells_x), f32)], [smem] + [vmem] * 4)(
        materials, *cells
    )
    edge = swap(edge, "narrow")
    head = boundary_operator[:, : wides * LANES]
    mine = lax.dynamic_slice_in_dim(head, n * targets, targets, 0)
    theirs = swap(lax.dynamic_slice_in_dim(head, (1 - n) * targets, targets, 0), "narrow")
    turned, even, odd = call(
        turn_kernel,
        [((slabs, cells_x, width), f32)] + [((slabs, HALO, width), f32)] * 2,
        [smem] + [vmem] * 5,
        [pltpu.VMEM((slabs, width, cells_x), f32)],
    )(materials, *cells, edge)
    even_pairs = [(i, i ^ 1) for i in range(wides)]
    odd_pairs = [(i, i + 1 if i % 2 else i - 1) for i in range(1, wides - 1)]
    even, odd = lax.ppermute(even, "wide", even_pairs), lax.ppermute(odd, "wide", odd_pairs)
    rows = cells_x + 2 * TILE
    full = (rows, width)
    pressure, trace, aux, near = call(
        sweep_kernel,
        [
            (forcing.shape, f32),
            ((BY * 2 * excite, cells_x), bf16),
            ((8, cells_x), f32),
            ((16, cells_x), f32),
        ],
        [vmem] * 3,
        [
            pltpu.VMEM((slabs,) + full, f32),
            pltpu.VMEM((4,) + full, f32),
            pltpu.VMEM((4 * excite,) + full, f32),
            pltpu.VMEM((4, 4 * excite) + full, f32),
            pltpu.VMEM((3, 4 * excite) + full, f32),
            pltpu.VMEM((4 * excite,) + full, f32),
        ],
    )(turned, even, odd)

    def gather(block):
        step = 1
        while step < wides:
            other = top_permute(block, lambda b, c: (b ^ step, c))
            block = jnp.concatenate([block, other], axis=0)
            step *= 2
        return block

    blocks = gather(trace[None])
    (sums,) = call(product_kernel, [((8, tile_rows), f32)], [vmem] * 3)(
        blocks, boundary_operator, aux
    )
    other = top_permute(sums, lambda b, c: (b, 1 - c))
    pair = jnp.stack([jnp.where(n == 0, sums, other), jnp.where(n == 0, other, sums)])
    blocks = gather(pair[None])
    traction, fix = call(
        couple_kernel,
        [((8, LANES), f32), ((16, cells_x), f32)],
        [vmem] * 3,
        [pltpu.VMEM((wides * 16, LANES), f32), pltpu.VMEM((2, 3, excite, wides, LANES), f32)],
    )(blocks, mine, theirs)
    (pressure,) = call(mend_kernel, [(forcing.shape, f32)], [vmem] * 3)(pressure, near, fix)
    lower = lax.ppermute(traction[0:1, :targets], "vol", [(1, 0)])
    column = jnp.where(v == vols - 1, traction[1:2, :targets], lower)
    return pressure, column.reshape(targets, 1)


def solution(mesh):
    placed = (
        P(None, "vol", "narrow", "wide"),
        P("vol", "narrow", "wide"),
        P(),
        P("wide", "narrow"),
    )
    return jax.shard_map(
        local,
        mesh=mesh,
        in_specs=placed,
        out_specs=(P(None, "vol", "narrow", "wide"), P(("wide", "narrow"), "vol")),
        check_vma=False,
    )
```

time: 237 us -> 81.9 us (0.35)
  blocking collectives: 69.3 us -> 0 us
  starting transfers between devices: 67.3 us -> 14 us
  other arithmetic: 24.9 us -> 5.34 us
  Pallas kernels: 0 us -> 19.3 us
  local copies, waits for them, and re-layouts: 23.5 us -> 4.67 us
  waiting for transfers between devices: 43.7 us -> 36.3 us
  matrix products: 5.73 us -> 0 us
    all_gather x3 -> x0, blocking collectives: 53.8 us -> none  [the longest x2 52 us: fold_traces(): lax.all_gather(mine, 'wide', axis=2, tiled=True)]
    ppermute x30 -> x14, starting transfers between devices: 67.3 us -> 14 us  [the longest x4 5.54 us: swap(): return lax.ppermute(x, axis, [(0, 1), (1, 0)])]
    pallas_call x0 -> x6, Pallas kernels: none -> 19.3 us  [the longest x1 6.38 us: local(): call(sweep_kernel, [(forcing.shape, f32), ((BY * 2 * excite, cells_x), bf...]
    psum x4 -> x0, blocking collectives: 15.5 us -> none  [the longest x2 10.5 us: local(): summed = lax.psum(partial_rows, 'narrow')]
    mul x6 -> x0, other arithmetic: 12.8 us -> none  [the longest x5 11.6 us: apply_operator(): weighted = box_sum(padded * cond_pad) - conductance * center]
    ppermute x30 -> x14, waiting for transfers between devices: 43.7 us -> 36.3 us  [the longest x1 28.5 us: local(): lower = lax.ppermute(traction[0:1, :targets], 'vol', [(1, 0)])]
    add x18 -> x0, other arithmetic: 7.19 us -> none  [the longest x8 4.11 us: box_sum(): along = padded[..., :-2] + padded[..., 1:-1] + padded[..., 2:]]
    slice x20 -> x3, local copies, waits for them, and re-layouts: 7.8 us -> 0.68 us  [the longest x1 0.67 us: local(): lower = lax.ppermute(traction[0:1, :targets], 'vol', [(1, 0)])]
  transfers between devices with their start and end apart: 30 -> 14, of which waited for: 11 -> 5; matrix products, arithmetic and copies ran while one was open for 6% -> 2% of each run, Pallas kernels for 0% -> 2%
where the time goes in v1:
time: 81.9 us; the launch traced here: 80.5 us
  waiting for transfers between devices  36.3 us (44%)
  Pallas kernels  19.3 us (24%)
  starting transfers between devices  14 us (17%)
  other arithmetic  5.34 us (7%)
  local copies, waits for them, and re-layouts  4.67 us (6%)
    ppermute x1, waiting for transfers between devices, local(): lower = lax.ppermute(traction[0:1, :targets], 'vol', [(1, 0)])  28.5 us
    pallas_call x1, Pallas kernels, local(): call(sweep_kernel, [(forcing.shape, f32), ((BY * 2 * excite, cells_x), bf...  6.38 us
    ppermute x4, waiting for transfers between devices, swap(): return lax.ppermute(x, axis, [(0, 1), (1, 0)])  6.09 us
    ppermute x4, starting transfers between devices, swap(): return lax.ppermute(x, axis, [(0, 1), (1, 0)])  5.54 us
    ppermute x7, starting transfers between devices, top_permute(): lax.ppermute(x, everyone, [(number(vols - 1, b, c), number(vols - 1, *par...  4.58 us
    pallas_call x1, Pallas kernels, local(): call(product_kernel, [((8, tile_rows), f32)], [vmem] * 3)  4.33 us
    concatenate x6, other arithmetic, gather(): block = jnp.concatenate([block, other], axis=0)  3.48 us
    unnamed x12, local copies, waits for them, and re-layouts  3.31 us
  transfers between devices with their start and end apart: 14, of which 5 were waited for; matrix products, arithmetic and copies ran while one was open for 2% of the time, Pallas kernels for 2%

profile of v1, /device:TPU:0, one launch (start us, length us, event | category | flops | bytes accessed | tf_op | source)
XLA Modules:
  0.0 80.5 jit_solution(5539211515713347651)
XLA Ops:
  1.3 1.8 %collective-permute-done.1.id_oth = s32[2,192,128]{2,1,0:T(8,128)S(1)} collective-permute-done((s32[2,192,128]{2,1,0:T(8,128)}, s32[2,192,128]{2,1,0:T(8,128)S(1)}, u32[]{:S(2)}, u32[]{:S(2)}) %collective-permute-start.1) | collective-permute-done | bytes 196640 | tf_op jit(solution)/shard_map/ppermute | solution.py:329
  3.0 0.7 copy-done.1
  3.7 0.7 copy-done
  4.5 1.9 %shard_map.59 = f32[12,4,128]{2,1,0:T(4,128)} custom-call(f32[8]{0:T(128)} %table.3, f32[2,2,192,128]{3,2,1,0:T(8,128)} %f_own.3, f32[2,2,192,128]{3,2,1,0:T(8,128)} %copy-done, s32[2,192,128]{2,1,0:T(8,128)} %id_own.3, s32[2,192,128]{2,1,0:T(8,128)} %copy-done.1), custom_call_target="tpu_custom_call" | custom-call | tf_op jit(solution)/shard_map/pallas_call | solution.py:347
  6.3 2.9 %collective-permute-start.2 = (f32[12,4,128]{2,1,0:T(4,128)}, f32[12,4,128]{2,1,0:T(4,128)S(1)}, u32[]{:S(2)}, u32[]{:S(2)}) collective-permute-start(f32[12,4,128]{2,1,0:T(4,128)} %shard_map.59), channel_id=1, source_target_pairs={{0,1},{1,0},{2,3},{3,2},{4,5},{5,4},{6,7},{7,6},{8,9},{9,8},{10,11... | collective-permute-start | bytes 73736 | tf_op jit(solution)/shard_map/ppermute | solution.py:329
  9.2 2.0 %collective-permute-done.2.got = f32[12,4,128]{2,1,0:T(4,128)S(1)} collective-permute-done((f32[12,4,128]{2,1,0:T(4,128)}, f32[12,4,128]{2,1,0:T(4,128)S(1)}, u32[]{:S(2)}, u32[]{:S(2)}) %collective-permute-start.2) | collective-permute-done | bytes 24608 | tf_op jit(solution)/shard_map/ppermute | solution.py:329
  11.8 3.0 %shard_map.60 = (f32[12,128,256]{2,1,0:T(8,128)}, f32[12,4,256]{2,1,0:T(4,128)}, f32[12,4,256]{2,1,0:T(4,128)}) custom-call(f32[8]{0:T(128)} %table.3, f32[2,2,192,128]{3,2,1,0:T(8,128)} %f_own.3, f32[2,2,192,128]{3,2,1,0:T(8,128)} %copy-done, s32[2,192,128]{2,1,0:T(8,128)} %id_own.3, s32[2,192,128]{2,1,0:T(8,128)} %copy-done.1, f32[12,4,128]{2,1,0:T(4,128)} %copy-done.5), custom_call_target="tpu_custom_call" | custom-call | tf_op jit(solution)/shard_map/pallas_call | solution.py:354
  14.8 2.0 %collective-permute-start.3 = (f32[12,4,256]{2,1,0:T(4,128)}, f32[12,4,256]{2,1,0:T(4,128)S(1)}, u32[]{:S(2)}, u32[]{:S(2)}) collective-permute-start(f32[12,4,256]{2,1,0:T(4,128)} %get-tuple-element.12), channel_id=1, source_target_pairs={{0,2},{2,0},{4,6},{6,4},{8,10},{10,8},{12,14},{14,12},{1,3},{3,1},... | collective-permute-start | bytes 147464 | tf_op jit(solution)/shard_map/ppermute | solution.py:362
  16.8 0.7 collective-permute-start.4
  17.5 1.6 %collective-permute-done.3.even = f32[12,4,256]{2,1,0:T(4,128)S(1)} collective-permute-done((f32[12,4,256]{2,1,0:T(4,128)}, f32[12,4,256]{2,1,0:T(4,128)S(1)}, u32[]{:S(2)}, u32[]{:S(2)}) %collective-permute-start.3) | collective-permute-done | bytes 49184 | tf_op jit(solution)/shard_map/ppermute | solution.py:362
  19.7 6.4 %shard_map.61 = (f32[2,2,192,128]{3,2,1,0:T(8,128)}, bf16[64,128]{1,0:T(8,128)(2,1)}, f32[8,128]{1,0:T(8,128)}, f32[16,128]{1,0:T(8,128)}) custom-call(f32[12,128,256]{2,1,0:T(8,128)} %get-tuple-element.11.turned, f32[12,4,256]{2,1,0:T(4,128)} %copy-done.3, f32[12,4,256]{2,1,0:T(4,128)} %copy-done.4), custom_call_target="tpu_custom_call" | custom-call | tf_op jit(solution)/shard_map/pallas_call | solution.py:365
  26.1 0.7 collective-permute-start.5
  26.8 0.7 pad_maximum_fusion.3
  27.5 0.7 collective-permute-start.6
  28.2 0.7 pad_maximum_fusion.1
  28.9 0.7 collective-permute-start.7
  29.6 1.4 %pad_maximum_fusion.blocks = bf16[8,64,128]{2,1,0:T(8,128)(2,1)} fusion(bf16[4,64,128]{2,1,0:T(8,128)(2,1)S(1)} %collective-permute-done.7, bf16[2,64,128]{2,1,0:T(8,128)(2,1)S(1)} %collective-permute-done.6, bf16[1,64,128]{2,1,0:T(8,128)(2,1)S(1)} %collective-permute-done.5, bf16[1,64,128]{2,1,0:T(8,128)(2,1)} %bitcast.12), kind=kLoop, calls=%fused_computation | loop fusion | flops 196608 | bytes 262144 | tf_op jit(solution)/shard_map/concatenate | solution.py:388
  31.0 4.3 %shard_map.62 = f32[8,128]{1,0:T(8,128)} custom-call(bf16[8,64,128]{2,1,0:T(8,128)(2,1)} %pad_maximum_fusion.blocks, bf16[128,16384]{1,0:T(8,128)(2,1)} %operator.1, f32[8,128]{1,0:T(8,128)} %get-tuple-element.17.aux), custom_call_target="tpu_custom_call" | custom-call | tf_op jit(solution)/shard_map/pallas_call | solution.py:393
  36.0 0.7 select_bitcast_fusion.1
  36.6 0.6 collective-permute-start.9
  37.3 0.7 collective-permute-start.10
  38.0 0.7 collective-permute-start.11
  38.7 0.7 constant_dynamic-slice_fusion
  39.4 2.0 %collective-permute-start.12 = (bf16[64,1024]{1,0:T(8,128)(2,1)S(1)}, bf16[64,1024]{1,0:T(8,128)(2,1)S(1)}, u32[]{:S(2)}, u32[]{:S(2)}) collective-permute-start(bf16[64,1024]{1,0:T(8,128)(2,1)S(1)} %get-tuple-element.20), channel_id=1, source_target_pairs={{0,1},{1,0},{2,3},{3,2},{4,5},{5,4},{6,7},{7,6},{8,9},{9,8},{10,11... | collective-permute-start | bytes 393224 | tf_op jit(solution)/shard_map/ppermute | solution.py:329
  42.0 2.3 %collective-permute-done.12.theirs = bf16[64,1024]{1,0:T(8,128)(2,1)S(1)} collective-permute-done((bf16[64,1024]{1,0:T(8,128)(2,1)S(1)}, bf16[64,1024]{1,0:T(8,128)(2,1)S(1)}, u32[]{:S(2)}, u32[]{:S(2)}) %collective-permute-start.12) | collective-permute-done | bytes 131104 | tf_op jit(solution)/shard_map/ppermute | solution.py:329
  44.4 0.7 copy-done.2
  45.0 2.0 %shard_map.63 = (f32[8,128]{1,0:T(8,128)}, f32[16,128]{1,0:T(8,128)}) custom-call(f32[8,2,8,128]{3,2,1,0:T(8,128)} %pad_maximum_fusion.2.blocks, bf16[64,1024]{1,0:T(8,128)(2,1)} %get-tuple-element.21.mine, bf16[64,1024]{1,0:T(8,128)(2,1)} %copy-done.2), custom_call_target="tpu_custom_call" | custom-call | tf_op jit(solution)/shard_map/pallas_call | solution.py:399
  47.0 0.7 slice.11
  47.7 1.3 %collective-permute-start.13 = (f32[1,64]{1,0:T(1,128)S(1)}, f32[1,64]{1,0:T(1,128)S(1)}, u32[]{:S(2)}, u32[]{:S(2)}) collective-permute-start(f32[1,64]{1,0:T(1,128)S(1)} %slice.11), channel_id=1, source_target_pairs={{16,0},{17,1},{18,2},{19,3},{20,4},{21,5},{22,6},{23,7},{24,8},{25... | collective-permute-start | bytes 776 | tf_op jit(solution)/shard_map/ppermute | solution.py:406
  49.0 1.8 %shard_map.64 = f32[2,2,192,128]{3,2,1,0:T(8,128)} custom-call(f32[2,2,192,128]{3,2,1,0:T(8,128)} %get-tuple-element.14.pressure, f32[16,128]{1,0:T(8,128)} %get-tuple-element.15.near, f32[16,128]{1,0:T(8,128)} %get-tuple-element.18.fix), custom_call_target="tpu_custom_call" | custom-call | tf_op jit(solution)/shard_map/pallas_call | solution.py:405
  50.8 28.5 %collective-permute-done.13 = f32[1,64]{1,0:T(1,128)S(1)} collective-permute-done((f32[1,64]{1,0:T(1,128)S(1)}, f32[1,64]{1,0:T(1,128)S(1)}, u32[]{:S(2)}, u32[]{:S(2)}) %collective-permute-start.13) | collective-permute-done | bytes 288 | tf_op jit(solution)/shard_map/ppermute | solution.py:406
  79.3 1.2 %fusion = f32[64,1]{0,1:T(1,128)} fusion(f32[1,64]{1,0:T(1,128)S(1)} %collective-permute-done.13, pred[]{:T(512)S(6)} %eq.8, f32[8,128]{1,0:T(8,128)} %get-tuple-element.19), kind=kLoop, calls=%fused_computation.10 | loop fusion | flops 64 | bytes 769 | tf_op jit(solution)/shard_map/reshape | solution.py:408
  (27 shorter events, 3.2 us)
Async XLA Ops:
  0.6 2.4 %collective-permute-start = (f32[2,2,192,128]{3,2,1,0:T(8,128)}, f32[2,2,192,128]{3,2,1,0:T(8,128)S(1)}, u32[]{:S(2)}, u32[]{:S(2)}) collective-permute-start(f32[2,2,192,128]{3,2,1,0:T(8,128)} %f_own.3), channel_id=1, source_target_pairs={{0,16},{16,0},{1,17},{17,1},{2,18},{18,2},{3,19},{19,3},{4,20},{20... | collective-permute-start | bytes 1179656 | tf_op jit(solution)/shard_map/ppermute | solution.py:329
  1.2 1.8 %collective-permute-start.1 = (s32[2,192,128]{2,1,0:T(8,128)}, s32[2,192,128]{2,1,0:T(8,128)S(1)}, u32[]{:S(2)}, u32[]{:S(2)}) collective-permute-start(s32[2,192,128]{2,1,0:T(8,128)} %id_own.3), channel_id=1, source_target_pairs={{0,16},{16,0},{1,17},{17,1},{2,18},{18,2},{3,19},{19,3},{4,20},{20... | collective-permute-start | bytes 589832 | tf_op jit(solution)/shard_map/ppermute | solution.py:329
  3.0 0.7 copy-start.1
  3.7 0.7 copy-start
  6.3 32.4 %slice-start = ((bf16[128,16384]{1,0:T(8,128)(2,1)}), bf16[128,1024]{1,0:T(8,128)(2,1)S(1)}, s32[]{:S(2)}) async-start(bf16[128,16384]{1,0:T(8,128)(2,1)} %operator.1), calls=%async_computation | async-start | bytes 524288 | tf_op jit(solution)/shard_map/slice | solution.py:351
  6.3 4.9 %collective-permute-start.2 = (f32[12,4,128]{2,1,0:T(4,128)}, f32[12,4,128]{2,1,0:T(4,128)S(1)}, u32[]{:S(2)}, u32[]{:S(2)}) collective-permute-start(f32[12,4,128]{2,1,0:T(4,128)} %shard_map.59), channel_id=1, source_target_pairs={{0,1},{1,0},{2,3},{3,2},{4,5},{5,4},{6,7},{7,6},{8,9},{9,8},{10,11... | collective-permute-start | bytes 73736 | tf_op jit(solution)/shard_map/ppermute | solution.py:329
  11.2 0.6 copy-start.5
  14.8 4.3 %collective-permute-start.3 = (f32[12,4,256]{2,1,0:T(4,128)}, f32[12,4,256]{2,1,0:T(4,128)S(1)}, u32[]{:S(2)}, u32[]{:S(2)}) collective-permute-start(f32[12,4,256]{2,1,0:T(4,128)} %get-tuple-element.12), channel_id=1, source_target_pairs={{0,2},{2,0},{4,6},{6,4},{8,10},{10,8},{12,14},{14,12},{1,3},{3,1},... | collective-permute-start | bytes 147464 | tf_op jit(solution)/shard_map/ppermute | solution.py:362
  16.8 2.3 %collective-permute-start.4 = (f32[12,4,256]{2,1,0:T(4,128)}, f32[12,4,256]{2,1,0:T(4,128)S(1)}, u32[]{:S(2)}, u32[]{:S(2)}) collective-permute-start(f32[12,4,256]{2,1,0:T(4,128)} %get-tuple-element.13), channel_id=1, source_target_pairs={{2,4},{4,2},{6,8},{8,6},{10,12},{12,10},{3,5},{5,3},{7,9},{9,7},{1... | collective-permute-start | bytes 147464 | tf_op jit(solution)/shard_map/ppermute | solution.py:362
  19.1 0.6 copy-start.3
  19.1 0.6 copy-start.4
  26.1 0.7 collective-permute-start.5
  27.5 0.7 collective-permute-start.6
  28.9 0.7 collective-permute-start.7
  35.3 0.7 collective-permute-start.8
  36.6 0.7 collective-permute-start.9
  37.3 0.7 collective-permute-start.10
  38.0 3.4 %collective-permute-start.11 = (f32[4,2,8,128]{3,2,1,0:T(8,128)S(1)}, f32[4,2,8,128]{3,2,1,0:T(8,128)S(1)}, u32[]{:S(2)}, u32[]{:S(2)}) collective-permute-start(f32[4,2,8,128]{3,2,1,0:T(8,128)S(1)} %pad_maximum_fusion.4), channel_id=1, source_target_pairs={{16,24},{17,25},{18,26},{19,27},{20,28},{21,29},{22,30},{23,31},{2... | collective-permute-start | bytes 98312 | tf_op jit(solution)/shard_map/ppermute | solution.py:335
  39.4 5.0 %collective-permute-start.12 = (bf16[64,1024]{1,0:T(8,128)(2,1)S(1)}, bf16[64,1024]{1,0:T(8,128)(2,1)S(1)}, u32[]{:S(2)}, u32[]{:S(2)}) collective-permute-start(bf16[64,1024]{1,0:T(8,128)(2,1)S(1)} %get-tuple-element.20), channel_id=1, source_target_pairs={{0,1},{1,0},{2,3},{3,2},{4,5},{5,4},{6,7},{7,6},{8,9},{9,8},{10,11... | collective-permute-start | bytes 393224 | tf_op jit(solution)/shard_map/ppermute | solution.py:329
  44.4 0.7 copy-start.2
  47.7 31.6 %collective-permute-start.13 = (f32[1,64]{1,0:T(1,128)S(1)}, f32[1,64]{1,0:T(1,128)S(1)}, u32[]{:S(2)}, u32[]{:S(2)}) collective-permute-start(f32[1,64]{1,0:T(1,128)S(1)} %slice.11), channel_id=1, source_target_pairs={{16,0},{17,1},{18,2},{19,3},{20,4},{21,5},{22,6},{23,7},{24,8},{25... | collective-permute-start | bytes 776 | tf_op jit(solution)/shard_map/ppermute | solution.py:406

commit v2 on v1

--- a/solution.py
+++ b/solution.py
@@ -84,6 +84,7 @@
 
 def sweep_kernel(turned, even, odd, pressure, trace, aux, near, ext, hh, qq, uu, cu, mv):
     v, w = lax.axis_index("vol"), lax.axis_index("wide")
+    inner = (w > 0) & (w < lax.axis_size("wide") - 1)
     excite = pressure.shape[0]
     cells_y, cells_x = pressure.shape[2], pressure.shape[3]
     rows, width = ext.shape[1], ext.shape[2]
@@ -93,8 +94,9 @@
         ext[slab, 0:TILE] = jnp.zeros((TILE, width), jnp.float32)
         ext[slab, right : right + TILE] = jnp.zeros((TILE, width), jnp.float32)
         ext[slab, TILE:right] = turned[slab]
-        ext[slab, TILE - HALO : TILE] = jnp.where(left, odd[slab], even[slab])
-        ext[slab, right : right + HALO] = jnp.where(left, even[slab], odd[slab])
+        outer = jnp.where(inner, odd[slab], 0.0)
+        ext[slab, TILE - HALO : TILE] = jnp.where(left, outer, even[slab])
+        ext[slab, right : right + HALO] = jnp.where(left, even[slab], outer)
 
     def box(ref, first, m):
         total = ref[first + m]
@@ -139,11 +141,11 @@
             )
 
     columns = 2 * excite
-    r = lax.broadcasted_iota(jnp.int32, trace.shape[:1] + (width,), 0)
-    lane = lax.broadcasted_iota(jnp.int32, trace.shape[:1] + (width,), 1)
+    r = lax.broadcasted_iota(jnp.int32, (trace.shape[1], width), 0)
+    lane = lax.broadcasted_iota(jnp.int32, (trace.shape[1], width), 1)
     s = lax.div(r, columns)
     hit = lane == s * (cells_y // BY)
-    picked = jnp.zeros(trace.shape, jnp.float32)
+    picked = jnp.zeros(trace.shape[1:], jnp.float32)
     for col in range(columns):
         e, late = col % excite, col >= excite
         match = hit & (lax.rem(r, columns) == col)
@@ -151,7 +153,8 @@
             match = match & (s > 0)
         values = uu[3 if late else 1, e * 4, TILE:right].astype(jnp.bfloat16)
         picked = picked + nt(jnp.where(match, 1.0, 0.0).astype(jnp.bfloat16), values)
-    trace[...] = picked.astype(jnp.bfloat16)
+    for j in range(trace.shape[0]):
+        trace[j] = picked.astype(jnp.bfloat16)
 
     aux[...] = jnp.zeros(aux.shape, jnp.float32)
     near[...] = jnp.zeros(near.shape, jnp.float32)
@@ -172,18 +175,14 @@
 
 
 def product_kernel(blocks, operator, aux, out):
-    w = lax.axis_index("wide")
     count = blocks.shape[0]
     tile_rows = operator.shape[0]
-    odd = lax.rem(w, 2)
 
     def pair(p, sums):
-        base = lax.div(w ^ (2 * p), 2) * 2
-        low, high = blocks[2 * p + odd], blocks[2 * p + 1 - odd]
-        both = jnp.concatenate([low, high], axis=1)
+        both = jnp.concatenate([blocks[2 * p], blocks[2 * p + 1]], axis=1)
         sums = list(sums)
         for s in range(BY):
-            start = pl.multiple_of(s * count * LANES + base * LANES, LANES)
+            start = pl.multiple_of(s * count * LANES + p * (2 * LANES), 2 * LANES)
             group = s // 4 * 16
             sums[s % 4] = sums[s % 4] + nt(both[group : group + 16], operator[:, pl.ds(start, 2 * LANES)])
         return tuple(sums)
@@ -197,17 +196,16 @@
     total = total[0:8] + total[8:16]
     total = total + pltpu.roll(total, 4, 0)
     r = lax.broadcasted_iota(jnp.int32, total.shape, 0)
-    out[...] = jnp.where(r < 4, total, pltpu.roll(aux[...], 4, 0))
-
-
-def couple_kernel(blocks, mine, theirs, traction, fix, flat, save):
-    v, w, n = lax.axis_index("vol"), lax.axis_index("wide"), lax.axis_index("narrow")
-    count = blocks.shape[0]
+    total = jnp.where(r < 4, total, pltpu.roll(aux[...], 4, 0))
+    for j in range(out.shape[0]):
+        out[j] = total
+
+
+def couple_kernel(flat, mine, theirs, traction, fix, save):
+    w, n = lax.axis_index("wide"), lax.axis_index("narrow")
+    count = flat.shape[0] // 16
     excite = 2
     targets = mine.shape[0]
-    for j in range(count):
-        flat[pl.ds(j * 16, 8), :] = blocks[w ^ j, 0]
-        flat[pl.ds(j * 16 + 8, 8), :] = blocks[w ^ j, 1]
 
     def field(k, r):
         return flat[pl.ds(k * 8 + r, count, stride=16), :]
@@ -259,7 +257,7 @@
             for j in range(8):
                 part = nt(left, ref[:, (8 * g + j) * LANES : (8 * g + j + 1) * LANES])
                 total = total + jnp.where((r & 7) == j, part, 0.0)
-    first = blocks[0, 0] + blocks[0, 1]
+    first = flat[pl.ds(pl.multiple_of(w * 16, 16), 8), :] + flat[pl.ds(pl.multiple_of(w * 16 + 8, 8), 8), :]
     first = jnp.where(n == 0, first, pltpu.roll(first, LANES - targets, 1))
     traction[...] = jnp.zeros(traction.shape, jnp.float32)
     for e in range(excite):
@@ -268,17 +266,14 @@
             + first[2 + e : 3 + e, 0:targets]
         )
 
-    top = v == lax.axis_size("vol") - 1
     fix[...] = jnp.zeros(fix.shape, jnp.float32)
     for e in range(excite):
         for i in range(3):
             row = 2 * i + e
-            fix[row : row + 1] = jnp.where(top, save[n, i, e, pl.ds(w, 1), :], 0.0)
+            fix[row : row + 1] = save[n, i, e, pl.ds(w, 1), :]
         for i in range(1, 3):
             row = 4 + 2 * i + e
-            fix[row : row + 1] = jnp.where(
-                top & (n == 0), save[1, i, e, pl.ds(w, 1), :], 0.0
-            )
+            fix[row : row + 1] = jnp.where(n == 0, save[1, i, e, pl.ds(w, 1), :], 0.0)
 
 
 def mend_kernel(pressure, near, fix, out):
@@ -316,13 +311,14 @@
     everyone = ("vol", "wide", "narrow")
     vmem, smem = pl.BlockSpec(memory_space=pltpu.VMEM), pl.BlockSpec(memory_space=pltpu.SMEM)
 
-    def call(kernel, shapes, specs, scratch=()):
+    def call(kernel, shapes, specs, scratch=(), limit=4):
         return pl.pallas_call(
             kernel,
             out_shape=[jax.ShapeDtypeStruct(*s) for s in shapes],
             in_specs=specs,
             out_specs=[vmem] * len(shapes),
             scratch_shapes=list(scratch),
+            compiler_params=pltpu.CompilerParams(vmem_limit_bytes=limit * 2**20),
         )
 
     def swap(x, axis):
@@ -330,17 +326,6 @@
 
     def number(a, b, c):
         return (a * wides + b) * narrows + c
-
-    def top_permute(x, partner):
-        return lax.ppermute(
-            x,
-            everyone,
-            [
-                (number(vols - 1, b, c), number(vols - 1, *partner(b, c)))
-                for b in range(wides)
-                for c in range(narrows)
-            ],
-        )
 
     f_other, id_other = swap(forcing, "vol"), swap(material_ids, "vol")
     cells = (forcing, f_other, material_ids, id_other)
@@ -356,17 +341,24 @@
         [((slabs, cells_x, width), f32)] + [((slabs, HALO, width), f32)] * 2,
         [smem] + [vmem] * 5,
         [pltpu.VMEM((slabs, width, cells_x), f32)],
+        8,
     )(materials, *cells, edge)
-    even_pairs = [(i, i ^ 1) for i in range(wides)]
-    odd_pairs = [(i, i + 1 if i % 2 else i - 1) for i in range(1, wides - 1)]
-    even, odd = lax.ppermute(even, "wide", even_pairs), lax.ppermute(odd, "wide", odd_pairs)
+    even = lax.ppermute(even, "wide", [(i, i ^ 1) for i in range(wides)])
+    odd_pairs = []
+    for a in range(vols):
+        for b in range(wides):
+            for c in range(narrows):
+                far = b + 1 if b % 2 else b - 1
+                there = (far, c) if 0 <= far < wides else (b, 1 - c)
+                odd_pairs.append((number(a, b, c), number(a, *there)))
+    odd = lax.ppermute(odd, everyone, odd_pairs)
     rows = cells_x + 2 * TILE
     full = (rows, width)
     pressure, trace, aux, near = call(
         sweep_kernel,
         [
             (forcing.shape, f32),
-            ((BY * 2 * excite, cells_x), bf16),
+            ((wides, BY * 2 * excite, cells_x), bf16),
             ((8, cells_x), f32),
             ((16, cells_x), f32),
         ],
@@ -379,32 +371,32 @@
             pltpu.VMEM((3, 4 * excite) + full, f32),
             pltpu.VMEM((4 * excite,) + full, f32),
         ],
+        24,
     )(turned, even, odd)
 
-    def gather(block):
-        step = 1
-        while step < wides:
-            other = top_permute(block, lambda b, c: (b ^ step, c))
-            block = jnp.concatenate([block, other], axis=0)
-            step *= 2
-        return block
-
-    blocks = gather(trace[None])
-    (sums,) = call(product_kernel, [((8, tile_rows), f32)], [vmem] * 3)(
-        blocks, boundary_operator, aux
+    def couple(trace, aux, boundary_operator, mine, theirs):
+        blocks = lax.all_to_all(trace, "wide", 0, 0)
+        (sums,) = call(product_kernel, [((wides * narrows, 8, tile_rows), f32)], [vmem] * 3, (), 24)(
+            blocks, boundary_operator, aux
+        )
+        blocks = lax.all_to_all(sums, ("wide", "narrow"), 0, 0)
+        return tuple(call(
+            couple_kernel,
+            [((8, LANES), f32), ((16, cells_x), f32)],
+            [vmem] * 3,
+            [pltpu.VMEM((2, 3, excite, wides, LANES), f32)],
+        )(blocks.reshape(wides * narrows * 8, LANES), mine, theirs))
+
+    def nothing(*_):
+        return jnp.zeros((8, LANES), f32), jnp.zeros((16, cells_x), f32)
+
+    traction, fix = lax.cond(
+        v == vols - 1, couple, nothing, trace, aux, boundary_operator, mine, theirs
     )
-    other = top_permute(sums, lambda b, c: (b, 1 - c))
-    pair = jnp.stack([jnp.where(n == 0, sums, other), jnp.where(n == 0, other, sums)])
-    blocks = gather(pair[None])
-    traction, fix = call(
-        couple_kernel,
-        [((8, LANES), f32), ((16, cells_x), f32)],
-        [vmem] * 3,
-        [pltpu.VMEM((wides * 16, LANES), f32), pltpu.VMEM((2, 3, excite, wides, LANES), f32)],
-    )(blocks, mine, theirs)
     (pressure,) = call(mend_kernel, [(forcing.shape, f32)], [vmem] * 3)(pressure, near, fix)
-    lower = lax.ppermute(traction[0:1, :targets], "vol", [(1, 0)])
-    column = jnp.where(v == vols - 1, traction[1:2, :targets], lower)
+    column = traction[0:2, :targets]
+    lower = swap(column, "vol")
+    column = jnp.where(v == vols - 1, column[1:2], lower[0:1])
     return pressure, column.reshape(targets, 1)
 
 

time: 81.9 us -> 51.1 us (0.62); the launches traced: 80.5 us -> 50.7 us
  waiting for transfers between devices: 36.3 us -> 6.69 us
  starting transfers between devices: 14 us -> 30 us
  Pallas kernels: 19.3 us -> 6.66 us
  other arithmetic: 5.34 us -> 0.51 us
  local copies, waits for them, and re-layouts: 4.67 us -> 6.15 us
    ppermute x10 -> x2, waiting for transfers between devices: 30.2 us -> 3.45 us  [the longest x1 1.96 us: local(): even = lax.ppermute(even, 'wide', [(i, i ^ 1) for i in range(wides)])]
    ppermute x4 -> x5, starting transfers between devices: 5.54 us -> 27.8 us  [swap(): return lax.ppermute(x, axis, [(0, 1), (1, 0)])]
    pallas_call x3 -> x1, Pallas kernels: 12.7 us -> 4.27 us  [local(): call(sweep_kernel, [(forcing.shape, f32), ((wides, BY * 2 * excite, cells...]
    ppermute x10 -> x2, starting transfers between devices: 8.51 us -> 2.19 us  [the longest x1 1.56 us: local(): even = lax.ppermute(even, 'wide', [(i, i ^ 1) for i in range(wides)])]
    concatenate x6 -> x0, other arithmetic: 3.48 us -> none  [gather(): block = jnp.concatenate([block, other], axis=0)]
    ppermute x4 -> x5, waiting for transfers between devices: 6.09 us -> 3.24 us  [swap(): return lax.ppermute(x, axis, [(0, 1), (1, 0)])]
    pallas_call x1, Pallas kernels: 2.98 us -> 1.04 us  [local(): call(turn_kernel, [((slabs, cells_x, width), f32)] + [((slabs, HALO, widt...]
    unnamed x12, local copies, waits for them, and re-layouts: 3.31 us -> 5.15 us
  transfers between devices with their start and end apart: 14 -> 7, of which waited for: 5 -> 3; matrix products, arithmetic and copies ran while one was open for 2% -> 2% of each run, Pallas kernels for 2% -> 13%
where the time goes in v2:
time: 51.1 us; the launch traced here: 50.7 us
  starting transfers between devices  30 us (59%)
  waiting for transfers between devices  6.69 us (13%)
  Pallas kernels  6.66 us (13%)
  local copies, waits for them, and re-layouts  6.15 us (12%)
  between operations  0.7 us (1%)
    ppermute x5, starting transfers between devices, swap(): return lax.ppermute(x, axis, [(0, 1), (1, 0)])  27.8 us
    unnamed x12, local copies, waits for them, and re-layouts  5.15 us
    pallas_call x1, Pallas kernels, local(): call(sweep_kernel, [(forcing.shape, f32), ((wides, BY * 2 * excite, cells...  4.27 us
    ppermute x5, waiting for transfers between devices, swap(): return lax.ppermute(x, axis, [(0, 1), (1, 0)])  3.24 us
    ppermute x1, waiting for transfers between devices, local(): even = lax.ppermute(even, 'wide', [(i, i ^ 1) for i in range(wides)])  1.96 us
    ppermute x1, starting transfers between devices, local(): even = lax.ppermute(even, 'wide', [(i, i ^ 1) for i in range(wides)])  1.56 us
    ppermute x1, waiting for transfers between devices, local(): odd = lax.ppermute(odd, everyone, odd_pairs)  1.49 us
    pallas_call x1, Pallas kernels, local(): call(turn_kernel, [((slabs, cells_x, width), f32)] + [((slabs, HALO, widt...  1.04 us
  transfers between devices with their start and end apart: 7, of which 3 were waited for; matrix products, arithmetic and copies ran while one was open for 2% of the time, Pallas kernels for 13%

profile of v2, /device:TPU:0, one launch (start us, length us, event | category | flops | bytes accessed | tf_op | source)
XLA Modules:
  0.0 50.7 jit_solution(16965101064359124558)
XLA Ops:
  0.6 0.6 %collective-permute-start = (f32[2,2,192,128]{3,2,1,0:T(8,128)}, f32[2,2,192,128]{3,2,1,0:T(8,128)S(1)}, u32[]{:S(2)}, u32[]{:S(2)}) collective-permute-start(f32[2,2,192,128]{3,2,1,0:T(8,128)} %f_own.3), channel_id=1, source_target_pairs={{0,16},{16,0},{1,17},{17,1},{2,18},{18,2},{3,19},{19,3},{4,20},{20... | collective-permute-start | bytes 1179656 | tf_op jit(solution)/shard_map/ppermute | solution.py:325
  1.2 0.1 collective-permute-start.1
  1.3 1.0 %slice.13 = bf16[128,1024]{1,0:T(8,128)(2,1)S(1)} slice(bf16[128,16384]{1,0:T(8,128)(2,1)} %param.9), slice={[0:128], [0:1024]} | slice | bytes 524288 | tf_op jit(solution)/shard_map/slice | solution.py:336
  2.3 3.0 %collective-permute-start.5 = (bf16[64,1024]{1,0:T(8,128)(2,1)S(1)}, bf16[64,1024]{1,0:T(8,128)(2,1)S(1)}, u32[]{:S(2)}, u32[]{:S(2)}) collective-permute-start(bf16[64,1024]{1,0:T(8,128)(2,1)S(1)} %constant_dynamic-slice_fusion.1), channel_id=1, source_target_pairs={{0,1},{1,0},{2,3},{3,2},{4,5},{5,4},{6,7},{7,6},{8,9},{9,8},{10,11... | collective-permute-start | bytes 393224 | tf_op jit(solution)/shard_map/ppermute | solution.py:325
  5.3 0.0 collective-permute-done.1.id_oth
  5.3 0.0 collective-permute-done.f_oth
  5.3 0.0 copy-start
  5.3 1.0 %copy-done = f32[2,2,192,128]{3,2,1,0:T(8,128)S(1)} copy-done((f32[2,2,192,128]{3,2,1,0:T(8,128)S(1)}, f32[2,2,192,128]{3,2,1,0:T(8,128)}, u32[]{:S(2)}) %copy-start) | copy-done | bytes 393240
  6.3 0.0 copy-start.2
  6.3 0.9 %copy-done.2 = s32[2,192,128]{2,1,0:T(8,128)S(1)} copy-done((s32[2,192,128]{2,1,0:T(8,128)S(1)}, s32[2,192,128]{2,1,0:T(8,128)}, u32[]{:S(2)}) %copy-start.2) | copy-done | bytes 196632
  7.2 0.0 copy-start.4
  7.2 0.7 %copy-done.4 = f32[8]{0:T(128)S(1)} copy-done((f32[8]{0:T(128)S(1)}, f32[8]{0:T(128)}, u32[]{:S(2)}) %copy-start.4) | copy-done | bytes 56
  7.9 0.6 %shard_map.59 = f32[12,4,128]{2,1,0:T(4,128)S(1)} custom-call(f32[8]{0:T(128)S(1)} %copy-done.4, f32[2,2,192,128]{3,2,1,0:T(8,128)S(1)} %copy-done, f32[2,2,192,128]{3,2,1,0:T(8,128)S(1)} %collective-permute-done.f_oth, s32[2,192,128]{2,1,0:T(8,128)S(1)} %copy-done.2, s32[2,192,128]{2,1,0:T(8,128)S(1)} %collective-permute-done.1.id_oth), custom_call_target="tpu_custom_call" | custom-call | tf_op jit(solution)/shard_map/pallas_call | solution.py:332
  8.4 0.7 %collective-permute-start.2 = (f32[12,4,128]{2,1,0:T(4,128)S(1)}, f32[12,4,128]{2,1,0:T(4,128)S(1)}, u32[]{:S(2)}, u32[]{:S(2)}) collective-permute-start(f32[12,4,128]{2,1,0:T(4,128)S(1)} %shard_map.59), channel_id=1, source_target_pairs={{0,1},{1,0},{2,3},{3,2},{4,5},{5,4},{6,7},{7,6},{8,9},{9,8},{10,11... | collective-permute-start | bytes 73736 | tf_op jit(solution)/shard_map/ppermute | solution.py:325
  9.1 3.2 %collective-permute-done.2.got = f32[12,4,128]{2,1,0:T(4,128)S(1)} collective-permute-done((f32[12,4,128]{2,1,0:T(4,128)S(1)}, f32[12,4,128]{2,1,0:T(4,128)S(1)}, u32[]{:S(2)}, u32[]{:S(2)}) %collective-permute-start.2) | collective-permute-done | bytes 24608 | tf_op jit(solution)/shard_map/ppermute | solution.py:325
  12.3 0.0 copy-start.1
  12.3 1.0 %copy-done.1 = f32[2,2,192,128]{3,2,1,0:T(8,128)S(1)} copy-done((f32[2,2,192,128]{3,2,1,0:T(8,128)S(1)}, f32[2,2,192,128]{3,2,1,0:T(8,128)}, u32[]{:S(2)}) %copy-start.1) | copy-done | bytes 393240
  13.3 0.0 copy-start.3
  13.3 0.9 %copy-done.3 = s32[2,192,128]{2,1,0:T(8,128)S(1)} copy-done((s32[2,192,128]{2,1,0:T(8,128)S(1)}, s32[2,192,128]{2,1,0:T(8,128)}, u32[]{:S(2)}) %copy-start.3) | copy-done | bytes 196632
  14.2 0.0 copy-start.5
  14.2 0.7 %copy-done.5 = f32[8]{0:T(128)S(1)} copy-done((f32[8]{0:T(128)S(1)}, f32[8]{0:T(128)}, u32[]{:S(2)}) %copy-start.5) | copy-done | bytes 56
  14.9 1.0 %shard_map.60 = (f32[12,128,256]{2,1,0:T(8,128)S(1)}, f32[12,4,256]{2,1,0:T(4,128)S(1)}, f32[12,4,256]{2,1,0:T(4,128)S(1)}) custom-call(f32[8]{0:T(128)S(1)} %copy-done.5, f32[2,2,192,128]{3,2,1,0:T(8,128)S(1)} %copy-done.1, f32[2,2,192,128]{3,2,1,0:T(8,128)S(1)} %collective-permute-done.f_oth, s32[2,192,128]{2,1,0:T(8,128)S(1)} %copy-done.3, ...), custom_call_target="tpu_custom_call" | custom-call | tf_op jit(solution)/shard_map/pallas_call | solution.py:339
  15.9 1.6 %collective-permute-start.3 = (f32[12,4,256]{2,1,0:T(4,128)S(1)}, f32[12,4,256]{2,1,0:T(4,128)S(1)}, u32[]{:S(2)}, u32[]{:S(2)}) collective-permute-start(f32[12,4,256]{2,1,0:T(4,128)S(1)} %get-tuple-element.41), channel_id=1, source_target_pairs={{0,2},{2,0},{4,6},{6,4},{8,10},{10,8},{12,14},{14,12},{1,3},{3,1},... | collective-permute-start | bytes 147464 | tf_op jit(solution)/shard_map/ppermute | solution.py:346
  17.5 0.6 %collective-permute-start.4 = (f32[12,4,256]{2,1,0:T(4,128)S(1)}, f32[12,4,256]{2,1,0:T(4,128)S(1)}, u32[]{:S(2)}, u32[]{:S(2)}) collective-permute-start(f32[12,4,256]{2,1,0:T(4,128)S(1)} %get-tuple-element.42), channel_id=1, source_target_pairs={{0,1},{1,0},{2,4},{3,5},{4,2},{5,3},{6,8},{7,9},{8,6},{9,7},{10,12... | collective-permute-start | bytes 147464 | tf_op jit(solution)/shard_map/ppermute | solution.py:354
  18.1 2.0 %collective-permute-done.3.even = f32[12,4,256]{2,1,0:T(4,128)S(1)} collective-permute-done((f32[12,4,256]{2,1,0:T(4,128)S(1)}, f32[12,4,256]{2,1,0:T(4,128)S(1)}, u32[]{:S(2)}, u32[]{:S(2)}) %collective-permute-start.3) | collective-permute-done | bytes 49184 | tf_op jit(solution)/shard_map/ppermute | solution.py:346
  20.1 1.5 %collective-permute-done.4.odd = f32[12,4,256]{2,1,0:T(4,128)S(1)} collective-permute-done((f32[12,4,256]{2,1,0:T(4,128)S(1)}, f32[12,4,256]{2,1,0:T(4,128)S(1)}, u32[]{:S(2)}, u32[]{:S(2)}) %collective-permute-start.4) | collective-permute-done | bytes 49184 | tf_op jit(solution)/shard_map/ppermute | solution.py:354
  21.6 4.3 %shard_map.61 = (f32[2,2,192,128]{3,2,1,0:T(8,128)S(1)}, bf16[8,64,128]{2,1,0:T(8,128)(2,1)S(1)}, f32[8,128]{1,0:T(8,128)S(1)}, f32[16,128]{1,0:T(8,128)S(1)}) custom-call(f32[12,128,256]{2,1,0:T(8,128)S(1)} %get-tuple-element.40.turned, f32[12,4,256]{2,1,0:T(4,128)S(1)} %collective-permute-done.3.even, f32[12,4,256]{2,1,0:T(4,128)S(1)} %collective-permute-done.4.odd), custom_call_target="tpu_custom_call" | custom-call | tf_op jit(solution)/shard_map/pallas_call | solution.py:357
  25.9 0.0 collective-permute-done.5
  25.9 23.4 %collective-permute-start.6 = (f32[2,64]{1,0:T(2,128)S(1)}, f32[2,64]{1,0:T(2,128)S(1)}, u32[]{:S(2)}, u32[]{:S(2)}) collective-permute-start(f32[2,64]{1,0:T(2,128)S(1)} %slice.15), channel_id=1, source_target_pairs={{0,16},{16,0},{1,17},{17,1},{2,18},{18,2},{3,19},{19,3},{4,20},{20... | collective-permute-start | bytes 1544 | tf_op jit(solution)/shard_map/ppermute | solution.py:325
  49.4 0.8 %shard_map.62 = f32[2,2,192,128]{3,2,1,0:T(8,128)} custom-call(f32[2,2,192,128]{3,2,1,0:T(8,128)S(1)} %get-tuple-element.43.pressure, f32[16,128]{1,0:T(8,128)S(1)} %get-tuple-element.44.near, f32[16,128]{1,0:T(8,128)S(1)} %get-tuple-element.47.fix), custom_call_target="tpu_custom_call" | custom-call | tf_op jit(solution)/shard_map/pallas_call | solution.py:396
  50.1 0.0 collective-permute-done.6
  50.2 0.5 %fusion = f32[64,1]{0,1:T(1,128)} fusion(pred[]{:T(512)S(6)} %eq.4, f32[2,64]{1,0:T(2,128)S(1)} %collective-permute-done.6, f32[8,128]{1,0:T(8,128)S(1)} %get-tuple-element.48), kind=kLoop, calls=%fused_computation.2 | loop fusion | flops 64 | bytes 769 | tf_op jit(solution)/shard_map/reshape | solution.py:400
  (5 shorter events, 0.1 us)
Async XLA Ops:
  0.6 4.6 %collective-permute-start = (f32[2,2,192,128]{3,2,1,0:T(8,128)}, f32[2,2,192,128]{3,2,1,0:T(8,128)S(1)}, u32[]{:S(2)}, u32[]{:S(2)}) collective-permute-start(f32[2,2,192,128]{3,2,1,0:T(8,128)} %f_own.3), channel_id=1, source_target_pairs={{0,16},{16,0},{1,17},{17,1},{2,18},{18,2},{3,19},{19,3},{4,20},{20... | collective-permute-start | bytes 1179656 | tf_op jit(solution)/shard_map/ppermute | solution.py:325
  1.2 4.1 %collective-permute-start.1 = (s32[2,192,128]{2,1,0:T(8,128)}, s32[2,192,128]{2,1,0:T(8,128)S(1)}, u32[]{:S(2)}, u32[]{:S(2)}) collective-permute-start(s32[2,192,128]{2,1,0:T(8,128)} %id_own.3), channel_id=1, source_target_pairs={{0,16},{16,0},{1,17},{17,1},{2,18},{18,2},{3,19},{19,3},{4,20},{20... | collective-permute-start | bytes 589832 | tf_op jit(solution)/shard_map/ppermute | solution.py:325
  2.3 23.6 %collective-permute-start.5 = (bf16[64,1024]{1,0:T(8,128)(2,1)S(1)}, bf16[64,1024]{1,0:T(8,128)(2,1)S(1)}, u32[]{:S(2)}, u32[]{:S(2)}) collective-permute-start(bf16[64,1024]{1,0:T(8,128)(2,1)S(1)} %constant_dynamic-slice_fusion.1), channel_id=1, source_target_pairs={{0,1},{1,0},{2,3},{3,2},{4,5},{5,4},{6,7},{7,6},{8,9},{9,8},{10,11... | collective-permute-start | bytes 393224 | tf_op jit(solution)/shard_map/ppermute | solution.py:325
  5.3 1.0 %copy-start = (f32[2,2,192,128]{3,2,1,0:T(8,128)S(1)}, f32[2,2,192,128]{3,2,1,0:T(8,128)}, u32[]{:S(2)}) copy-start(f32[2,2,192,128]{3,2,1,0:T(8,128)} %f_own.3) | copy-start | bytes 1179652
  6.3 0.9 %copy-start.2 = (s32[2,192,128]{2,1,0:T(8,128)S(1)}, s32[2,192,128]{2,1,0:T(8,128)}, u32[]{:S(2)}) copy-start(s32[2,192,128]{2,1,0:T(8,128)} %id_own.3) | copy-start | bytes 589828
  7.2 0.7 %copy-start.4 = (f32[8]{0:T(128)S(1)}, f32[8]{0:T(128)}, u32[]{:S(2)}) copy-start(f32[8]{0:T(128)} %table.3) | copy-start | bytes 100
  8.4 3.9 %collective-permute-start.2 = (f32[12,4,128]{2,1,0:T(4,128)S(1)}, f32[12,4,128]{2,1,0:T(4,128)S(1)}, u32[]{:S(2)}, u32[]{:S(2)}) collective-permute-start(f32[12,4,128]{2,1,0:T(4,128)S(1)} %shard_map.59), channel_id=1, source_target_pairs={{0,1},{1,0},{2,3},{3,2},{4,5},{5,4},{6,7},{7,6},{8,9},{9,8},{10,11... | collective-permute-start | bytes 73736 | tf_op jit(solution)/shard_map/ppermute | solution.py:325
  12.3 1.0 %copy-start.1 = (f32[2,2,192,128]{3,2,1,0:T(8,128)S(1)}, f32[2,2,192,128]{3,2,1,0:T(8,128)}, u32[]{:S(2)}) copy-start(f32[2,2,192,128]{3,2,1,0:T(8,128)} %f_own.3) | copy-start | bytes 1179652
  13.3 0.9 %copy-start.3 = (s32[2,192,128]{2,1,0:T(8,128)S(1)}, s32[2,192,128]{2,1,0:T(8,128)}, u32[]{:S(2)}) copy-start(s32[2,192,128]{2,1,0:T(8,128)} %id_own.3) | copy-start | bytes 589828
  14.2 0.7 %copy-start.5 = (f32[8]{0:T(128)S(1)}, f32[8]{0:T(128)}, u32[]{:S(2)}) copy-start(f32[8]{0:T(128)} %table.3) | copy-start | bytes 100
  15.9 4.2 %collective-permute-start.3 = (f32[12,4,256]{2,1,0:T(4,128)S(1)}, f32[12,4,256]{2,1,0:T(4,128)S(1)}, u32[]{:S(2)}, u32[]{:S(2)}) collective-permute-start(f32[12,4,256]{2,1,0:T(4,128)S(1)} %get-tuple-element.41), channel_id=1, source_target_pairs={{0,2},{2,0},{4,6},{6,4},{8,10},{10,8},{12,14},{14,12},{1,3},{3,1},... | collective-permute-start | bytes 147464 | tf_op jit(solution)/shard_map/ppermute | solution.py:346
  17.5 4.1 %collective-permute-start.4 = (f32[12,4,256]{2,1,0:T(4,128)S(1)}, f32[12,4,256]{2,1,0:T(4,128)S(1)}, u32[]{:S(2)}, u32[]{:S(2)}) collective-permute-start(f32[12,4,256]{2,1,0:T(4,128)S(1)} %get-tuple-element.42), channel_id=1, source_target_pairs={{0,1},{1,0},{2,4},{3,5},{4,2},{5,3},{6,8},{7,9},{8,6},{9,7},{10,12... | collective-permute-start | bytes 147464 | tf_op jit(solution)/shard_map/ppermute | solution.py:354
  25.9 24.3 %collective-permute-start.6 = (f32[2,64]{1,0:T(2,128)S(1)}, f32[2,64]{1,0:T(2,128)S(1)}, u32[]{:S(2)}, u32[]{:S(2)}) collective-permute-start(f32[2,64]{1,0:T(2,128)S(1)} %slice.15), channel_id=1, source_target_pairs={{0,16},{16,0},{1,17},{17,1},{2,18},{18,2},{3,19},{19,3},{4,20},{20... | collective-permute-start | bytes 1544 | tf_op jit(solution)/shard_map/ppermute | solution.py:325

commit v3 on v2

v3 whole, which is shorter than its diff:
```python
import functools

import jax
import jax.numpy as jnp
from jax import lax
from jax.experimental import pallas as pl
from jax.experimental.pallas import tpu as pltpu
from jax.sharding import PartitionSpec as P

BY = 16
HALO = 4
TILE = 8
LANES = 128

lower_edge = 0.25
upper_edge = 1.75
mass_ratio = 26.0
couple_gain = 40.0


def sweep_weights():
    middle = (upper_edge + lower_edge) / 2.0
    spread = (upper_edge - lower_edge) / 2.0
    center_ratio = middle / spread
    ratio_last = 1.0 / center_ratio
    ratio_next = 1.0 / (2.0 * center_ratio - ratio_last)
    return 1.0 / middle, ratio_next * ratio_last, 2.0 * ratio_next / spread


GAIN0, KEEP1, GAIN1 = sweep_weights()


def lookup(ids, table):
    found = jnp.zeros(ids.shape, jnp.float32)
    for number in range(table.shape[0]):
        found = jnp.where(ids == number, table[number], found)
    return found


def nt(a, b):
    return lax.dot_general(a, b, (((1,), (1,)), ((), ())), preferred_element_type=jnp.float32)


def inner_first(k, v):
    return v if k % 2 == 0 else 1 - v


def turn(block, out, slab):
    cells_y, cells_x = block.shape
    behind = jnp.zeros((out.shape[2] - cells_y, cells_x), jnp.float32)
    out[slab] = jnp.concatenate([block, behind], axis=0).T


def edge_rows(n, ref, *at):
    cells_y = ref.shape[-2]
    return jnp.where(
        n == 0, ref[*at, cells_y - HALO : cells_y, :], ref[*at, 0:HALO, :]
    )


def own_kernel(
    table, forcing, ids, operator, turned, edge, spread, sent, kept, f_in, id_in, table_in, sems
):
    v, n = lax.axis_index("vol"), lax.axis_index("narrow")
    targets, columns = sent.shape
    copies = [
        pltpu.make_async_copy(table, table_in, sems.at[0]),
        pltpu.make_async_copy(ids, id_in, sems.at[1]),
        pltpu.make_async_copy(forcing, f_in, sems.at[2]),
    ]
    for row, out in ((1 - n, sent), (n, kept)):
        rows = pl.ds(pl.multiple_of(row * targets, targets), targets)
        source = operator.at[rows, 0:columns]
        copies.append(pltpu.make_async_copy(source, out, sems.at[len(copies)]))
    for copy in copies:
        copy.start()
    excite = forcing.shape[0]
    copies[0].wait()
    for k in range(spread.shape[0]):
        spread[k : k + 1] = jnp.full((1, spread.shape[1]), table_in[k], jnp.float32)
    copies[1].wait()
    for m in range(2):
        li = inner_first(m, v)
        edge[2 * excite + m] = lookup(edge_rows(n, id_in, li), table_in)
        turn(lookup(id_in[li], table_in), turned, 2 * excite + m)
    copies[2].wait()
    for e in range(excite):
        for m in range(2):
            li = inner_first(m, v)
            edge[2 * e + m] = edge_rows(n, f_in, e, li)
            turn(f_in[e, li], turned, 2 * e + m)
    copies[3].wait()
    copies[4].wait()


def look_rows(ids, spread):
    found = jnp.zeros(ids.shape, jnp.float32)
    for number in range(spread.shape[0]):
        found = jnp.where(ids == number, spread[number : number + 1], found)
    return found


def edge_kernel(forcing, ids, own_edge, spread, edge):
    v, n = lax.axis_index("vol"), lax.axis_index("narrow")
    excite = forcing.shape[0]
    half = own_edge.shape[0]
    edge[0:half] = own_edge[...]
    for m in range(2):
        li = inner_first(m, v)
        edge[half + 2 * excite + m] = look_rows(edge_rows(n, ids, li), spread)
        for e in range(excite):
            edge[half + 2 * e + m] = edge_rows(n, forcing, e, li)


def other_kernel(forcing, ids, spread, turned):
    v = lax.axis_index("vol")
    excite = forcing.shape[0]
    for m in range(2):
        li = inner_first(m, v)
        turn(look_rows(ids[li], spread), turned, 2 * excite + m)
        for e in range(excite):
            turn(forcing[e, li], turned, 2 * e + m)


def turned_edge(got):
    slabs, halo, cells_x = got.shape
    rows = jnp.concatenate([got[k] for k in range(slabs)], axis=0)
    behind = jnp.zeros((LANES - slabs * halo, cells_x), jnp.float32)
    return jnp.concatenate([rows, behind], axis=0).T


def with_edge(last, rows, slab, used, n):
    base = jnp.where(n == 0, used, LANES - HALO)
    lane = lax.broadcasted_iota(jnp.int32, last.shape, 1)
    moved = pltpu.roll(rows, lax.rem(base - HALO * slab + LANES, LANES), 1)
    return jnp.where((lane >= base) & (lane < base + HALO), moved, last)


def side_kernel(used, own, other, got, even, odd, turned):
    w, n = lax.axis_index("wide"), lax.axis_index("narrow")
    half = own.shape[0]
    cells_x, width = own.shape[1], own.shape[2]
    rows = turned_edge(got)
    turned[...] = rows
    left = lax.rem(w, 2) == 0
    for slab in range(2 * half):
        ref, k = (own, slab) if slab < half else (other, slab - half)
        sides = []
        for at in (0, cells_x - TILE):
            last = with_edge(ref[k, at : at + TILE, width - LANES :], rows[at : at + TILE], slab, used, n)
            sides.append(jnp.concatenate([ref[k, at : at + TILE, : width - LANES], last], axis=1))
        first, last = sides[0][0:HALO], sides[1][TILE - HALO :]
        even[slab] = jnp.where(left, last, first)
        odd[slab] = jnp.where(left, first, last)


def order(excite):
    half = 2 * excite + 2
    kinds = list(range(excite)) + [excite]
    return [(0 if m < 2 else half) + 2 * k + m % 2 for k in kinds for m in range(4)]


def extend_kernel(used, own, other, turned, even, ext):
    n = lax.axis_index("narrow")
    half = own.shape[0]
    cells_x, width = own.shape[1], own.shape[2]
    right = TILE + cells_x
    left = lax.rem(lax.axis_index("wide"), 2) == 0
    rows = turned[...]
    for place, slab in enumerate(order((half - 2) // 2)):
        ref, k = (own, slab) if slab < half else (other, slab - half)
        ext[place, 0:TILE] = jnp.zeros((TILE, width), jnp.float32)
        ext[place, right : right + TILE] = jnp.zeros((TILE, width), jnp.float32)
        ext[place, TILE:right, : width - LANES] = ref[k, :, : width - LANES]
        ext[place, TILE:right, width - LANES :] = with_edge(
            ref[k, :, width - LANES :], rows, slab, used, n
        )
        ext[place, TILE - HALO : TILE] = jnp.where(left, 0.0, even[slab])
        ext[place, right : right + HALO] = jnp.where(left, even[slab], 0.0)


def box(ref, first, m):
    total = ref[first + m]
    for z in (m - 1, m + 1):
        if 0 <= z < 4:
            total = total + ref[first + z]
    rows, width = total.shape
    total = total + pltpu.roll(total, 1, 0) + pltpu.roll(total, rows - 1, 0)
    return total + pltpu.roll(total, 1, 1) + pltpu.roll(total, width - 1, 1)


def residual(ext, hh, qq, u, cu, e, m):
    base = ext.shape[0] - 4
    c, k = ext[base + m], e * 4 + m
    near_sum = box(u, e * 4, m) - u[k]
    weighted = box(cu, e * 4, m) - cu[k]
    return (qq[k] - u[k]) + hh[m] * (c * near_sum + weighted)


def second(ext, hh, qq, u1, cu1, u2, cu2, e, m):
    k = e * 4 + m
    p = (1.0 + KEEP1) * u1[k] + GAIN1 * residual(ext, hh, qq, u1, cu1, e, m)
    u2[k] = p
    cu2[k] = p * ext[ext.shape[0] - 4 + m]


def third(ext, hh, qq, u2, cu2, u3, cu3, mv, e, m):
    k = e * 4 + m
    step = GAIN0 * residual(ext, hh, qq, u2, cu2, e, m)
    p = u2[k] + step
    mv[k] = step
    u3[k] = p
    cu3[k] = p * ext[ext.shape[0] - 4 + m]


def fourth(ext, hh, qq, u3, cu3, mv, e, m):
    k = e * 4 + m
    return u3[k] + KEEP1 * mv[k] + GAIN1 * residual(ext, hh, qq, u3, cu3, e, m)


def start_sweeps(ext, hh, qq, u1, cu1):
    base = ext.shape[0] - 4
    for m in range(4):
        c = ext[base + m]
        diagonal = 0.5 * (26.0 * c + (box(ext, base, m) - c)) + mass_ratio * c
        inverse = jnp.where(c > 0.0, 1.0 / diagonal, 0.0)
        hh[m] = 0.5 * inverse
        for e in range(base // 4):
            q = ext[e * 4 + m] * inverse
            qq[e * 4 + m] = q
            u1[e * 4 + m] = GAIN0 * q
            cu1[e * 4 + m] = (GAIN0 * q) * c


def sweep_kernel(stride, _, odd, ext, trace, aux, hh, qq, u1, cu1, u2, cu2, u3, cu3, mv, u4):
    w = lax.axis_index("wide")
    inner = (w > 0) & (w < lax.axis_size("wide") - 1)
    excite = u4.shape[0]
    width = ext.shape[2]
    cells_x = ext.shape[1] - 2 * TILE
    right = TILE + cells_x
    left = lax.rem(w, 2) == 0
    for place, slab in enumerate(order(excite)):
        outer = jnp.where(inner, odd[slab], 0.0)
        for at, here in ((TILE - HALO, left), (right, ~left)):
            ext[place, at : at + HALO] = jnp.where(here, outer, ext[place, at : at + HALO])
    start_sweeps(ext, hh, qq, u1, cu1)
    for e in range(excite):
        for m in range(3):
            second(ext, hh, qq, u1, cu1, u2, cu2, e, m)
        for m in range(2):
            third(ext, hh, qq, u2, cu2, u3, cu3, mv, e, m)
        u4[e] = fourth(ext, hh, qq, u3, cu3, mv, e, 0)

    columns = 2 * excite
    r = lax.broadcasted_iota(jnp.int32, (trace.shape[1], width), 0)
    lane = lax.broadcasted_iota(jnp.int32, (trace.shape[1], width), 1)
    s = lax.div(r, columns)
    hit = lane == s * stride
    picked = jnp.zeros(trace.shape[1:], jnp.float32)
    for col in range(columns):
        e, late = col % excite, col >= excite
        match = hit & (lax.rem(r, columns) == col)
        if late:
            match = match & (s > 0)
        values = (u4[e, TILE:right] if late else u2[e * 4, TILE:right]).astype(jnp.bfloat16)
        picked = picked + nt(jnp.where(match, 1.0, 0.0).astype(jnp.bfloat16), values)
    for j in range(trace.shape[0]):
        trace[j] = picked.astype(jnp.bfloat16)
    aux[...] = jnp.zeros(aux.shape, jnp.float32)
    for k, source in enumerate([u4[e] for e in range(excite)] + [ext[4 * excite], hh[0]]):
        aux[k : k + 1] = source[TILE:right, 0:LANES].T[0:1]


def field_kernel(ext, pressure, near, hh, qq, u1, cu1, u2, cu2, u3, cu3, mv):
    v = lax.axis_index("vol")
    excite, _, cells_y, _ = pressure.shape
    right = ext.shape[1] - TILE
    start_sweeps(ext, hh, qq, u1, cu1)
    for e in range(excite):
        for m in range(4):
            second(ext, hh, qq, u1, cu1, u2, cu2, e, m)
        for m in range(3):
            third(ext, hh, qq, u2, cu2, u3, cu3, mv, e, m)
        for m in range(2):
            p = fourth(ext, hh, qq, u3, cu3, mv, e, m)
            pressure[e, inner_first(m, v)] = p[TILE:right].T[0:cells_y]
    near[...] = jnp.zeros(near.shape, jnp.float32)
    for m in range(2):
        for k, source in enumerate((ext[4 * excite + m, TILE:right], hh[m, TILE:right])):
            back = source.T
            for i, y in enumerate((0, 1, cells_y - 1)):
                row = 6 * k + 3 * m + i
                near[row : row + 1] = back[y : y + 1]


def product_kernel(blocks, operator, aux, out):
    count = blocks.shape[0]
    tile_rows = operator.shape[0]

    def pair(p, sums):
        both = jnp.concatenate([blocks[2 * p], blocks[2 * p + 1]], axis=1)
        sums = list(sums)
        for s in range(BY):
            start = pl.multiple_of(s * count * LANES + p * (2 * LANES), 2 * LANES)
            group = s // 4 * 16
            sums[s % 4] = sums[s % 4] + nt(both[group : group + 16], operator[:, pl.ds(start, 2 * LANES)])
        return tuple(sums)

    zero = jnp.zeros((16, tile_rows), jnp.float32)
    sums = lax.fori_loop(0, count // 2, pair, (zero,) * 4)
    r = lax.broadcasted_iota(jnp.int32, zero.shape, 0)
    total = zero
    for q in range(4):
        total = total + jnp.where((r >= 4 * q) & (r < 4 * q + 4), sums[q], 0.0)
    total = total[0:8] + total[8:16]
    total = total + pltpu.roll(total, 4, 0)
    r = lax.broadcasted_iota(jnp.int32, total.shape, 0)
    total = jnp.where(r < 4, total, pltpu.roll(aux[...], 4, 0))
    for j in range(out.shape[0]):
        out[j] = total


def couple_kernel(flat, mine, theirs, traction, fix, save):
    w, n = lax.axis_index("wide"), lax.axis_index("narrow")
    count = flat.shape[0] // 16
    excite = 2
    targets = mine.shape[0]

    def field(k, r):
        return flat[pl.ds(k * 8 + r, count, stride=16), :]

    lane = lax.broadcasted_iota(jnp.int32, (count, LANES), 1)
    sub = lax.broadcasted_iota(jnp.int32, (count, LANES), 0)

    def before(a):
        return pltpu.roll(a, 1, 1)

    def after(a):
        moved = pltpu.roll(a, LANES - 1, 1)
        following = jnp.where(sub == count - 1, 0.0, pltpu.roll(moved, count - 1, 0))
        return jnp.where(lane == LANES - 1, following, moved)

    own = (1.0 + KEEP1) * GAIN0 + GAIN1 - GAIN1 * GAIN0
    sides = []
    for k in range(2):
        c, h = field(k, 4 + excite), field(k, 5 + excite)
        rows = []
        for e in range(excite):
            t = field(0, e) + field(1, e)
            if k:
                t = pltpu.roll(t, LANES - targets, 1)
            t = jnp.where(lane < targets, t, 0.0)
            u = (2.0 * couple_gain) * h * t
            cu = c * u
            around, c_around = before(u) + after(u), before(cu) + after(cu)
            change = own * u + (GAIN0 * GAIN1) * h * (c * around + c_around)
            save[k, 0, e] = change
            save[k, 1, e] = around + u
            save[k, 2, e] = c_around + cu
            rows.append(field(k, 4 + e) + change)
        sides.append(rows)

    groups = count // 8
    total = jnp.zeros((16, targets), jnp.float32)
    r = lax.broadcasted_iota(jnp.int32, total.shape, 0)
    for g in range(groups):
        both = [
            jnp.concatenate([sides[k][e][8 * g : 8 * g + 8] for e in range(excite)], axis=0)
            for k in range(2)
        ]
        for ref, left in (
            (mine, jnp.where(n == 0, both[0], both[1])),
            (theirs, jnp.where(n == 0, both[1], both[0])),
        ):
            left = left.astype(jnp.bfloat16)
            for j in range(8):
                part = nt(left, ref[:, (8 * g + j) * LANES : (8 * g + j + 1) * LANES])
                total = total + jnp.where((r & 7) == j, part, 0.0)
    first = flat[pl.ds(pl.multiple_of(w * 16, 16), 8), :] + flat[pl.ds(pl.multiple_of(w * 16 + 8, 8), 8), :]
    first = jnp.where(n == 0, first, pltpu.roll(first, LANES - targets, 1))
    traction[...] = jnp.zeros(traction.shape, jnp.float32)
    for e in range(excite):
        traction[e : e + 1, 0:targets] = (
            jnp.sum(total[8 * e : 8 * e + 8], axis=0, keepdims=True)
            + first[2 + e : 3 + e, 0:targets]
        )

    fix[...] = jnp.zeros(fix.shape, jnp.float32)
    for e in range(excite):
        for i in range(3):
            row = 2 * i + e
            fix[row : row + 1] = save[n, i, e, pl.ds(w, 1), :]
        for i in range(1, 3):
            row = 4 + 2 * i + e
            fix[row : row + 1] = jnp.where(n == 0, save[1, i, e, pl.ds(w, 1), :], 0.0)


def mend_kernel(pressure, near, fix, out):
    v = lax.axis_index("vol")
    excite, _, cells_y, cells_x = pressure.shape
    r = lax.broadcasted_iota(jnp.int32, (8, cells_x), 0)
    out[...] = pressure[...]
    for e in range(excite):
        for m in range(2):
            li = v if m == 0 else 1 - v

            def change(i, a, b):
                c, h = near[3 * m + i : 3 * m + i + 1], near[6 + 3 * m + i : 7 + 3 * m + i]
                return (GAIN0 * GAIN1) * h * (c * fix[a + e : a + e + 1] + fix[b + e : b + e + 1])

            row0 = fix[e : e + 1] if m == 0 else change(0, 2, 4)
            delta = jnp.where(r == 0, row0, jnp.where(r == 1, change(1, 2, 4), 0.0))
            out[e, li, 0:8] = pressure[e, li, 0:8] + delta
            delta = jnp.where(r == 7, change(2, 6, 8), 0.0)
            out[e, li, cells_y - 8 : cells_y] = pressure[e, li, cells_y - 8 : cells_y] + delta


def local(forcing, material_ids, materials, boundary_operator):
    vols, wides, narrows = (lax.axis_size(a) for a in ("vol", "wide", "narrow"))
    v = lax.axis_index("vol")
    excite, layers, cells_y, cells_x = forcing.shape
    assert (vols, narrows, excite, layers, cells_x) == (2, 2, 2, 2, LANES)
    assert wides % 8 == 0 and wides & (wides - 1) == 0
    tile_rows = boundary_operator.shape[0]
    targets = tile_rows // narrows
    assert tile_rows == LANES and BY * 2 * excite == 64
    width = -(-(cells_y + 2 * HALO) // LANES) * LANES
    slabs = 4 * excite + 4
    f32, bf16 = jnp.float32, jnp.bfloat16
    everyone = ("vol", "wide", "narrow")
    vmem = pl.BlockSpec(memory_space=pltpu.VMEM)

    hbm = pl.BlockSpec(memory_space=pltpu.HBM)

    def call(kernel, shapes, specs, scratch=(), limit=4, **more):
        return pl.pallas_call(
            kernel,
            out_shape=[jax.ShapeDtypeStruct(*s) for s in shapes],
            in_specs=specs,
            out_specs=[vmem] * len(shapes),
            scratch_shapes=list(scratch),
            compiler_params=pltpu.CompilerParams(vmem_limit_bytes=limit * 2**20),
            **more,
        )

    def swap(x, axis):
        return lax.ppermute(x, axis, [(0, 1), (1, 0)])

    def number(a, b, c):
        return (a * wides + b) * narrows + c

    def in_hbm(x):
        return pltpu.with_memory_space_constraint(x, pltpu.HBM)

    dma = pltpu.SemaphoreType.DMA
    half = slabs // 2
    f_other, id_other = swap(forcing, "vol"), swap(material_ids, "vol")
    own, edge, spread, sent, mine = call(
        own_kernel,
        [
            ((half, cells_x, width), f32),
            ((half, HALO, cells_x), f32),
            ((materials.shape[0], LANES), f32),
        ]
        + [((targets, wides * LANES), bf16)] * 2,
        [hbm] * 4,
        [
            pltpu.VMEM(forcing.shape, f32),
            pltpu.VMEM(material_ids.shape, jnp.int32),
            pltpu.SMEM(materials.shape, f32),
            dma((5,)),
        ],
    )(in_hbm(materials), in_hbm(forcing), in_hbm(material_ids), in_hbm(boundary_operator))
    (edge,) = call(edge_kernel, [((slabs, HALO, cells_x), f32)], [vmem] * 4)(
        f_other, id_other, edge, spread
    )
    edge = swap(edge, "narrow")
    (other,) = call(other_kernel, [((half, cells_x, width), f32)], [vmem] * 3)(
        f_other, id_other, spread
    )
    used = cells_y - (width - LANES)
    even, odd, turned = call(
        functools.partial(side_kernel, used),
        [((slabs, HALO, width), f32)] * 2 + [((cells_x, LANES), f32)],
        [vmem] * 3,
    )(own, other, edge)
    even = lax.ppermute(even, "wide", [(i, i ^ 1) for i in range(wides)])
    odd_pairs = []
    for a in range(vols):
        for b in range(wides):
            for c in range(narrows):
                far = b + 1 if b % 2 else b - 1
                there = (far, c) if 0 <= far < wides else (b, 1 - c)
                odd_pairs.append((number(a, b, c), number(a, *there)))
    odd = lax.ppermute(odd, everyone, odd_pairs)
    rows = cells_x + 2 * TILE
    full = (rows, width)
    (ext,) = call(
        functools.partial(extend_kernel, used), [((slabs,) + full, f32)], [vmem] * 4
    )(own, other, turned, even)
    theirs = swap(sent, "narrow")
    many = pltpu.VMEM((4 * excite,) + full, f32)
    scratch = [pltpu.VMEM((4,) + full, f32)] + [many] * 8
    ext, trace, aux = call(
        functools.partial(sweep_kernel, cells_y // BY),
        [
            ((slabs,) + full, f32),
            ((wides, BY * 2 * excite, cells_x), bf16),
            ((8, cells_x), f32),
        ],
        [vmem] * 2,
        scratch + [pltpu.VMEM((excite,) + full, f32)],
        20,
        input_output_aliases={0: 0},
    )(ext, odd)

    def field(ext):
        shapes = [(forcing.shape, f32), ((16, cells_x), f32)]
        return call(field_kernel, shapes, [vmem], scratch, 20)(ext)

    def couple(ext, trace, aux, operator, theirs):
        blocks = lax.all_to_all(trace, "wide", 0, 0)
        pressure, near = field(ext)
        (sums,) = call(product_kernel, [((wides * narrows, 8, tile_rows), f32)], [vmem] * 3, (), 24)(
            blocks, operator, aux
        )
        blocks = lax.all_to_all(sums, ("wide", "narrow"), 0, 0)
        traction, fix = call(
            couple_kernel,
            [((8, LANES), f32), ((16, cells_x), f32)],
            [vmem] * 3,
            [pltpu.VMEM((2, 3, excite, wides, LANES), f32)],
        )(blocks.reshape(wides * narrows * 8, LANES), mine, theirs)
        return pressure, near, traction, fix

    def nothing(ext, *_):
        pressure, near = field(ext)
        return pressure, near, jnp.zeros((8, LANES), f32), jnp.zeros((16, cells_x), f32)

    pressure, near, traction, fix = lax.cond(
        v == vols - 1, couple, nothing, ext, trace, aux, boundary_operator, theirs
    )
    (pressure,) = call(mend_kernel, [(forcing.shape, f32)], [vmem] * 3)(pressure, near, fix)
    column = traction[0:2, :targets]
    lower = swap(column, "vol")
    column = jnp.where(v == vols - 1, column[1:2], lower[0:1])
    return pressure, column.reshape(targets, 1)


def solution(mesh):
    placed = (
        P(None, "vol", "narrow", "wide"),
        P("vol", "narrow", "wide"),
        P(),
        P("wide", "narrow"),
    )

    return jax.shard_map(
        local,
        mesh=mesh,
        in_specs=placed,
        out_specs=(P(None, "vol", "narrow", "wide"), P(("wide", "narrow"), "vol")),
        check_vma=False,
    )
```

time: 51.1 us -> 44 us (0.86)
  local copies, waits for them, and re-layouts: 6.15 us -> 0.02 us
  starting transfers between devices: 30 us -> 26.2 us
  Pallas kernels: 6.66 us -> 10.1 us
  waiting for transfers between devices: 6.69 us -> 5.97 us
    unnamed x12 -> x2, local copies, waits for them, and re-layouts: 5.15 us -> 0.01 us
    ppermute x5, starting transfers between devices: 27.8 us -> 22.9 us  [swap(): return lax.ppermute(x, axis, [(0, 1), (1, 0)])]
    pallas_call x3 -> x7, Pallas kernels: 5.88 us -> 9.33 us  [the longest x1 4.16 us: field(): return call(field_kernel, shapes, [vmem], scratch, 20)(ext)]
    ppermute x1, waiting for transfers between devices: 1.96 us -> 0.86 us  [local(): even = lax.ppermute(even, 'wide', [(i, i ^ 1) for i in range(wides)])]
    slice x1 -> x0, local copies, waits for them, and re-layouts: 0.97 us -> none  [local(): head = boundary_operator[:, :wides * LANES]]
    ppermute x1, starting transfers between devices: 0.64 us -> 1.52 us  [local(): odd = lax.ppermute(odd, everyone, odd_pairs)]
  transfers between devices with their start and end apart: 7 -> 7, of which waited for: 3 -> 3; matrix products, arithmetic and copies ran while one was open for 2% -> 0% of each run, Pallas kernels for 13% -> 14%
where the time goes in v3:
time: 44 us; the launch traced here: 43.8 us
  starting transfers between devices  26.2 us (60%)
  Pallas kernels  10.1 us (23%)
  waiting for transfers between devices  5.97 us (14%)
  between operations  0.71 us (2%)
  other arithmetic  0.51 us (1%)
    ppermute x5, starting transfers between devices, swap(): return lax.ppermute(x, axis, [(0, 1), (1, 0)])  22.9 us
    pallas_call x1, Pallas kernels, field(): return call(field_kernel, shapes, [vmem], scratch, 20)(ext)  4.16 us
    ppermute x5, waiting for transfers between devices, swap(): return lax.ppermute(x, axis, [(0, 1), (1, 0)])  3.68 us
    pallas_call x1, Pallas kernels, local(): call(functools.partial(sweep_kernel, cells_y // BY), [((slabs,) + full, f...  3.06 us
    ppermute x1, starting transfers between devices, local(): even = lax.ppermute(even, 'wide', [(i, i ^ 1) for i in range(wides)])  1.78 us
    ppermute x1, starting transfers between devices, local(): odd = lax.ppermute(odd, everyone, odd_pairs)  1.52 us
    ppermute x1, waiting for transfers between devices, local(): odd = lax.ppermute(odd, everyone, odd_pairs)  1.43 us
    pallas_call x1, Pallas kernels, local(): call(own_kernel, [((half, cells_x, width), f32), ((half, HALO, cells_x),...  1.36 us
  transfers between devices with their start and end apart: 7, of which 3 were waited for; matrix products, arithmetic and copies ran while one was open for 0% of the time, Pallas kernels for 14%

profile of v3, /device:TPU:0, one launch (start us, length us, event | category | flops | bytes accessed | tf_op | source)
XLA Modules:
  0.0 43.8 jit_solution(7915116934688192776)
XLA Ops:
  0.6 0.6 %collective-permute-start = (f32[2,2,192,128]{3,2,1,0:T(8,128)}, f32[2,2,192,128]{3,2,1,0:T(8,128)S(1)}, u32[]{:S(2)}, u32[]{:S(2)}) collective-permute-start(f32[2,2,192,128]{3,2,1,0:T(8,128)} %forcing.1), channel_id=1, source_target_pairs={{0,16},{16,0},{1,17},{17,1},{2,18},{18,2},{3,19},{19,3},{4,20},{20... | collective-permute-start | bytes 1179656 | tf_op jit(solution)/shard_map/ppermute | solution.py:448
  1.2 0.1 collective-permute-start.1
  1.3 1.4 %shard_map.59 = (f32[6,128,256]{2,1,0:T(8,128)S(1)}, f32[6,4,128]{2,1,0:T(4,128)S(1)}, f32[8,128]{1,0:T(8,128)S(1)}, bf16[64,1024]{1,0:T(8,128)(2,1)S(1)}, bf16[64,1024]{1,0:T(8,128)(2,1)S(1)}) custom-call(f32[8]{0:T(128)} %table.1, f32[2,2,192,128]{3,2,1,0:T(8,128)} %forcing.1, s32[2,192,128]{2,1,0:T(8,128)} %ids.1, bf16[128,16384]{1,0:T(8,128)(2,1)} %operator.1), custom_call_target="tpu_custom_call" | custom-call | tf_op jit(solution)/shard_map/pallas_call | solution.py:459
  2.6 3.0 %collective-permute-start.5 = (bf16[64,1024]{1,0:T(8,128)(2,1)S(1)}, bf16[64,1024]{1,0:T(8,128)(2,1)S(1)}, u32[]{:S(2)}, u32[]{:S(2)}) collective-permute-start(bf16[64,1024]{1,0:T(8,128)(2,1)S(1)} %get-tuple-element.52), channel_id=1, source_target_pairs={{0,1},{1,0},{2,3},{3,2},{4,5},{5,4},{6,7},{7,6},{8,9},{9,8},{10,11... | collective-permute-start | bytes 393224 | tf_op jit(solution)/shard_map/ppermute | solution.py:448
  5.6 0.0 collective-permute-done.1.ids
  5.6 0.0 collective-permute-done.forcing
  5.7 0.3 collective-permute-start.2
  6.0 0.3 shard_map.60.other
  6.3 3.6 %collective-permute-done.2.got = f32[12,4,128]{2,1,0:T(4,128)S(1)} collective-permute-done((f32[12,4,128]{2,1,0:T(4,128)S(1)}, f32[12,4,128]{2,1,0:T(4,128)S(1)}, u32[]{:S(2)}, u32[]{:S(2)}) %collective-permute-start.2) | collective-permute-done | bytes 24608 | tf_op jit(solution)/shard_map/ppermute | solution.py:448
  9.9 0.2 shard_map.62
  10.1 1.8 %collective-permute-start.3 = (f32[12,4,256]{2,1,0:T(4,128)S(1)}, f32[12,4,256]{2,1,0:T(4,128)S(1)}, u32[]{:S(2)}, u32[]{:S(2)}) collective-permute-start(f32[12,4,256]{2,1,0:T(4,128)S(1)} %get-tuple-element.46), channel_id=1, source_target_pairs={{0,2},{2,0},{4,6},{6,4},{8,10},{10,8},{12,14},{14,12},{1,3},{3,1},... | collective-permute-start | bytes 147464 | tf_op jit(solution)/shard_map/ppermute | solution.py:488
  11.9 1.5 %collective-permute-start.4 = (f32[12,4,256]{2,1,0:T(4,128)S(1)}, f32[12,4,256]{2,1,0:T(4,128)S(1)}, u32[]{:S(2)}, u32[]{:S(2)}) collective-permute-start(f32[12,4,256]{2,1,0:T(4,128)S(1)} %get-tuple-element.47), channel_id=1, source_target_pairs={{0,1},{1,0},{2,4},{3,5},{4,2},{5,3},{6,8},{7,9},{8,6},{9,7},{10,12... | collective-permute-start | bytes 147464 | tf_op jit(solution)/shard_map/ppermute | solution.py:496
  13.4 0.9 %collective-permute-done.3.even = f32[12,4,256]{2,1,0:T(4,128)S(1)} collective-permute-done((f32[12,4,256]{2,1,0:T(4,128)S(1)}, f32[12,4,256]{2,1,0:T(4,128)S(1)}, u32[]{:S(2)}, u32[]{:S(2)}) %collective-permute-start.3) | collective-permute-done | bytes 49184 | tf_op jit(solution)/shard_map/ppermute | solution.py:488
  14.3 0.0 copy-start.2
  14.3 0.3 shard_map.63._
  14.5 1.4 %collective-permute-done.4.odd = f32[12,4,256]{2,1,0:T(4,128)S(1)} collective-permute-done((f32[12,4,256]{2,1,0:T(4,128)S(1)}, f32[12,4,256]{2,1,0:T(4,128)S(1)}, u32[]{:S(2)}, u32[]{:S(2)}) %collective-permute-start.4) | collective-permute-done | bytes 49184 | tf_op jit(solution)/shard_map/ppermute | solution.py:496
  16.0 3.1 %shard_map.64 = (f32[12,144,256]{2,1,0:T(8,128)S(1)}, bf16[8,64,128]{2,1,0:T(8,128)(2,1)S(1)}, f32[8,128]{1,0:T(8,128)S(1)}) custom-call(f32[12,144,256]{2,1,0:T(8,128)S(1)} %shard_map.63._, f32[12,4,256]{2,1,0:T(4,128)S(1)} %collective-permute-done.4.odd), custom_call_target="tpu_custom_call", output_to_operand_aliasing={{0}: (0, {})} | custom-call | tf_op jit(solution)/shard_map/pallas_call | solution.py:505
  19.0 0.0 collective-permute-done.5
  19.0 0.0 copy-done.2
  19.1 4.4 %conditional.1 = (f32[2,2,192,128]{3,2,1,0:T(8,128)S(1)}, f32[16,128]{1,0:T(8,128)S(1)}, f32[8,128]{1,0:T(8,128)S(1)}, f32[16,128]{1,0:T(8,128)S(1)}) conditional(s32[]{:T(128)} %convert_element_type.3, f32[12,144,256]{2,1,0:T(8,128)S(1)} %get-tuple-element.48, (f32[12,144,256]{2,1,0:T(8,128)S(1)}, bf16[8,64,128]{2,1,0:T(8,128)(2,1)S(1)}, ...), branch_computations={%region_0.0_spmd, %region_1.0_spmd} | conditional | bytes 14614648 | solution.py:541
  19.1 4.2 %branch_0_fun.1 = (f32[2,2,192,128]{3,2,1,0:T(8,128)S(1)}, f32[16,128]{1,0:T(8,128)S(1)}) custom-call(f32[12,144,256]{2,1,0:T(8,128)S(1)} %ext), custom_call_target="tpu_custom_call" | custom-call | tf_op jit(solution)/shard_map/cond/branch_0_fun/pallas_call | solution.py:520
  23.5 19.0 %collective-permute-start.6 = (f32[2,64]{1,0:T(2,128)S(1)}, f32[2,64]{1,0:T(2,128)S(1)}, u32[]{:S(2)}, u32[]{:S(2)}) collective-permute-start(f32[2,64]{1,0:T(2,128)S(1)} %slice.11), channel_id=1, source_target_pairs={{0,16},{16,0},{1,17},{17,1},{2,18},{18,2},{3,19},{19,3},{4,20},{20... | collective-permute-start | bytes 1544 | tf_op jit(solution)/shard_map/ppermute | solution.py:448
  42.5 0.8 %shard_map.65 = f32[2,2,192,128]{3,2,1,0:T(8,128)} custom-call(f32[2,2,192,128]{3,2,1,0:T(8,128)S(1)} %get-tuple-element.53.pressure, f32[16,128]{1,0:T(8,128)S(1)} %get-tuple-element.54.near, f32[16,128]{1,0:T(8,128)S(1)} %get-tuple-element.55.fix), custom_call_target="tpu_custom_call" | custom-call | tf_op jit(solution)/shard_map/pallas_call | solution.py:544
  43.2 0.0 collective-permute-done.6
  43.3 0.5 %fusion = f32[64,1]{0,1:T(1,128)} fusion(pred[]{:T(512)S(6)} %eq.4, f32[2,64]{1,0:T(2,128)S(1)} %collective-permute-done.6, f32[8,128]{1,0:T(8,128)S(1)} %get-tuple-element.56), kind=kLoop, calls=%fused_computation.1 | loop fusion | flops 64 | bytes 769 | tf_op jit(solution)/shard_map/reshape | solution.py:548
  (4 shorter events, 0.0 us)
Async XLA Ops:
  0.6 5.0 %collective-permute-start = (f32[2,2,192,128]{3,2,1,0:T(8,128)}, f32[2,2,192,128]{3,2,1,0:T(8,128)S(1)}, u32[]{:S(2)}, u32[]{:S(2)}) collective-permute-start(f32[2,2,192,128]{3,2,1,0:T(8,128)} %forcing.1), channel_id=1, source_target_pairs={{0,16},{16,0},{1,17},{17,1},{2,18},{18,2},{3,19},{19,3},{4,20},{20... | collective-permute-start | bytes 1179656 | tf_op jit(solution)/shard_map/ppermute | solution.py:448
  1.2 4.5 %collective-permute-start.1 = (s32[2,192,128]{2,1,0:T(8,128)}, s32[2,192,128]{2,1,0:T(8,128)S(1)}, u32[]{:S(2)}, u32[]{:S(2)}) collective-permute-start(s32[2,192,128]{2,1,0:T(8,128)} %ids.1), channel_id=1, source_target_pairs={{0,16},{16,0},{1,17},{17,1},{2,18},{18,2},{3,19},{19,3},{4,20},{20... | collective-permute-start | bytes 589832 | tf_op jit(solution)/shard_map/ppermute | solution.py:448
  2.6 16.4 %collective-permute-start.5 = (bf16[64,1024]{1,0:T(8,128)(2,1)S(1)}, bf16[64,1024]{1,0:T(8,128)(2,1)S(1)}, u32[]{:S(2)}, u32[]{:S(2)}) collective-permute-start(bf16[64,1024]{1,0:T(8,128)(2,1)S(1)} %get-tuple-element.52), channel_id=1, source_target_pairs={{0,1},{1,0},{2,3},{3,2},{4,5},{5,4},{6,7},{7,6},{8,9},{9,8},{10,11... | collective-permute-start | bytes 393224 | tf_op jit(solution)/shard_map/ppermute | solution.py:448
  5.7 4.2 %collective-permute-start.2 = (f32[12,4,128]{2,1,0:T(4,128)S(1)}, f32[12,4,128]{2,1,0:T(4,128)S(1)}, u32[]{:S(2)}, u32[]{:S(2)}) collective-permute-start(f32[12,4,128]{2,1,0:T(4,128)S(1)} %shard_map.61), channel_id=1, source_target_pairs={{0,1},{1,0},{2,3},{3,2},{4,5},{5,4},{6,7},{7,6},{8,9},{9,8},{10,11... | collective-permute-start | bytes 73736 | tf_op jit(solution)/shard_map/ppermute | solution.py:448
  10.1 4.2 %collective-permute-start.3 = (f32[12,4,256]{2,1,0:T(4,128)S(1)}, f32[12,4,256]{2,1,0:T(4,128)S(1)}, u32[]{:S(2)}, u32[]{:S(2)}) collective-permute-start(f32[12,4,256]{2,1,0:T(4,128)S(1)} %get-tuple-element.46), channel_id=1, source_target_pairs={{0,2},{2,0},{4,6},{6,4},{8,10},{10,8},{12,14},{14,12},{1,3},{3,1},... | collective-permute-start | bytes 147464 | tf_op jit(solution)/shard_map/ppermute | solution.py:488
  11.9 4.1 %collective-permute-start.4 = (f32[12,4,256]{2,1,0:T(4,128)S(1)}, f32[12,4,256]{2,1,0:T(4,128)S(1)}, u32[]{:S(2)}, u32[]{:S(2)}) collective-permute-start(f32[12,4,256]{2,1,0:T(4,128)S(1)} %get-tuple-element.47), channel_id=1, source_target_pairs={{0,1},{1,0},{2,4},{3,5},{4,2},{5,3},{6,8},{7,9},{8,6},{9,7},{10,12... | collective-permute-start | bytes 147464 | tf_op jit(solution)/shard_map/ppermute | solution.py:496
  14.3 4.8 %copy-start.2 = (bf16[128,16384]{1,0:T(8,128)(2,1)S(1)}, bf16[128,16384]{1,0:T(8,128)(2,1)}, u32[]{:S(2)}) copy-start(bf16[128,16384]{1,0:T(8,128)(2,1)} %operator.1) | copy-start | bytes 12582916
  23.5 19.8 %collective-permute-start.6 = (f32[2,64]{1,0:T(2,128)S(1)}, f32[2,64]{1,0:T(2,128)S(1)}, u32[]{:S(2)}, u32[]{:S(2)}) collective-permute-start(f32[2,64]{1,0:T(2,128)S(1)} %slice.11), channel_id=1, source_target_pairs={{0,16},{16,0},{1,17},{17,1},{2,18},{18,2},{3,19},{19,3},{4,20},{20... | collective-permute-start | bytes 1544 | tf_op jit(solution)/shard_map/ppermute | solution.py:448

commit v4 on v3

--- a/solution.py
+++ b/solution.py
@@ -160,13 +160,14 @@
     return [(0 if m < 2 else half) + 2 * k + m % 2 for k in kinds for m in range(4)]
 
 
-def extend_kernel(used, own, other, turned, even, ext):
+def extend_kernel(used, own, other, turned, even, ext, saved, sems):
     n = lax.axis_index("narrow")
     half = own.shape[0]
     cells_x, width = own.shape[1], own.shape[2]
     right = TILE + cells_x
     left = lax.rem(lax.axis_index("wide"), 2) == 0
     rows = turned[...]
+    copies = []
     for place, slab in enumerate(order((half - 2) // 2)):
         ref, k = (own, slab) if slab < half else (other, slab - half)
         ext[place, 0:TILE] = jnp.zeros((TILE, width), jnp.float32)
@@ -177,6 +178,10 @@
         )
         ext[place, TILE - HALO : TILE] = jnp.where(left, 0.0, even[slab])
         ext[place, right : right + HALO] = jnp.where(left, even[slab], 0.0)
+        copies.append(pltpu.make_async_copy(ext.at[place], saved.at[place], sems.at[place]))
+        copies[place].start()
+    for copy in copies:
+        copy.wait()
 
 
 def box(ref, first, m):
@@ -232,7 +237,9 @@
             cu1[e * 4 + m] = (GAIN0 * q) * c
 
 
-def sweep_kernel(stride, _, odd, ext, trace, aux, hh, qq, u1, cu1, u2, cu2, u3, cu3, mv, u4):
+def sweep_kernel(
+    stride, _, __, odd, ext, saved, trace, aux, hh, qq, u1, cu1, u2, cu2, u3, cu3, mv, u4, sems
+):
     w = lax.axis_index("wide")
     inner = (w > 0) & (w < lax.axis_size("wide") - 1)
     excite = u4.shape[0]
@@ -244,6 +251,11 @@
         outer = jnp.where(inner, odd[slab], 0.0)
         for at, here in ((TILE - HALO, left), (right, ~left)):
             ext[place, at : at + HALO] = jnp.where(here, outer, ext[place, at : at + HALO])
+    copies = []
+    for k, at in enumerate((0, right)):
+        edge = ext.at[:, at : at + TILE], saved.at[:, at : at + TILE]
+        copies.append(pltpu.make_async_copy(*edge, sems.at[k]))
+        copies[k].start()
     start_sweeps(ext, hh, qq, u1, cu1)
     for e in range(excite):
         for m in range(3):
@@ -270,6 +282,8 @@
     aux[...] = jnp.zeros(aux.shape, jnp.float32)
     for k, source in enumerate([u4[e] for e in range(excite)] + [ext[4 * excite], hh[0]]):
         aux[k : k + 1] = source[TILE:right, 0:LANES].T[0:1]
+    for copy in copies:
+        copy.wait()
 
 
 def field_kernel(ext, pressure, near, hh, qq, u1, cu1, u2, cu2, u3, cu3, mv):
@@ -298,17 +312,27 @@
     count = blocks.shape[0]
     tile_rows = operator.shape[0]
 
-    def pair(p, sums):
-        both = jnp.concatenate([blocks[2 * p], blocks[2 * p + 1]], axis=1)
+    def pairs(first, sums):
         sums = list(sums)
-        for s in range(BY):
-            start = pl.multiple_of(s * count * LANES + p * (2 * LANES), 2 * LANES)
-            group = s // 4 * 16
-            sums[s % 4] = sums[s % 4] + nt(both[group : group + 16], operator[:, pl.ds(start, 2 * LANES)])
+        for p in range(4):
+            p = first * 4 + p
+            both = jnp.concatenate([blocks[2 * p], blocks[2 * p + 1]], axis=1)
+            for s in range(BY):
+                start = s * count * LANES + p * (2 * LANES)
+                if not isinstance(start, int):
+                    start = pl.multiple_of(start, 2 * LANES)
+                group = s // 4 * 16
+                sums[s % 4] = sums[s % 4] + nt(
+                    both[group : group + 16], operator[:, pl.ds(start, 2 * LANES)]
+                )
         return tuple(sums)
 
     zero = jnp.zeros((16, tile_rows), jnp.float32)
-    sums = lax.fori_loop(0, count // 2, pair, (zero,) * 4)
+    sums = (zero,) * 4
+    if count == 8:
+        sums = pairs(0, sums)
+    else:
+        sums = lax.fori_loop(0, count // 8, pairs, sums)
     r = lax.broadcasted_iota(jnp.int32, zero.shape, 0)
     total = zero
     for q in range(4):
@@ -433,12 +457,12 @@
 
     hbm = pl.BlockSpec(memory_space=pltpu.HBM)
 
-    def call(kernel, shapes, specs, scratch=(), limit=4, **more):
+    def call(kernel, shapes, specs, scratch=(), limit=4, outs=None, **more):
         return pl.pallas_call(
             kernel,
-            out_shape=[jax.ShapeDtypeStruct(*s) for s in shapes],
+            out_shape=[jax.ShapeDtypeStruct(*s) if isinstance(s, tuple) else s for s in shapes],
             in_specs=specs,
-            out_specs=[vmem] * len(shapes),
+            out_specs=outs or [vmem] * len(shapes),
             scratch_shapes=list(scratch),
             compiler_params=pltpu.CompilerParams(vmem_limit_bytes=limit * 2**20),
             **more,
@@ -496,24 +520,30 @@
     odd = lax.ppermute(odd, everyone, odd_pairs)
     rows = cells_x + 2 * TILE
     full = (rows, width)
-    (ext,) = call(
-        functools.partial(extend_kernel, used), [((slabs,) + full, f32)], [vmem] * 4
+    ext, saved = call(
+        functools.partial(extend_kernel, used),
+        [((slabs,) + full, f32), pltpu.HBM((slabs,) + full, f32)],
+        [vmem] * 4,
+        [dma((slabs,))],
+        outs=[vmem, hbm],
     )(own, other, turned, even)
     theirs = swap(sent, "narrow")
     many = pltpu.VMEM((4 * excite,) + full, f32)
     scratch = [pltpu.VMEM((4,) + full, f32)] + [many] * 8
-    ext, trace, aux = call(
+    _, ext, trace, aux = call(
         functools.partial(sweep_kernel, cells_y // BY),
         [
             ((slabs,) + full, f32),
+            pltpu.HBM((slabs,) + full, f32),
             ((wides, BY * 2 * excite, cells_x), bf16),
             ((8, cells_x), f32),
         ],
-        [vmem] * 2,
-        scratch + [pltpu.VMEM((excite,) + full, f32)],
+        [vmem, hbm, vmem],
+        scratch + [pltpu.VMEM((excite,) + full, f32), dma((2,))],
         20,
-        input_output_aliases={0: 0},
-    )(ext, odd)
+        outs=[vmem, hbm, vmem, vmem],
+        input_output_aliases={0: 0, 1: 1},
+    )(ext, saved, odd)
 
     def field(ext):
         shapes = [(forcing.shape, f32), ((16, cells_x), f32)]

time: 44 us -> 42.6 us (0.968)
  starting transfers between devices: 26.2 us -> 23.3 us
  Pallas kernels: 10.1 us -> 12.8 us
  waiting for transfers between devices: 5.97 us -> 4.79 us
    ppermute x5, starting transfers between devices: 22.9 us -> 20 us  [swap(): return lax.ppermute(x, axis, [(0, 1), (1, 0)])]
    pallas_call x1, Pallas kernels: 4.16 us -> 5.63 us  [field(): return call(field_kernel, shapes, [vmem], scratch, 20)(ext)]
    ppermute x1, waiting for transfers between devices: 1.43 us -> 0.25 us  [local(): odd = lax.ppermute(odd, everyone, odd_pairs)]
    pallas_call x1, Pallas kernels: 0.28 us -> 1.45 us  [local(): call(functools.partial(extend_kernel, used), [((slabs,) + full, f32), plt...]
  transfers between devices with their start and end apart: 7 -> 7, of which waited for: 3 -> 3; matrix products, arithmetic and copies ran while one was open for 0% -> 0% of each run, Pallas kernels for 14% -> 17%
where the time goes in v4:
time: 42.6 us; the launch traced here: 42.4 us
  starting transfers between devices  23.3 us (55%)
  Pallas kernels  12.8 us (30%)
  waiting for transfers between devices  4.79 us (11%)
  between operations  0.72 us (2%)
  other arithmetic  0.51 us (1%)
    ppermute x5, starting transfers between devices, swap(): return lax.ppermute(x, axis, [(0, 1), (1, 0)])  20 us
    pallas_call x1, Pallas kernels, field(): return call(field_kernel, shapes, [vmem], scratch, 20)(ext)  5.63 us
    ppermute x5, waiting for transfers between devices, swap(): return lax.ppermute(x, axis, [(0, 1), (1, 0)])  3.68 us
    pallas_call x1, Pallas kernels, local(): call(functools.partial(sweep_kernel, cells_y // BY), [((slabs,) + full, f...  3.09 us
    ppermute x1, starting transfers between devices, local(): even = lax.ppermute(even, 'wide', [(i, i ^ 1) for i in range(wides)])  1.78 us
    ppermute x1, starting transfers between devices, local(): odd = lax.ppermute(odd, everyone, odd_pairs)  1.52 us
    pallas_call x1, Pallas kernels, local(): call(functools.partial(extend_kernel, used), [((slabs,) + full, f32), plt...  1.45 us
    pallas_call x1, Pallas kernels, local(): call(own_kernel, [((half, cells_x, width), f32), ((half, HALO, cells_x),...  1.36 us
  transfers between devices with their start and end apart: 7, of which 3 were waited for; matrix products, arithmetic and copies ran while one was open for 0% of the time, Pallas kernels for 17%

profile of v4, /device:TPU:0, one launch (start us, length us, event | category | flops | bytes accessed | tf_op | source)
XLA Modules:
  0.0 42.4 jit_solution(9606162280748898506)
XLA Ops:
  0.6 0.6 %collective-permute-start = (f32[2,2,192,128]{3,2,1,0:T(8,128)}, f32[2,2,192,128]{3,2,1,0:T(8,128)S(1)}, u32[]{:S(2)}, u32[]{:S(2)}) collective-permute-start(f32[2,2,192,128]{3,2,1,0:T(8,128)} %forcing.1), channel_id=1, source_target_pairs={{0,16},{16,0},{1,17},{17,1},{2,18},{18,2},{3,19},{19,3},{4,20},{20... | collective-permute-start | bytes 1179656 | tf_op jit(solution)/shard_map/ppermute | solution.py:472
  1.2 0.1 collective-permute-start.1
  1.3 1.4 %shard_map.59 = (f32[6,128,256]{2,1,0:T(8,128)S(1)}, f32[6,4,128]{2,1,0:T(4,128)S(1)}, f32[8,128]{1,0:T(8,128)S(1)}, bf16[64,1024]{1,0:T(8,128)(2,1)S(1)}, bf16[64,1024]{1,0:T(8,128)(2,1)S(1)}) custom-call(f32[8]{0:T(128)} %table.1, f32[2,2,192,128]{3,2,1,0:T(8,128)} %forcing.1, s32[2,192,128]{2,1,0:T(8,128)} %ids.1, bf16[128,16384]{1,0:T(8,128)(2,1)} %operator.1), custom_call_target="tpu_custom_call" | custom-call | tf_op jit(solution)/shard_map/pallas_call | solution.py:483
  2.6 3.0 %collective-permute-start.5 = (bf16[64,1024]{1,0:T(8,128)(2,1)S(1)}, bf16[64,1024]{1,0:T(8,128)(2,1)S(1)}, u32[]{:S(2)}, u32[]{:S(2)}) collective-permute-start(bf16[64,1024]{1,0:T(8,128)(2,1)S(1)} %get-tuple-element.56), channel_id=1, source_target_pairs={{0,1},{1,0},{2,3},{3,2},{4,5},{5,4},{6,7},{7,6},{8,9},{9,8},{10,11... | collective-permute-start | bytes 393224 | tf_op jit(solution)/shard_map/ppermute | solution.py:472
  5.6 0.0 collective-permute-done.1.ids
  5.6 0.0 collective-permute-done.forcing
  5.7 0.3 collective-permute-start.2
  6.0 0.3 shard_map.60.other
  6.3 3.6 %collective-permute-done.2.got = f32[12,4,128]{2,1,0:T(4,128)S(1)} collective-permute-done((f32[12,4,128]{2,1,0:T(4,128)S(1)}, f32[12,4,128]{2,1,0:T(4,128)S(1)}, u32[]{:S(2)}, u32[]{:S(2)}) %collective-permute-start.2) | collective-permute-done | bytes 24608 | tf_op jit(solution)/shard_map/ppermute | solution.py:472
  9.9 0.2 shard_map.62
  10.1 1.8 %collective-permute-start.3 = (f32[12,4,256]{2,1,0:T(4,128)S(1)}, f32[12,4,256]{2,1,0:T(4,128)S(1)}, u32[]{:S(2)}, u32[]{:S(2)}) collective-permute-start(f32[12,4,256]{2,1,0:T(4,128)S(1)} %get-tuple-element.48), channel_id=1, source_target_pairs={{0,2},{2,0},{4,6},{6,4},{8,10},{10,8},{12,14},{14,12},{1,3},{3,1},... | collective-permute-start | bytes 147464 | tf_op jit(solution)/shard_map/ppermute | solution.py:512
  11.9 1.5 %collective-permute-start.4 = (f32[12,4,256]{2,1,0:T(4,128)S(1)}, f32[12,4,256]{2,1,0:T(4,128)S(1)}, u32[]{:S(2)}, u32[]{:S(2)}) collective-permute-start(f32[12,4,256]{2,1,0:T(4,128)S(1)} %get-tuple-element.51), channel_id=1, source_target_pairs={{0,1},{1,0},{2,4},{3,5},{4,2},{5,3},{6,8},{7,9},{8,6},{9,7},{10,12... | collective-permute-start | bytes 147464 | tf_op jit(solution)/shard_map/ppermute | solution.py:520
  13.4 0.9 %collective-permute-done.3.even = f32[12,4,256]{2,1,0:T(4,128)S(1)} collective-permute-done((f32[12,4,256]{2,1,0:T(4,128)S(1)}, f32[12,4,256]{2,1,0:T(4,128)S(1)}, u32[]{:S(2)}, u32[]{:S(2)}) %collective-permute-start.3) | collective-permute-done | bytes 49184 | tf_op jit(solution)/shard_map/ppermute | solution.py:512
  14.3 0.0 copy-start
  14.3 1.5 %shard_map.63 = (f32[12,144,256]{2,1,0:T(8,128)S(1)}, f32[12,144,256]{2,1,0:T(8,128)}) custom-call(f32[6,128,256]{2,1,0:T(8,128)S(1)} %get-tuple-element.44.own, f32[6,128,256]{2,1,0:T(8,128)S(1)} %shard_map.60.other, f32[128,128]{1,0:T(8,128)S(1)} %get-tuple-element.47.turned, f32[12,4,256]{2,1,0:T(4,128)S(1)} %collective-permute-done.3.even), custom_call_target="tpu_custom_call" | custom-call | tf_op jit(solution)/shard_map/pallas_call | solution.py:523
  15.7 0.2 collective-permute-done.4.odd
  16.0 3.1 %shard_map.64 = (f32[12,144,256]{2,1,0:T(8,128)S(1)}, f32[12,144,256]{2,1,0:T(8,128)}, bf16[8,64,128]{2,1,0:T(8,128)(2,1)S(1)}, f32[8,128]{1,0:T(8,128)S(1)}) custom-call(f32[12,144,256]{2,1,0:T(8,128)S(1)} %get-tuple-element.49._, f32[12,144,256]{2,1,0:T(8,128)} %get-tuple-element.50.__, ...), custom_call_target="tpu_custom_call", output_to_operand_aliasing={{0}: (0, {}), {1}: (1, {})} | custom-call | tf_op jit(solution)/shard_map/pallas_call | solution.py:533
  19.1 0.0 collective-permute-done.5
  19.1 0.0 copy-done
  19.1 5.9 %conditional.1 = (f32[2,2,192,128]{3,2,1,0:T(8,128)S(1)}, f32[16,128]{1,0:T(8,128)S(1)}, f32[8,128]{1,0:T(8,128)S(1)}, f32[16,128]{1,0:T(8,128)S(1)}) conditional(s32[]{:T(128)} %convert_element_type.3, f32[12,144,256]{2,1,0:T(8,128)} %get-tuple-element.52, (f32[12,144,256]{2,1,0:T(8,128)}, bf16[8,64,128]{2,1,0:T(8,128)(2,1)S(1)}, ...), branch_computations={%region_0.0_spmd, %region_1.0_spmd} | conditional | bytes 7536732 | solution.py:571
  19.1 5.6 %branch_0_fun.1 = (f32[2,2,192,128]{3,2,1,0:T(8,128)S(1)}, f32[16,128]{1,0:T(8,128)S(1)}) custom-call(f32[12,144,256]{2,1,0:T(8,128)} %ext), custom_call_target="tpu_custom_call" | custom-call | tf_op jit(solution)/shard_map/cond/branch_0_fun/pallas_call | solution.py:550
  25.0 16.1 %collective-permute-start.6 = (f32[2,64]{1,0:T(2,128)S(1)}, f32[2,64]{1,0:T(2,128)S(1)}, u32[]{:S(2)}, u32[]{:S(2)}) collective-permute-start(f32[2,64]{1,0:T(2,128)S(1)} %slice.11), channel_id=1, source_target_pairs={{0,16},{16,0},{1,17},{17,1},{2,18},{18,2},{3,19},{19,3},{4,20},{20... | collective-permute-start | bytes 1544 | tf_op jit(solution)/shard_map/ppermute | solution.py:472
  41.1 0.8 %shard_map.65 = f32[2,2,192,128]{3,2,1,0:T(8,128)} custom-call(f32[2,2,192,128]{3,2,1,0:T(8,128)S(1)} %get-tuple-element.57.pressure, f32[16,128]{1,0:T(8,128)S(1)} %get-tuple-element.58.near, f32[16,128]{1,0:T(8,128)S(1)} %get-tuple-element.59.fix), custom_call_target="tpu_custom_call" | custom-call | tf_op jit(solution)/shard_map/pallas_call | solution.py:574
  41.9 0.0 collective-permute-done.6
  41.9 0.5 %fusion = f32[64,1]{0,1:T(1,128)} fusion(pred[]{:T(512)S(6)} %eq.4, f32[2,64]{1,0:T(2,128)S(1)} %collective-permute-done.6, f32[8,128]{1,0:T(8,128)S(1)} %get-tuple-element.60), kind=kLoop, calls=%fused_computation.1 | loop fusion | flops 64 | bytes 769 | tf_op jit(solution)/shard_map/reshape | solution.py:578
  (4 shorter events, 0.0 us)
Async XLA Ops:
  0.6 5.0 %collective-permute-start = (f32[2,2,192,128]{3,2,1,0:T(8,128)}, f32[2,2,192,128]{3,2,1,0:T(8,128)S(1)}, u32[]{:S(2)}, u32[]{:S(2)}) collective-permute-start(f32[2,2,192,128]{3,2,1,0:T(8,128)} %forcing.1), channel_id=1, source_target_pairs={{0,16},{16,0},{1,17},{17,1},{2,18},{18,2},{3,19},{19,3},{4,20},{20... | collective-permute-start | bytes 1179656 | tf_op jit(solution)/shard_map/ppermute | solution.py:472
  1.2 4.5 %collective-permute-start.1 = (s32[2,192,128]{2,1,0:T(8,128)}, s32[2,192,128]{2,1,0:T(8,128)S(1)}, u32[]{:S(2)}, u32[]{:S(2)}) collective-permute-start(s32[2,192,128]{2,1,0:T(8,128)} %ids.1), channel_id=1, source_target_pairs={{0,16},{16,0},{1,17},{17,1},{2,18},{18,2},{3,19},{19,3},{4,20},{20... | collective-permute-start | bytes 589832 | tf_op jit(solution)/shard_map/ppermute | solution.py:472
  2.6 16.4 %collective-permute-start.5 = (bf16[64,1024]{1,0:T(8,128)(2,1)S(1)}, bf16[64,1024]{1,0:T(8,128)(2,1)S(1)}, u32[]{:S(2)}, u32[]{:S(2)}) collective-permute-start(bf16[64,1024]{1,0:T(8,128)(2,1)S(1)} %get-tuple-element.56), channel_id=1, source_target_pairs={{0,1},{1,0},{2,3},{3,2},{4,5},{5,4},{6,7},{7,6},{8,9},{9,8},{10,11... | collective-permute-start | bytes 393224 | tf_op jit(solution)/shard_map/ppermute | solution.py:472
  5.7 4.2 %collective-permute-start.2 = (f32[12,4,128]{2,1,0:T(4,128)S(1)}, f32[12,4,128]{2,1,0:T(4,128)S(1)}, u32[]{:S(2)}, u32[]{:S(2)}) collective-permute-start(f32[12,4,128]{2,1,0:T(4,128)S(1)} %shard_map.61), channel_id=1, source_target_pairs={{0,1},{1,0},{2,3},{3,2},{4,5},{5,4},{6,7},{7,6},{8,9},{9,8},{10,11... | collective-permute-start | bytes 73736 | tf_op jit(solution)/shard_map/ppermute | solution.py:472
  10.1 4.2 %collective-permute-start.3 = (f32[12,4,256]{2,1,0:T(4,128)S(1)}, f32[12,4,256]{2,1,0:T(4,128)S(1)}, u32[]{:S(2)}, u32[]{:S(2)}) collective-permute-start(f32[12,4,256]{2,1,0:T(4,128)S(1)} %get-tuple-element.48), channel_id=1, source_target_pairs={{0,2},{2,0},{4,6},{6,4},{8,10},{10,8},{12,14},{14,12},{1,3},{3,1},... | collective-permute-start | bytes 147464 | tf_op jit(solution)/shard_map/ppermute | solution.py:512
  11.9 4.1 %collective-permute-start.4 = (f32[12,4,256]{2,1,0:T(4,128)S(1)}, f32[12,4,256]{2,1,0:T(4,128)S(1)}, u32[]{:S(2)}, u32[]{:S(2)}) collective-permute-start(f32[12,4,256]{2,1,0:T(4,128)S(1)} %get-tuple-element.51), channel_id=1, source_target_pairs={{0,1},{1,0},{2,4},{3,5},{4,2},{5,3},{6,8},{7,9},{8,6},{9,7},{10,12... | collective-permute-start | bytes 147464 | tf_op jit(solution)/shard_map/ppermute | solution.py:520
  14.3 4.8 %copy-start = (bf16[128,16384]{1,0:T(8,128)(2,1)S(1)}, bf16[128,16384]{1,0:T(8,128)(2,1)}, u32[]{:S(2)}) copy-start(bf16[128,16384]{1,0:T(8,128)(2,1)} %operator.1) | copy-start | bytes 12582916
  25.0 16.9 %collective-permute-start.6 = (f32[2,64]{1,0:T(2,128)S(1)}, f32[2,64]{1,0:T(2,128)S(1)}, u32[]{:S(2)}, u32[]{:S(2)}) collective-permute-start(f32[2,64]{1,0:T(2,128)S(1)} %slice.11), channel_id=1, source_target_pairs={{0,16},{16,0},{1,17},{17,1},{2,18},{18,2},{3,19},{19,3},{4,20},{20... | collective-permute-start | bytes 1544 | tf_op jit(solution)/shard_map/ppermute | solution.py:472

commit v5 on v4

--- a/solution.py
+++ b/solution.py
@@ -160,12 +160,11 @@
     return [(0 if m < 2 else half) + 2 * k + m % 2 for k in kinds for m in range(4)]
 
 
-def extend_kernel(used, own, other, turned, even, ext, saved, sems):
+def extend_kernel(used, own, other, turned, ext, saved, sems):
     n = lax.axis_index("narrow")
     half = own.shape[0]
     cells_x, width = own.shape[1], own.shape[2]
     right = TILE + cells_x
-    left = lax.rem(lax.axis_index("wide"), 2) == 0
     rows = turned[...]
     copies = []
     for place, slab in enumerate(order((half - 2) // 2)):
@@ -176,8 +175,6 @@
         ext[place, TILE:right, width - LANES :] = with_edge(
             ref[k, :, width - LANES :], rows, slab, used, n
         )
-        ext[place, TILE - HALO : TILE] = jnp.where(left, 0.0, even[slab])
-        ext[place, right : right + HALO] = jnp.where(left, even[slab], 0.0)
         copies.append(pltpu.make_async_copy(ext.at[place], saved.at[place], sems.at[place]))
         copies[place].start()
     for copy in copies:
@@ -194,17 +191,22 @@
     return total + pltpu.roll(total, 1, 1) + pltpu.roll(total, width - 1, 1)
 
 
-def residual(ext, hh, qq, u, cu, e, m):
+def drawn(ext, hh, u, cu, e, m):
     base = ext.shape[0] - 4
     c, k = ext[base + m], e * 4 + m
     near_sum = box(u, e * 4, m) - u[k]
     weighted = box(cu, e * 4, m) - cu[k]
-    return (qq[k] - u[k]) + hh[m] * (c * near_sum + weighted)
-
-
-def second(ext, hh, qq, u1, cu1, u2, cu2, e, m):
+    return hh[m] * (c * near_sum + weighted)
+
+
+def residual(ext, hh, qq, u, cu, e, m):
     k = e * 4 + m
-    p = (1.0 + KEEP1) * u1[k] + GAIN1 * residual(ext, hh, qq, u1, cu1, e, m)
+    return (qq[k] - u[k]) + drawn(ext, hh, u, cu, e, m)
+
+
+def second(ext, hh, u1, cu1, u2, cu2, e, m):
+    k = e * 4 + m
+    p = (1.0 + KEEP1 + GAIN1 / GAIN0 - GAIN1) * u1[k] + GAIN1 * drawn(ext, hh, u1, cu1, e, m)
     u2[k] = p
     cu2[k] = p * ext[ext.shape[0] - 4 + m]
 
@@ -237,20 +239,25 @@
             cu1[e * 4 + m] = (GAIN0 * q) * c
 
 
-def sweep_kernel(
-    stride, _, __, odd, ext, saved, trace, aux, hh, qq, u1, cu1, u2, cu2, u3, cu3, mv, u4, sems
-):
+def merge_sides(even, odd, ext):
     w = lax.axis_index("wide")
     inner = (w > 0) & (w < lax.axis_size("wide") - 1)
+    left = lax.rem(w, 2) == 0
+    right = ext.shape[1] - TILE
+    for place, slab in enumerate(order(ext.shape[0] // 4 - 1)):
+        outer = jnp.where(inner, odd[slab], 0.0)
+        ext[place, TILE - HALO : TILE] = jnp.where(left, outer, even[slab])
+        ext[place, right : right + HALO] = jnp.where(left, even[slab], outer)
+
+
+def sweep_kernel(
+    stride, _, __, even, odd, ext, saved, trace, aux, hh, qq, u1, cu1, u2, cu2, u3, cu3, mv, u4, sems
+):
     excite = u4.shape[0]
     width = ext.shape[2]
     cells_x = ext.shape[1] - 2 * TILE
     right = TILE + cells_x
-    left = lax.rem(w, 2) == 0
-    for place, slab in enumerate(order(excite)):
-        outer = jnp.where(inner, odd[slab], 0.0)
-        for at, here in ((TILE - HALO, left), (right, ~left)):
-            ext[place, at : at + HALO] = jnp.where(here, outer, ext[place, at : at + HALO])
+    merge_sides(even, odd, ext)
     copies = []
     for k, at in enumerate((0, right)):
         edge = ext.at[:, at : at + TILE], saved.at[:, at : at + TILE]
@@ -259,7 +266,7 @@
     start_sweeps(ext, hh, qq, u1, cu1)
     for e in range(excite):
         for m in range(3):
-            second(ext, hh, qq, u1, cu1, u2, cu2, e, m)
+            second(ext, hh, u1, cu1, u2, cu2, e, m)
         for m in range(2):
             third(ext, hh, qq, u2, cu2, u3, cu3, mv, e, m)
         u4[e] = fourth(ext, hh, qq, u3, cu3, mv, e, 0)
@@ -293,7 +300,7 @@
     start_sweeps(ext, hh, qq, u1, cu1)
     for e in range(excite):
         for m in range(4):
-            second(ext, hh, qq, u1, cu1, u2, cu2, e, m)
+            second(ext, hh, u1, cu1, u2, cu2, e, m)
         for m in range(3):
             third(ext, hh, qq, u2, cu2, u3, cu3, mv, e, m)
         for m in range(2):
@@ -306,6 +313,11 @@
             for i, y in enumerate((0, 1, cells_y - 1)):
                 row = 6 * k + 3 * m + i
                 near[row : row + 1] = back[y : y + 1]
+
+
+def lower_kernel(_, even, odd, ext, pressure, near, *scratch):
+    merge_sides(even, odd, ext)
+    field_kernel(ext, pressure, near, *scratch)
 
 
 def product_kernel(blocks, operator, aux, out):
@@ -487,7 +499,7 @@
             ((half, HALO, cells_x), f32),
             ((materials.shape[0], LANES), f32),
         ]
-        + [((targets, wides * LANES), bf16)] * 2,
+        + [pltpu.VMEM((targets, wides * LANES), bf16)] * 2,
         [hbm] * 4,
         [
             pltpu.VMEM(forcing.shape, f32),
@@ -504,12 +516,6 @@
         f_other, id_other, spread
     )
     used = cells_y - (width - LANES)
-    even, odd, turned = call(
-        functools.partial(side_kernel, used),
-        [((slabs, HALO, width), f32)] * 2 + [((cells_x, LANES), f32)],
-        [vmem] * 3,
-    )(own, other, edge)
-    even = lax.ppermute(even, "wide", [(i, i ^ 1) for i in range(wides)])
     odd_pairs = []
     for a in range(vols):
         for b in range(wides):
@@ -517,41 +523,56 @@
                 far = b + 1 if b % 2 else b - 1
                 there = (far, c) if 0 <= far < wides else (b, 1 - c)
                 odd_pairs.append((number(a, b, c), number(a, *there)))
-    odd = lax.ppermute(odd, everyone, odd_pairs)
     rows = cells_x + 2 * TILE
     full = (rows, width)
-    ext, saved = call(
-        functools.partial(extend_kernel, used),
-        [((slabs,) + full, f32), pltpu.HBM((slabs,) + full, f32)],
-        [vmem] * 4,
-        [dma((slabs,))],
-        outs=[vmem, hbm],
-    )(own, other, turned, even)
-    theirs = swap(sent, "narrow")
     many = pltpu.VMEM((4 * excite,) + full, f32)
     scratch = [pltpu.VMEM((4,) + full, f32)] + [many] * 8
-    _, ext, trace, aux = call(
-        functools.partial(sweep_kernel, cells_y // BY),
-        [
-            ((slabs,) + full, f32),
-            pltpu.HBM((slabs,) + full, f32),
-            ((wides, BY * 2 * excite, cells_x), bf16),
-            ((8, cells_x), f32),
-        ],
-        [vmem, hbm, vmem],
-        scratch + [pltpu.VMEM((excite,) + full, f32), dma((2,))],
-        20,
-        outs=[vmem, hbm, vmem, vmem],
-        input_output_aliases={0: 0, 1: 1},
-    )(ext, saved, odd)
-
-    def field(ext):
-        shapes = [(forcing.shape, f32), ((16, cells_x), f32)]
-        return call(field_kernel, shapes, [vmem], scratch, 20)(ext)
-
-    def couple(ext, trace, aux, operator, theirs):
+    outputs = [(forcing.shape, f32), ((16, cells_x), f32)]
+
+    def sides(own, other, edge):
+        return call(
+            functools.partial(side_kernel, used),
+            [((slabs, HALO, width), f32)] * 2 + [((cells_x, LANES), f32)],
+            [vmem] * 3,
+        )(own, other, edge)
+
+    def trade_even(even):
+        return lax.ppermute(even, "wide", [(i, i ^ 1) for i in range(wides)])
+
+    def trade_odd(odd):
+        return lax.ppermute(odd, everyone, odd_pairs)
+
+    def extend(own, other, turned):
+        return call(
+            functools.partial(extend_kernel, used),
+            [((slabs,) + full, f32), pltpu.HBM((slabs,) + full, f32)],
+            [vmem] * 3,
+            [dma((slabs,))],
+            outs=[vmem, hbm],
+        )(own, other, turned)
+
+    def upper(own, other, edge, operator, sent, mine):
+        even, odd, turned = sides(own, other, edge)
+        even = trade_even(even)
+        odd = trade_odd(odd)
+        ext, saved = extend(own, other, turned)
+        theirs = swap(sent, "narrow")
+        _, saved, trace, aux = call(
+            functools.partial(sweep_kernel, cells_y // BY),
+            [
+                ((slabs,) + full, f32),
+                pltpu.HBM((slabs,) + full, f32),
+                ((wides, BY * 2 * excite, cells_x), bf16),
+                ((8, cells_x), f32),
+            ],
+            [vmem, hbm, vmem, vmem],
+            scratch + [pltpu.VMEM((excite,) + full, f32), dma((2,))],
+            20,
+            outs=[vmem, hbm, vmem, vmem],
+            input_output_aliases={0: 0, 1: 1},
+        )(ext, saved, even, odd)
         blocks = lax.all_to_all(trace, "wide", 0, 0)
-        pressure, near = field(ext)
+        pressure, near = call(field_kernel, outputs, [vmem], scratch, 20)(saved)
         (sums,) = call(product_kernel, [((wides * narrows, 8, tile_rows), f32)], [vmem] * 3, (), 24)(
             blocks, operator, aux
         )
@@ -564,17 +585,23 @@
         )(blocks.reshape(wides * narrows * 8, LANES), mine, theirs)
         return pressure, near, traction, fix
 
-    def nothing(ext, *_):
-        pressure, near = field(ext)
+    def lower(own, other, edge, *_):
+        even, odd, turned = sides(own, other, edge)
+        ext, _ = extend(own, other, turned)
+        even, odd, ext = lax.optimization_barrier((even, odd, ext))
+        even, odd = trade_even(even), trade_odd(odd)
+        _, pressure, near = call(
+            lower_kernel, [((slabs,) + full, f32)] + outputs, [vmem] * 3, scratch, 20, input_output_aliases={0: 0}
+        )(ext, even, odd)
         return pressure, near, jnp.zeros((8, LANES), f32), jnp.zeros((16, cells_x), f32)
 
     pressure, near, traction, fix = lax.cond(
-        v == vols - 1, couple, nothing, ext, trace, aux, boundary_operator, theirs
+        v == vols - 1, upper, lower, own, other, edge, boundary_operator, sent, mine
     )
     (pressure,) = call(mend_kernel, [(forcing.shape, f32)], [vmem] * 3)(pressure, near, fix)
     column = traction[0:2, :targets]
-    lower = swap(column, "vol")
-    column = jnp.where(v == vols - 1, column[1:2], lower[0:1])
+    first = swap(column, "vol")
+    column = jnp.where(v == vols - 1, column[1:2], first[0:1])
     return pressure, column.reshape(targets, 1)
 
 

time: 42.6 us -> 43.4 us (1.019)
  starting transfers between devices: 23.3 us -> 28.9 us
  Pallas kernels: 12.8 us -> 8.26 us
    ppermute x5 -> x4, starting transfers between devices: 20 us -> 25.3 us  [swap(): return lax.ppermute(x, axis, [(0, 1), (1, 0)])]
    pallas_call x4 -> x3, Pallas kernels: 10.4 us -> 5.83 us  [the longest x1 4.2 us: lower(): call(lower_kernel, [((slabs,) + full, f32)] + outputs, [vmem] * 3, scratc...]
    ppermute x5 -> x4, waiting for transfers between devices: 3.68 us -> 1.96 us  [swap(): return lax.ppermute(x, axis, [(0, 1), (1, 0)])]
    ppermute x2, waiting for transfers between devices: 1.11 us -> 2.57 us  [the longest x1 1.99 us: trade_odd(): return lax.ppermute(odd, everyone, odd_pairs)]
  transfers between devices with their start and end apart: 7 -> 6, of which waited for: 3 -> 4; matrix products, arithmetic and copies ran while one was open for 0% -> 0% of each run, Pallas kernels for 17% -> 6%
where the time goes in v5:
time: 43.4 us; the launch traced here: 43.2 us
  starting transfers between devices  28.9 us (67%)
  Pallas kernels  8.26 us (19%)
  waiting for transfers between devices  4.53 us (10%)
  between operations  0.67 us (2%)
  other arithmetic  0.51 us (1%)
    ppermute x4, starting transfers between devices, swap(): return lax.ppermute(x, axis, [(0, 1), (1, 0)])  25.3 us
    pallas_call x1, Pallas kernels, lower(): call(lower_kernel, [((slabs,) + full, f32)] + outputs, [vmem] * 3, scratc...  4.2 us
    ppermute x1, starting transfers between devices, trade_even(): return lax.ppermute(even, 'wide', [(i, i ^ 1) for i in range(wides)])  2.06 us
    ppermute x1, waiting for transfers between devices, trade_odd(): return lax.ppermute(odd, everyone, odd_pairs)  1.99 us
    ppermute x4, waiting for transfers between devices, swap(): return lax.ppermute(x, axis, [(0, 1), (1, 0)])  1.96 us
    ppermute x1, starting transfers between devices, trade_odd(): return lax.ppermute(odd, everyone, odd_pairs)  1.52 us
    pallas_call x1, Pallas kernels, extend(): call(functools.partial(extend_kernel, used), [((slabs,) + full, f32), plt...  1.44 us
    pallas_call x1, Pallas kernels, local(): call(own_kernel, [((half, cells_x, width), f32), ((half, HALO, cells_x),...  1.36 us
  transfers between devices with their start and end apart: 6, of which 4 were waited for; matrix products, arithmetic and copies ran while one was open for 0% of the time, Pallas kernels for 6%

profile of v5, /device:TPU:0, one launch (start us, length us, event | category | flops | bytes accessed | tf_op | source)
XLA Modules:
  0.0 43.2 jit_solution(3961257193345546557)
XLA Ops:
  0.6 0.6 %collective-permute-start.5 = (f32[2,2,192,128]{3,2,1,0:T(8,128)}, f32[2,2,192,128]{3,2,1,0:T(8,128)S(1)}, u32[]{:S(2)}, u32[]{:S(2)}) collective-permute-start(f32[2,2,192,128]{3,2,1,0:T(8,128)} %forcing.1), channel_id=1, source_target_pairs={{0,16},{16,0},{1,17},{17,1},{2,18},{18,2},{3,19},{19,3},{4,20},{20... | collective-permute-start | bytes 1179656 | tf_op jit(solution)/shard_map/ppermute | solution.py:484
  1.2 0.1 collective-permute-start.6
  1.3 1.4 %shard_map.59 = (f32[6,128,256]{2,1,0:T(8,128)S(1)}, f32[6,4,128]{2,1,0:T(4,128)S(1)}, f32[8,128]{1,0:T(8,128)S(1)}, bf16[64,1024]{1,0:T(8,128)(2,1)S(1)}, bf16[64,1024]{1,0:T(8,128)(2,1)S(1)}) custom-call(f32[8]{0:T(128)} %table.1, f32[2,2,192,128]{3,2,1,0:T(8,128)} %forcing.1, s32[2,192,128]{2,1,0:T(8,128)} %ids.1, bf16[128,16384]{1,0:T(8,128)(2,1)} %operator.1), custom_call_target="tpu_custom_call" | custom-call | tf_op jit(solution)/shard_map/pallas_call | solution.py:495
  2.6 0.4 collective-permute-done.6.ids
  3.0 0.0 collective-permute-done.5.forcing
  3.0 2.9 %collective-permute-start.7 = (f32[12,4,128]{2,1,0:T(4,128)S(1)}, f32[12,4,128]{2,1,0:T(4,128)S(1)}, u32[]{:S(2)}, u32[]{:S(2)}) collective-permute-start(f32[12,4,128]{2,1,0:T(4,128)S(1)} %shard_map.61), channel_id=1, source_target_pairs={{0,1},{1,0},{2,3},{3,2},{4,5},{5,4},{6,7},{7,6},{8,9},{9,8},{10,11... | collective-permute-start | bytes 73736 | tf_op jit(solution)/shard_map/ppermute | solution.py:484
  6.0 0.3 shard_map.60
  6.3 1.5 %collective-permute-done.7 = f32[12,4,128]{2,1,0:T(4,128)S(1)} collective-permute-done((f32[12,4,128]{2,1,0:T(4,128)S(1)}, f32[12,4,128]{2,1,0:T(4,128)S(1)}, u32[]{:S(2)}, u32[]{:S(2)}) %collective-permute-start.7) | collective-permute-done | bytes 24608 | tf_op jit(solution)/shard_map/ppermute | solution.py:484
  7.8 12.2 %conditional.1 = (f32[2,2,192,128]{3,2,1,0:T(8,128)S(1)}, f32[16,128]{1,0:T(8,128)S(1)}, f32[8,128]{1,0:T(8,128)S(1)}, f32[16,128]{1,0:T(8,128)S(1)}) conditional(s32[]{:T(128)} %convert_element_type.3, (f32[6,128,256]{2,1,0:T(8,128)S(1)}, f32[6,128,256]{2,1,0:T(8,128)S(1)}, f32[12,4,128]{2,1,0:T(4,128)S(1)}) %tuple.17, ...), branch_computations={%region_0.0_spmd, %region_1.0_spmd} | conditional | bytes 8585460 | solution.py:598
  7.8 0.2 branch_0_fun.3
  8.0 1.4 %branch_0_fun.4 = (f32[12,144,256]{2,1,0:T(8,128)S(1)}, f32[12,144,256]{2,1,0:T(8,128)}) custom-call(f32[6,128,256]{2,1,0:T(8,128)S(1)} %get-tuple-element.18.own, f32[6,128,256]{2,1,0:T(8,128)S(1)} %get-tuple-element.19.other, f32[128,128]{1,0:T(8,128)S(1)} %get-tuple-element.23.turned), custom_call_target="tpu_custom_call" | custom-call | tf_op jit(solution)/shard_map/cond/branch_0_fun/pallas_call | solution.py:546
  9.5 2.1 %collective-permute-start = (f32[12,4,256]{2,1,0:T(4,128)S(1)}, f32[12,4,256]{2,1,0:T(4,128)S(1)}, u32[]{:S(2)}, u32[]{:S(2)}) collective-permute-start(f32[12,4,256]{2,1,0:T(4,128)S(1)} %get-tuple-element.26), channel_id=1, source_target_pairs={{0,2},{2,0},{4,6},{6,4},{8,10},{10,8},{12,14},{14,12},{1,3},{3,1},... | collective-permute-start | bytes 147464 | tf_op jit(solution)/shard_map/cond/branch_0_fun/ppermute | solution.py:540
  11.5 1.5 %collective-permute-start.1 = (f32[12,4,256]{2,1,0:T(4,128)S(1)}, f32[12,4,256]{2,1,0:T(4,128)S(1)}, u32[]{:S(2)}, u32[]{:S(2)}) collective-permute-start(f32[12,4,256]{2,1,0:T(4,128)S(1)} %get-tuple-element.27), channel_id=1, source_target_pairs={{0,1},{1,0},{2,4},{3,5},{4,2},{5,3},{6,8},{7,9},{8,6},{9,7},{10,12... | collective-permute-start | bytes 147464 | tf_op jit(solution)/shard_map/cond/branch_0_fun/ppermute | solution.py:543
  13.0 0.6 %collective-permute-done.even = f32[12,4,256]{2,1,0:T(4,128)S(1)} collective-permute-done((f32[12,4,256]{2,1,0:T(4,128)S(1)}, f32[12,4,256]{2,1,0:T(4,128)S(1)}, u32[]{:S(2)}, u32[]{:S(2)}) %collective-permute-start) | collective-permute-done | bytes 49184 | tf_op jit(solution)/shard_map/cond/branch_0_fun/ppermute | solution.py:540
  13.6 2.0 %collective-permute-done.1.odd = f32[12,4,256]{2,1,0:T(4,128)S(1)} collective-permute-done((f32[12,4,256]{2,1,0:T(4,128)S(1)}, f32[12,4,256]{2,1,0:T(4,128)S(1)}, u32[]{:S(2)}, u32[]{:S(2)}) %collective-permute-start.1) | collective-permute-done | bytes 49184 | tf_op jit(solution)/shard_map/cond/branch_0_fun/ppermute | solution.py:543
  15.6 4.2 %branch_0_fun.5 = (f32[12,144,256]{2,1,0:T(8,128)S(1)}, f32[2,2,192,128]{3,2,1,0:T(8,128)S(1)}, f32[16,128]{1,0:T(8,128)S(1)}) custom-call(f32[12,144,256]{2,1,0:T(8,128)S(1)} %get-tuple-element.25._, f32[12,4,256]{2,1,0:T(4,128)S(1)} %collective-permute-done.even, f32[12,4,256]{2,1,0:T(4,128)S(1)} %collective-permute-done.1.odd), custom_call_target="tpu_custom_call", output_to_operand_aliasing={{0}: (0, {})} | custom-call | tf_op jit(solution)/shard_map/cond/branch_0_fun/pallas_call | solution.py:593
  20.1 21.8 %collective-permute-start.8 = (f32[2,64]{1,0:T(2,128)S(1)}, f32[2,64]{1,0:T(2,128)S(1)}, u32[]{:S(2)}, u32[]{:S(2)}) collective-permute-start(f32[2,64]{1,0:T(2,128)S(1)} %slice.11), channel_id=1, source_target_pairs={{0,16},{16,0},{1,17},{17,1},{2,18},{18,2},{3,19},{19,3},{4,20},{20... | collective-permute-start | bytes 1544 | tf_op jit(solution)/shard_map/ppermute | solution.py:484
  41.8 0.8 %shard_map.62 = f32[2,2,192,128]{3,2,1,0:T(8,128)} custom-call(f32[2,2,192,128]{3,2,1,0:T(8,128)S(1)} %get-tuple-element.64.pressure, f32[16,128]{1,0:T(8,128)S(1)} %get-tuple-element.65.near, f32[16,128]{1,0:T(8,128)S(1)} %get-tuple-element.66.fix), custom_call_target="tpu_custom_call" | custom-call | tf_op jit(solution)/shard_map/pallas_call | solution.py:601
  42.6 0.0 collective-permute-done.8
  42.6 0.5 %fusion = f32[64,1]{0,1:T(1,128)} fusion(pred[]{:T(512)S(6)} %eq.4, f32[2,64]{1,0:T(2,128)S(1)} %collective-permute-done.8, f32[8,128]{1,0:T(8,128)S(1)} %get-tuple-element.67), kind=kLoop, calls=%fused_computation.1 | loop fusion | flops 64 | bytes 769 | tf_op jit(solution)/shard_map/reshape | solution.py:605
  (4 shorter events, 0.0 us)
Async XLA Ops:
  0.6 2.4 %collective-permute-start.5 = (f32[2,2,192,128]{3,2,1,0:T(8,128)}, f32[2,2,192,128]{3,2,1,0:T(8,128)S(1)}, u32[]{:S(2)}, u32[]{:S(2)}) collective-permute-start(f32[2,2,192,128]{3,2,1,0:T(8,128)} %forcing.1), channel_id=1, source_target_pairs={{0,16},{16,0},{1,17},{17,1},{2,18},{18,2},{3,19},{19,3},{4,20},{20... | collective-permute-start | bytes 1179656 | tf_op jit(solution)/shard_map/ppermute | solution.py:484
  1.2 1.8 %collective-permute-start.6 = (s32[2,192,128]{2,1,0:T(8,128)}, s32[2,192,128]{2,1,0:T(8,128)S(1)}, u32[]{:S(2)}, u32[]{:S(2)}) collective-permute-start(s32[2,192,128]{2,1,0:T(8,128)} %ids.1), channel_id=1, source_target_pairs={{0,16},{16,0},{1,17},{17,1},{2,18},{18,2},{3,19},{19,3},{4,20},{20... | collective-permute-start | bytes 589832 | tf_op jit(solution)/shard_map/ppermute | solution.py:484
  3.0 4.7 %collective-permute-start.7 = (f32[12,4,128]{2,1,0:T(4,128)S(1)}, f32[12,4,128]{2,1,0:T(4,128)S(1)}, u32[]{:S(2)}, u32[]{:S(2)}) collective-permute-start(f32[12,4,128]{2,1,0:T(4,128)S(1)} %shard_map.61), channel_id=1, source_target_pairs={{0,1},{1,0},{2,3},{3,2},{4,5},{5,4},{6,7},{7,6},{8,9},{9,8},{10,11... | collective-permute-start | bytes 73736 | tf_op jit(solution)/shard_map/ppermute | solution.py:484
  9.5 4.2 %collective-permute-start = (f32[12,4,256]{2,1,0:T(4,128)S(1)}, f32[12,4,256]{2,1,0:T(4,128)S(1)}, u32[]{:S(2)}, u32[]{:S(2)}) collective-permute-start(f32[12,4,256]{2,1,0:T(4,128)S(1)} %get-tuple-element.26), channel_id=1, source_target_pairs={{0,2},{2,0},{4,6},{6,4},{8,10},{10,8},{12,14},{14,12},{1,3},{3,1},... | collective-permute-start | bytes 147464 | tf_op jit(solution)/shard_map/cond/branch_0_fun/ppermute | solution.py:540
  11.5 4.1 %collective-permute-start.1 = (f32[12,4,256]{2,1,0:T(4,128)S(1)}, f32[12,4,256]{2,1,0:T(4,128)S(1)}, u32[]{:S(2)}, u32[]{:S(2)}) collective-permute-start(f32[12,4,256]{2,1,0:T(4,128)S(1)} %get-tuple-element.27), channel_id=1, source_target_pairs={{0,1},{1,0},{2,4},{3,5},{4,2},{5,3},{6,8},{7,9},{8,6},{9,7},{10,12... | collective-permute-start | bytes 147464 | tf_op jit(solution)/shard_map/cond/branch_0_fun/ppermute | solution.py:543
  20.1 22.6 %collective-permute-start.8 = (f32[2,64]{1,0:T(2,128)S(1)}, f32[2,64]{1,0:T(2,128)S(1)}, u32[]{:S(2)}, u32[]{:S(2)}) collective-permute-start(f32[2,64]{1,0:T(2,128)S(1)} %slice.11), channel_id=1, source_target_pairs={{0,16},{16,0},{1,17},{17,1},{2,18},{18,2},{3,19},{19,3},{4,20},{20... | collective-permute-start | bytes 1544 | tf_op jit(solution)/shard_map/ppermute | solution.py:484
